TPU v7x, 32 devices: a whole 2x2x4 slice. The times are simulated.
32 devices in a mesh: dp: 2 (over y), wide: 16 (over z, x, core).
Axes of the slice: x: 2, y: 2, z: 4, core: 2. Of those that a mesh axis runs over, the one named last changes fastest.
Arguments:
- patches: bfloat16 [128, 576, 1024], P(('dp', 'wide')), may hold values from -6 to 6
- counts: int32 [32], P(('dp', 'wide')), may hold values from 0 to 4, as said below
- cotangent: bfloat16 [128, 144, 4096], P('dp', None, 'wide'), may hold values from -6 to 6
- filters: float32 [4, 1024, 1024], P(None, ('dp', 'wide')), may hold values from -0.1875 to 0.1875
- filters_moment: float32 [4, 1024, 1024], P(None, ('dp', 'wide')), may hold values from -128 to 128
- filters_square: float32 [4, 1024, 1024], P(None, ('dp', 'wide')), may hold values from 576 to 2304
- filters_average: float32 [4, 1024, 1024], P(None, ('dp', 'wide')), may hold values from -0.1875 to 0.1875
- vectors: float32 [2, 15, 1024], P(None, None, ('dp', 'wide')), as said below
- vectors_moment: float32 [2, 15, 1024], P(None, None, ('dp', 'wide')), may hold values from -256 to 256
- vectors_square: float32 [2, 15, 1024], P(None, None, ('dp', 'wide')), may hold values from 2304 to 9216
- vectors_average: float32 [2, 15, 1024], P(None, None, ('dp', 'wide')), as said below
- expand: float32 [1024, 4096], P(None, 'wide'), may hold values from -0.1875 to 0.1875
- expand_moment: float32 [1024, 4096], P(None, 'wide'), may hold values from -192 to 192
- expand_square: float32 [1024, 4096], P(None, 'wide'), may hold values from 972.8 to 3840
- expand_average: float32 [1024, 4096], P(None, 'wide'), may hold values from -0.1875 to 0.1875
- project: float32 [4096, 4096], P(None, 'wide'), may hold values from -0.09375 to 0.09375
- project_moment: float32 [4096, 4096], P(None, 'wide'), may hold values from -256 to 256
- project_square: float32 [4096, 4096], P(None, 'wide'), may hold values from 1664 to 6656
- project_average: float32 [4096, 4096], P(None, 'wide'), may hold values from -0.09375 to 0.09375
- offsets: float32 [2, 4096], P(None, 'wide'), may hold values from -1.75 to 1.75
- offsets_moment: float32 [2, 4096], P(None, 'wide'), may hold values from -640 to 640
- offsets_square: float32 [2, 4096], P(None, 'wide'), may hold values from 5888 to 23552
- offsets_average: float32 [2, 4096], P(None, 'wide'), may hold values from -1.75 to 1.75
Outputs:
- readout: bfloat16 [128, 144, 4096], P('dp', None, 'wide')
- patch_gradient: bfloat16 [128, 576, 1024], P(('dp', 'wide'))
- filters_updated: float32 [4, 1024, 1024], P(None, ('dp', 'wide'))
- filters_momentum: float32 [4, 1024, 1024], P(None, ('dp', 'wide'))
- filters_variance: float32 [4, 1024, 1024], P(None, ('dp', 'wide'))
- filters_smoothed: float32 [4, 1024, 1024], P(None, ('dp', 'wide'))
- filters_bfloat: bfloat16 [4, 1024, 1024], P(None, ('dp', 'wide'))
- vectors_updated: float32 [2, 15, 1024], P(None, None, ('dp', 'wide'))
- vectors_momentum: float32 [2, 15, 1024], P(None, None, ('dp', 'wide'))
- vectors_variance: float32 [2, 15, 1024], P(None, None, ('dp', 'wide'))
- vectors_smoothed: float32 [2, 15, 1024], P(None, None, ('dp', 'wide'))
- vectors_bfloat: bfloat16 [2, 15, 1024], P(None, None, ('dp', 'wide'))
- expand_updated: float32 [1024, 4096], P(None, 'wide')
- expand_momentum: float32 [1024, 4096], P(None, 'wide')
- expand_variance: float32 [1024, 4096], P(None, 'wide')
- expand_smoothed: float32 [1024, 4096], P(None, 'wide')
- expand_bfloat: bfloat16 [1024, 4096], P(None, 'wide')
- project_updated: float32 [4096, 4096], P(None, 'wide')
- project_momentum: float32 [4096, 4096], P(None, 'wide')
- project_variance: float32 [4096, 4096], P(None, 'wide')
- project_smoothed: float32 [4096, 4096], P(None, 'wide')
- project_bfloat: bfloat16 [4096, 4096], P(None, 'wide')
- offsets_updated: float32 [2, 4096], P(None, 'wide')
- offsets_momentum: float32 [2, 4096], P(None, 'wide')
- offsets_variance: float32 [2, 4096], P(None, 'wide')
- offsets_smoothed: float32 [2, 4096], P(None, 'wide')
- offsets_bfloat: bfloat16 [2, 4096], P(None, 'wide')
Inputs may be any that keep to these rules, and one draw needn't show every extreme that they name: counts[s] image slots of sample s hold an image, the slots below counts[s]; some sample has 4. `vectors`: rows 9, 11, 13 of each block are norm gains, rows 10, 12, 14 norm shifts. `vectors_average`: laid out as vectors.
All inputs are finite; a program needn't handle non-finite values.
Results may differ from a plain program's by a relative error of at most 0.023.
The roundings to bfloat16 on the way count: a program that leaves them out, or rounds other values in their place, can miss the bound.
Values may be sent and summed in bfloat16 or wider, within the bound.
No kernel may reach another device: no remote copies, remote signals or barrier semaphores. Data moves between devices by JAX's collectives and lax.ppermute only.
A program may use at most 512 MiB of HBM per device.

v0:
```python
from functools import partial

import jax
import jax.numpy as jnp
from jax import lax
from jax.sharding import PartitionSpec as P

GRID = 24
POOL = 12
SLOTS = 4
STEP = 3


beta_one = 0.5
beta_two = 0.5
adam_eps = 1e-08
ema_keep = 0.75
norm_eps = 1e-06


def layer_norm(value, gain, shift):
    center = jnp.mean(value, axis=-1, keepdims=True)
    centered = value - center
    spread = jnp.mean(centered * centered, axis=-1, keepdims=True)
    return centered * lax.rsqrt(spread + norm_eps) * gain + shift


def depthwise(field, taps):
    side = field.shape[1]
    padded = jnp.pad(field, ((0, 0), (1, 1), (1, 1), (0, 0)))
    total = jnp.zeros(field.shape, jnp.float32)
    for row in range(3):
        for column in range(3):
            total = (
                total
                + padded[:, row : row + side, column : column + side, :] * taps[row * 3 + column]
            )
    return total


def middle(a_lin, vecs, side):
    width = a_lin.shape[1]
    count = a_lin.shape[0] // (side * side)
    active = jax.nn.silu(layer_norm(a_lin, vecs[9], vecs[10]))
    mixed = depthwise(active.reshape(count, side, side, width), vecs[0:9]).reshape(
        count * side * side, width
    )
    return jax.nn.silu(layer_norm(mixed, vecs[11], vecs[12]))


def closing(c_lin, residual, vecs):
    return jax.nn.silu(residual + layer_norm(c_lin, vecs[13], vecs[14]))


def gelu_exact(value):
    return jax.nn.gelu(value, approximate=False)


def contract_rows(left, right):
    return lax.dot_general(
        left, right, (((0,), (0,)), ((), ())), preferred_element_type=jnp.float32
    )


def contract_cols(left, right):
    return lax.dot_general(
        left, right, (((1,), (1,)), ((), ())), preferred_element_type=jnp.float32
    )


def block_forward(rows, w_in, w_out, vecs, side):
    a_lin = jnp.dot(rows, w_in, preferred_element_type=jnp.float32)
    narrow, middle_back = jax.vjp(partial(middle, side=side), a_lin, vecs)
    narrow_low = narrow.astype(jnp.bfloat16)
    c_lin = jnp.dot(narrow_low, w_out, preferred_element_type=jnp.float32)
    result, closing_back = jax.vjp(closing, c_lin, rows.astype(jnp.float32), vecs)
    return (result, (rows, narrow_low, middle_back, closing_back))


def block_backward(d_result, saved, w_in, w_out):
    rows, narrow_low, middle_back, closing_back = saved
    d_clin, d_resid, d_vecs_close = closing_back(d_result)
    d_clin_low = d_clin.astype(jnp.bfloat16)
    grad_out = contract_rows(narrow_low, d_clin_low)
    d_narrow = contract_cols(d_clin_low, w_out)
    d_alin, d_vecs_mid = middle_back(d_narrow)
    d_alin_low = d_alin.astype(jnp.bfloat16)
    grad_in = contract_rows(rows, d_alin_low)
    d_rows = d_resid + contract_cols(d_alin_low, w_in)
    return (d_rows, grad_in, grad_out, d_vecs_mid + d_vecs_close)


def pool(rows, side):
    width = rows.shape[1]
    half = side // 2
    count = rows.shape[0] // (side * side)
    grid = rows.reshape(count, half, 2, half, 2, width)
    return jnp.mean(grid, axis=(2, 4)).reshape(count * half * half, width)


def unpool(grads, side):
    width = grads.shape[1]
    half = side // 2
    count = grads.shape[0] // (half * half)
    spread = grads.reshape(count, half, 1, half, 1, width) * 0.25
    return jnp.broadcast_to(spread, (count, half, 2, half, 2, width)).reshape(
        count * side * side, width
    )


def adamw(weight, grad, moment, square, average, rate, decay):
    momentum = beta_one * moment + (1.0 - beta_one) * grad
    variance = beta_two * square + (1.0 - beta_two) * grad * grad
    scaled_m = momentum / (1.0 - beta_one**STEP)
    scaled_v = variance / (1.0 - beta_two**STEP)
    updated = weight - rate * (scaled_m / (jnp.sqrt(scaled_v) + adam_eps) + decay * weight)
    smoothed = ema_keep * average + (1.0 - ema_keep) * updated
    return (updated, momentum, variance, smoothed, updated.astype(jnp.bfloat16))


def shards(
    patches,
    counts,
    cotangent,
    filters,
    filters_moment,
    filters_square,
    filters_average,
    vectors,
    vectors_moment,
    vectors_square,
    vectors_average,
    expand,
    expand_moment,
    expand_square,
    expand_average,
    project,
    project_moment,
    project_square,
    project_average,
    offsets,
    offsets_moment,
    offsets_square,
    offsets_average,
):
    whole_filters, whole_vectors = (
        lax.all_gather(filters.astype(jnp.bfloat16), ("dp", "wide"), axis=1, tiled=True),
        lax.all_gather(vectors.astype(jnp.bfloat16), ("dp", "wide"), axis=2, tiled=True),
    )
    vec_full = whole_vectors.astype(jnp.float32)
    images = patches.shape[0]
    width = patches.shape[2]
    columns = expand.shape[1]
    samples = counts.shape[0]
    image_index = jnp.arange(images, dtype=jnp.int32)
    owner = image_index // SLOTS
    slot = image_index % SLOTS
    matches = owner[:, None] == jnp.arange(samples, dtype=jnp.int32)[None, :]
    chosen = jnp.sum(jnp.where(matches, counts[None, :], 0), axis=1)
    live = (slot < chosen).astype(jnp.float32)
    mask_rows = jnp.repeat(live, POOL * POOL)[:, None]
    rows = patches.reshape(images * GRID * GRID, width)
    first, first_saved = block_forward(rows, whole_filters[0], whole_filters[1], vec_full[0], GRID)
    pooled = pool(first, GRID).astype(jnp.bfloat16)
    second, second_saved = block_forward(
        pooled, whole_filters[2], whole_filters[3], vec_full[1], POOL
    )
    tokens = (second * mask_rows).astype(jnp.bfloat16)
    expand_low = expand.astype(jnp.bfloat16)
    project_low = project.astype(jnp.bfloat16)
    offsets_low = offsets.astype(jnp.bfloat16)
    d_cols = cotangent.reshape(-1, columns)
    full_expand, full_project, full_offsets = (
        lax.all_gather(expand_low, "wide", axis=1, tiled=True),
        lax.all_gather(project_low, "wide", axis=1, tiled=True),
        lax.all_gather(offsets_low, "wide", axis=1, tiled=True),
    )
    pre = jnp.dot(tokens, full_expand, preferred_element_type=jnp.float32) + full_offsets[0].astype(
        jnp.float32
    )
    hidden_val, gelu_back = jax.vjp(gelu_exact, pre)
    hidden = hidden_val.astype(jnp.bfloat16)
    full_out = jnp.dot(hidden, full_project, preferred_element_type=jnp.float32) + full_offsets[
        1
    ].astype(jnp.float32)
    out_cols = lax.all_to_all(
        full_out.astype(jnp.bfloat16), "wide", split_axis=1, concat_axis=0, tiled=True
    )
    readout = out_cols.reshape(-1, POOL * POOL, columns)
    d_full = lax.all_to_all(d_cols, "wide", split_axis=0, concat_axis=1, tiled=True)
    g_project_full = contract_rows(hidden, d_full)
    g_out_full = jnp.sum(d_full.astype(jnp.float32), axis=0)
    d_hidden = contract_cols(d_full, full_project)
    d_pre = gelu_back(d_hidden)[0].astype(jnp.bfloat16)
    g_expand_full = contract_rows(tokens, d_pre)
    g_in_full = jnp.sum(d_pre.astype(jnp.float32), axis=0)
    d_tokens = contract_cols(d_pre, full_expand)
    g_expand, g_project, g_offsets = (
        lax.psum_scatter(
            g_expand_full.astype(jnp.bfloat16), "wide", scatter_dimension=1, tiled=True
        ).astype(jnp.float32),
        lax.psum_scatter(
            g_project_full.astype(jnp.bfloat16), "wide", scatter_dimension=1, tiled=True
        ).astype(jnp.float32),
        lax.psum_scatter(
            jnp.stack([g_in_full, g_out_full]).astype(jnp.bfloat16),
            "wide",
            scatter_dimension=1,
            tiled=True,
        ).astype(jnp.float32),
    )
    g_expand, g_project, g_offsets = (
        lax.psum(g_expand.astype(jnp.bfloat16), "dp").astype(jnp.float32),
        lax.psum(g_project.astype(jnp.bfloat16), "dp").astype(jnp.float32),
        lax.psum(g_offsets.astype(jnp.bfloat16), "dp").astype(jnp.float32),
    )
    d_second = d_tokens * mask_rows
    d_pooled, g_in_two, g_out_two, g_vec_two = block_backward(
        d_second, second_saved, whole_filters[2], whole_filters[3]
    )
    d_first = unpool(d_pooled, GRID)
    d_rows, g_in_one, g_out_one, g_vec_one = block_backward(
        d_first, first_saved, whole_filters[0], whole_filters[1]
    )
    patch_gradient = d_rows.astype(jnp.bfloat16).reshape(images, GRID * GRID, width)
    g_filters = jnp.stack([g_in_one, g_out_one, g_in_two, g_out_two])
    g_vectors = jnp.stack([g_vec_one, g_vec_two])
    g_filters, g_vectors = (
        lax.psum_scatter(g_filters, ("dp", "wide"), scatter_dimension=1, tiled=True),
        lax.psum_scatter(g_vectors, ("dp", "wide"), scatter_dimension=2, tiled=True),
    )
    filters_out = adamw(
        filters, g_filters, filters_moment, filters_square, filters_average, 0.03, 0.05
    )
    vectors_out = adamw(
        vectors, g_vectors, vectors_moment, vectors_square, vectors_average, 0.3, 0.0
    )
    expand_out = adamw(expand, g_expand, expand_moment, expand_square, expand_average, 0.03, 0.05)
    project_out = adamw(
        project, g_project, project_moment, project_square, project_average, 0.016, 0.05
    )
    offsets_out = adamw(
        offsets, g_offsets, offsets_moment, offsets_square, offsets_average, 0.1, 0.0
    )
    return (
        readout,
        patch_gradient,
        filters_out[0],
        filters_out[1],
        filters_out[2],
        filters_out[3],
        filters_out[4],
        vectors_out[0],
        vectors_out[1],
        vectors_out[2],
        vectors_out[3],
        vectors_out[4],
        expand_out[0],
        expand_out[1],
        expand_out[2],
        expand_out[3],
        expand_out[4],
        project_out[0],
        project_out[1],
        project_out[2],
        project_out[3],
        project_out[4],
        offsets_out[0],
        offsets_out[1],
        offsets_out[2],
        offsets_out[3],
        offsets_out[4],
    )


def solution(mesh):
    in_specs = (
        P(("dp", "wide"), None, None),
        P(("dp", "wide")),
        P("dp", None, "wide"),
        P(None, ("dp", "wide"), None),
        P(None, ("dp", "wide"), None),
        P(None, ("dp", "wide"), None),
        P(None, ("dp", "wide"), None),
        P(None, None, ("dp", "wide")),
        P(None, None, ("dp", "wide")),
        P(None, None, ("dp", "wide")),
        P(None, None, ("dp", "wide")),
        P(None, "wide"),
        P(None, "wide"),
        P(None, "wide"),
        P(None, "wide"),
        P(None, "wide"),
        P(None, "wide"),
        P(None, "wide"),
        P(None, "wide"),
        P(None, "wide"),
        P(None, "wide"),
        P(None, "wide"),
        P(None, "wide"),
    )
    out_specs = (
        P("dp", None, "wide"),
        P(("dp", "wide"), None, None),
        P(None, ("dp", "wide"), None),
        P(None, ("dp", "wide"), None),
        P(None, ("dp", "wide"), None),
        P(None, ("dp", "wide"), None),
        P(None, ("dp", "wide"), None),
        P(None, None, ("dp", "wide")),
        P(None, None, ("dp", "wide")),
        P(None, None, ("dp", "wide")),
        P(None, None, ("dp", "wide")),
        P(None, None, ("dp", "wide")),
        P(None, "wide"),
        P(None, "wide"),
        P(None, "wide"),
        P(None, "wide"),
        P(None, "wide"),
        P(None, "wide"),
        P(None, "wide"),
        P(None, "wide"),
        P(None, "wide"),
        P(None, "wide"),
        P(None, "wide"),
        P(None, "wide"),
        P(None, "wide"),
        P(None, "wide"),
        P(None, "wide"),
    )
    return jax.shard_map(shards, mesh=mesh, in_specs=in_specs, out_specs=out_specs, check_vma=False)
```

profile of v0, /device:TPU:0, one launch (start us, length us, event | category | flops | bytes accessed | tf_op | source)
XLA Modules:
  0.0 1608.2 jit_solution(16742563195878083436)
XLA Ops:
  15.0 7.4 all-to-all-start.1
  24.0 174.1 %all_gather.16 = bf16[2,15,1024]{1,0,2:T(2,128)(2,1)S(1)} all-gather(bf16[2,15,32]{1,0,2:T(2,128)(2,1)S(1)} %copy.143), channel_id=1, replica_groups=mesh['dp'=2,'wide'=16] {'dp','wide'}, dimensions={2}, use_global_device_ids=true | all-gather | bytes 63360 | tf_op jit(solution)/shard_map/all_gather | solution.py:148
  198.5 17.7 %all_gather.18 = bf16[2,4096]{1,0:T(2,128)(2,1)S(1)} all-gather(bf16[2,256]{1,0:T(2,128)(2,1)S(1)} %convert_element_type.149), channel_id=1, replica_groups=mesh['dp'=2,'wide'=16] {'wide'}, dimensions={1}, use_global_device_ids=true | all-gather | bytes 17408 | tf_op jit(solution)/shard_map/all_gather | solution.py:176
  216.2 42.8 %slice_reduce_fusion.27 = (f32[1024]{0:T(1024)S(1)}, f32[1024]{0:T(1024)S(1)}, f32[1024]{0:T(1024)S(1)}, f32[1024]{0:T(1024)S(1)}, f32[1024]{0:T(1024)S(1)}, /*i...) fusion(f32[2,15,1024]{1,0,2:T(2,128)S(1)} %convert_element_type.138), kind=kLoop, calls=%fused_computation.225 | loop fusion | bytes 90112 | tf_op jit(solution)/shard_map/jvp()/slice | solution.py:36
  259.8 77.1 %slice_reduce_fusion.3 = (f32[1024]{0:T(1024)S(1)}, f32[1024]{0:T(1024)}, f32[1024]{0:T(1024)}, f32[1024]{0:T(1024)}, f32[1024]{0:T(1024)S(1)}, /*index=5*/f32[1...) fusion(f32[2,15,1024]{1,0,2:T(2,128)S(1)} %convert_element_type.138), kind=kLoop, calls=%fused_computation.201 | loop fusion | bytes 155648 | tf_op jit(solution)/shard_map/jvp()/slice | solution.py:48
  337.0 5.2 copy.170
  342.2 7.7 fusion.70
  353.6 5.8 fusion.13
  359.4 32.7 %fusion.69 = (f32[4,24,24]{2,1,0:T(8,128)S(1)}, f32[4,24,24,1024]{3,2,1,0:T(8,128)}) fusion(f32[1024]{0:T(1024)S(1)} %get-tuple-element.216, f32[1024]{0:T(1024)S(1)} %get-tuple-element.217, f32[1024]{0:T(1024)S(1)} %get-tuple-element.218, f32[1024]{0:T(1024)S(1)} %get-tuple-element.219, f32[4,24,24,1024]{3,2,1,0:T(8,128)} %bitcast.154, ...), kind=kLoop, calls=%fused_computation.303 | loop fusion | flops 42465024 | bytes 18920448 | tf_op jit(solution)/shard_map/jvp()/reduce_sum | solution.py:22
  392.2 5.7 multiply_reduce_fusion.16
  403.0 6.9 fusion.71
  413.6 6.2 fusion.12
  419.8 12.3 reshape.572
  432.1 10.3 reduce_sum.510
  471.0 12.3 fusion.46
  483.4 49.1 %fusion.49 = (bf16[4096]{0:T(1024)(128)(2,1)}, bf16[576,4096]{1,0:T(8,128)(2,1)}, f32[576,4096]{1,0:T(8,128)}) fusion(f32[576,4096]{1,0:T(8,128)} %fusion.46, f32[4096]{0:T(1024)S(1)} %bitcast.172, bf16[576,4096]{1,0:T(8,128)(2,1)} %bitcast.166, bf16[4096,4096]{1,0:T(8,128)(2,1)} %all-gather.8.cloned.1.call-done), kind=kOutput, calls=%fused_computation.291 | convolution fusion | flops 19501936640 | bytes 61890560 | tf_op jit(solution)/shard_map/dot_general | solution.py:66
  532.5 12.1 convolution_convert_fusion.1
  544.7 11.1 multiply_convert_fusion.1
  555.8 33.6 %convolution_convert_fusion = bf16[4096,4096]{1,0:T(8,128)(2,1)} fusion(bf16[576,4096]{1,0:T(8,128)(2,1)} %multiply_convert_fusion.1, bf16[576,4096]{1,0:T(8,128)(2,1)} %bitcast.167), kind=kOutput, calls=%fused_computation | convolution fusion | flops 19344130048 | bytes 42991616 | tf_op jit(solution)/shard_map/dot_general | solution.py:60
  596.6 13.1 multiply_reduce_fusion.27
  626.4 18.6 %multiply_reduce_fusion.25 = (f32[1024]{0:T(1024)}, f32[1024]{0:T(1024)}, f32[1024]{0:T(1024)}, f32[1024]{0:T(1024)}, f32[1024]{0:T(1024)}, /*index=5*/f32[1024]...) fusion(f32[4,12,12,1024]{3,2,1,0:T(8,128)} %reshape.576, ...), kind=kLoop, calls=%fused_computation.128 | loop fusion | flops 14737408 | bytes 26021888 | tf_op jit(solution)/shard_map/transpose(jvp())/reduce_sum | solution.py:36
  645.0 5.4 pad_add_fusion.7
  650.4 6.7 pad_add_fusion.8
  675.9 5.5 broadcast_in_dim.147
  681.4 14.3 reshape.578
  695.7 15.6 multiply_reduce_fusion
  711.4 12.2 fusion.62
  723.7 16.1 multiply_reduce_fusion.11
  739.8 7.2 fusion.61
  747.2 6.1 multiply_reduce_fusion.6
  753.4 57.0 %multiply_reduce_fusion.10 = (f32[1024]{0:T(1024)S(1)}, f32[1024]{0:T(1024)S(1)}, f32[1024]{0:T(1024)S(1)}, f32[1024]{0:T(1024)S(1)}, f32[1024]{0:T(1024)S(1)}, ...) fusion(f32[4,24,24,1024]{3,2,1,0:T(8,128)} %bitcast.156, ...), kind=kLoop, calls=%fused_computation.44 | loop fusion | flops 58974208 | bytes 103878656 | tf_op jit(solution)/shard_map/transpose(jvp())/reduce_sum | solution.py:36
  810.4 15.6 pad_add_fusion
  826.1 29.6 %pad_add_fusion.1 = f32[4,24,24,1024]{3,2,1,0:T(8,128)} fusion(f32[4,24,24,1024]{3,2,1,0:T(8,128)} %get-tuple-element.275, f32[4,24,24,1024]{3,2,1,0:T(8,128)} %get-tuple-element.276, f32[4,24,24,1024]{3,2,1,0:T(8,128)} %get-tuple-element.277, f32[4,24,24,1024]{3,2,1,0:T(8,128)} %get-tuple-element.278, f32[4,24,24,1024]{3,2,1,0:T(8,128)} %get-tuple-element.279, ...), kind=kLoop, calls=%fused_computation.25 | loop fusion | flops 14155776 | bytes 75497472 | tf_op jit(solution)/shard_map/transpose(jvp())/add_any | solution.py:36
  855.7 10.9 multiply_reduce_fusion.1
  866.7 10.7 fusion.59
  881.6 5.8 convolution_bitcast_fusion
  887.5 6.9 convolution_bitcast_fusion.2
  894.7 10.6 convolution_bitcast_fusion.3
  907.6 12.0 pad_maximum_fusion
  919.6 20.2 %copy.149 = f32[4,1024,1024]{2,0,1:T(4,128)} copy(f32[4,1024,1024]{1,2,0:T(8,128)} %pad_maximum_fusion) | data formatting | bytes 33554432 | tf_op jit(solution)/shard_map/stack | solution.py:226
  940.5 25.2 %add_convert_fusion.4 = bf16[576,4096]{1,0:T(8,128)(2,1)S(1)} fusion(bf16[576,4096]{1,0:T(8,128)(2,1)} %multiply_convert_fusion.1, bf16[4096,4096]{1,0:T(8,128)(2,1)} %all-gather.8.cloned.1.call-done, f32[4096]{0:T(1024)S(1)} %bitcast.200), kind=kOutput, calls=%fused_computation.56 | convolution fusion | flops 19332071424 | bytes 43008000 | tf_op jit(solution)/shard_map/dot_general | solution.py:183
  973.0 43.0 %reduce-scatter.11.cloned.1.call-done = bf16[4096,256]{1,0:T(8,128)(2,1)} async-done(((bf16[4096,4096]{1,0:T(8,128)(2,1)}), bf16[4096,256]{1,0:T(8,128)(2,1)}) %reduce-scatter.11.cloned.1.call-update) | async-done | bytes 2097168 | tf_op jit(solution)/shard_map/reduce_scatter | solution.py:202
  1016.2 11.5 add_convert_fusion
  1027.7 58.1 %reduce-scatter.15.cloned.1.call-done = bf16[256,2]{1,0:T(8,128)(2,1)} async-done(((bf16[4096,2]{1,0:T(8,128)(2,1)}), bf16[256,2]{1,0:T(8,128)(2,1)}) %reduce-scatter.15.cloned.1.call-update) | async-done | bytes 1040
  1092.8 129.5 %reduce-scatter.13.cloned.1.call-done = f32[32,30]{1,0:T(8,128)} async-done(((f32[1024,30]{1,0:T(8,128)}), f32[32,30]{1,0:T(8,128)}) %reduce-scatter.13.cloned.1.call-update) | async-done | bytes 3856
  1226.3 276.3 %all-reduce.57.cloned.1.call-done = f32[4,1024,1024]{2,0,1:T(4,128)} async-done(((f32[4,1024,1024]{2,0,1:T(4,128)}), f32[4,1024,1024]{2,0,1:T(4,128)}) %all-reduce.57.cloned.1.call-update) | async-done | bytes 16777232
  1508.6 70.8 %all-reduce.59.cloned.1.call-done = (bf16[1024,256]{1,0:T(8,128)(2,1)}, bf16[4096,256]{1,0:T(8,128)(2,1)}) async-done(((bf16[1024,256]{1,0:T(8,128)(2,1)}, bf16[4096,256]{1,0:T(8,128)(2,1)}), (bf16[1024,256]{1,0:T(8,128)(2,1)}, bf16[4096,256]{1,0:T(8,128)(2,1)})) %all-reduce.59.cloned.1.call-update) | async-done | bytes 2621456 | tf_op jit(solution)/shard_map/psum | solution.py:213
  1586.5 6.9 fusion.51
  (472 shorter events, 139.5 us)
Async XLA Ops:
  7.2 335.0 %all-gather.4.cloned.1.call-start = ((), (), s32[]{:S(2)}) async-start(), calls=%async_computation.6 | async-start | bytes 8650752 | tf_op jit(solution)/shard_map/all_gather | solution.py:147
  9.1 462.0 %all-gather.6.cloned.1.call-start = ((), (), s32[]{:S(2)}) async-start(), calls=%async_computation.7 | async-start | bytes 8912896 | tf_op jit(solution)/shard_map/all_gather | solution.py:174
  11.2 472.2 %all-gather.8.cloned.1.call-start = ((), (), s32[]{:S(2)}) async-start(), calls=%async_computation.8 | async-start | bytes 35651584 | tf_op jit(solution)/shard_map/all_gather | solution.py:175
  15.0 322.0 %all-to-all-start.1 = ((bf16[16,576,256]{2,1,0:T(8,128)(2,1)}), bf16[16,576,256]{2,1,0:T(8,128)(2,1)}, u32[]{:S(2)}, u32[]{:S(2)}) async-start(bf16[16,576,256]{2,1,0:T(8,128)(2,1)} %bitcast.165), calls=%async_computation.1 | async-start | bytes 9437184 | tf_op jit(solution)/shard_map/all_to_all | solution.py:190
  22.4 950.6 %reduce-scatter.9.cloned.1.call-start = ((), (), s32[]{:S(2)}) async-start(), calls=%async_computation.9 | async-start | bytes 8912896 | tf_op jit(solution)/shard_map/reduce_scatter | solution.py:199
  259.0 92.0 %copy-start.56 = (f32[1024]{0:T(1024)}, f32[1024]{0:T(1024)S(1)}, u32[]{:S(2)}) copy-start(f32[1024]{0:T(1024)S(1)} %get-tuple-element.225) | copy-start | bytes 12292
  259.0 92.0 %copy-start.62 = (f32[1024]{0:T(1024)}, f32[1024]{0:T(1024)S(1)}, u32[]{:S(2)}) copy-start(f32[1024]{0:T(1024)S(1)} %get-tuple-element.224) | copy-start | bytes 12292
  259.0 100.3 %copy-start.69 = (f32[1024]{0:T(1024)}, f32[1024]{0:T(1024)S(1)}, u32[]{:S(2)}) copy-start(f32[1024]{0:T(1024)S(1)} %get-tuple-element.215) | copy-start | bytes 12292
  259.1 100.3 %copy-start.71 = (f32[1024]{0:T(1024)}, f32[1024]{0:T(1024)S(1)}, u32[]{:S(2)}) copy-start(f32[1024]{0:T(1024)S(1)} %get-tuple-element.216) | copy-start | bytes 12292
  259.1 100.3 %copy-start.73 = (f32[1024]{0:T(1024)}, f32[1024]{0:T(1024)S(1)}, u32[]{:S(2)}) copy-start(f32[1024]{0:T(1024)S(1)} %get-tuple-element.217) | copy-start | bytes 12292
  259.1 100.3 %copy-start.75 = (f32[1024]{0:T(1024)}, f32[1024]{0:T(1024)S(1)}, u32[]{:S(2)}) copy-start(f32[1024]{0:T(1024)S(1)} %get-tuple-element.218) | copy-start | bytes 12292
  259.1 100.3 %copy-start.77 = (f32[1024]{0:T(1024)}, f32[1024]{0:T(1024)S(1)}, u32[]{:S(2)}) copy-start(f32[1024]{0:T(1024)S(1)} %get-tuple-element.219) | copy-start | bytes 12292
  259.1 100.3 %copy-start.79 = (f32[1024]{0:T(1024)}, f32[1024]{0:T(1024)S(1)}, u32[]{:S(2)}) copy-start(f32[1024]{0:T(1024)S(1)} %get-tuple-element.220) | copy-start | bytes 12292
  259.1 100.3 %copy-start.81 = (f32[1024]{0:T(1024)}, f32[1024]{0:T(1024)S(1)}, u32[]{:S(2)}) copy-start(f32[1024]{0:T(1024)S(1)} %get-tuple-element.221) | copy-start | bytes 12292
  259.1 100.3 %copy-start.83 = (f32[1024]{0:T(1024)}, f32[1024]{0:T(1024)S(1)}, u32[]{:S(2)}) copy-start(f32[1024]{0:T(1024)S(1)} %get-tuple-element.222) | copy-start | bytes 12292
  259.1 100.3 %copy-start.85 = (f32[1024]{0:T(1024)}, f32[1024]{0:T(1024)S(1)}, u32[]{:S(2)}) copy-start(f32[1024]{0:T(1024)S(1)} %get-tuple-element.223) | copy-start | bytes 12292
  336.9 75.3 %copy-start.58 = (f32[1024]{0:T(1024)}, f32[1024]{0:T(1024)S(1)}, u32[]{:S(2)}) copy-start(f32[1024]{0:T(1024)S(1)} %get-tuple-element.212) | copy-start | bytes 12292
  336.9 75.4 %copy-start.89 = (f32[1024]{0:T(1024)}, f32[1024]{0:T(1024)S(1)}, u32[]{:S(2)}) copy-start(f32[1024]{0:T(1024)S(1)} %get-tuple-element.211) | copy-start | bytes 12292
  336.9 113.3 %copy-start.52 = (f32[1024]{0:T(1024)}, f32[1024]{0:T(1024)S(1)}, u32[]{:S(2)}) copy-start(f32[1024]{0:T(1024)S(1)} %get-tuple-element.210) | copy-start | bytes 12292
  336.9 113.3 %copy-start.60 = (f32[1024]{0:T(1024)}, f32[1024]{0:T(1024)S(1)}, u32[]{:S(2)}) copy-start(f32[1024]{0:T(1024)S(1)} %get-tuple-element.209) | copy-start | bytes 12292
  336.9 119.0 %copy-start.98 = (f32[1024]{0:T(1024)}, f32[1024]{0:T(1024)S(1)}, u32[]{:S(2)}) copy-start(f32[1024]{0:T(1024)S(1)} %get-tuple-element.200) | copy-start | bytes 12292
  336.9 119.0 %copy-start.100 = (f32[1024]{0:T(1024)}, f32[1024]{0:T(1024)S(1)}, u32[]{:S(2)}) copy-start(f32[1024]{0:T(1024)S(1)} %get-tuple-element.201) | copy-start | bytes 12292
  336.9 119.0 %copy-start.102 = (f32[1024]{0:T(1024)}, f32[1024]{0:T(1024)S(1)}, u32[]{:S(2)}) copy-start(f32[1024]{0:T(1024)S(1)} %get-tuple-element.202) | copy-start | bytes 12292
  337.0 119.0 %copy-start.104 = (f32[1024]{0:T(1024)}, f32[1024]{0:T(1024)S(1)}, u32[]{:S(2)}) copy-start(f32[1024]{0:T(1024)S(1)} %get-tuple-element.203) | copy-start | bytes 12292
  337.0 119.0 %copy-start.106 = (f32[1024]{0:T(1024)}, f32[1024]{0:T(1024)S(1)}, u32[]{:S(2)}) copy-start(f32[1024]{0:T(1024)S(1)} %get-tuple-element.204) | copy-start | bytes 12292
  337.0 119.0 %copy-start.108 = (f32[1024]{0:T(1024)}, f32[1024]{0:T(1024)S(1)}, u32[]{:S(2)}) copy-start(f32[1024]{0:T(1024)S(1)} %get-tuple-element.205) | copy-start | bytes 12292
  337.0 119.0 %copy-start.110 = (f32[1024]{0:T(1024)}, f32[1024]{0:T(1024)S(1)}, u32[]{:S(2)}) copy-start(f32[1024]{0:T(1024)S(1)} %get-tuple-element.206) | copy-start | bytes 12292
  337.0 125.2 %copy-start.66 = (f32[1024]{0:T(1024)}, f32[1024]{0:T(1024)S(1)}, u32[]{:S(2)}) copy-start(f32[1024]{0:T(1024)S(1)} %get-tuple-element.196) | copy-start | bytes 12292
  468.8 63.7 %copy-start.11 = (f32[576,1024]{1,0:T(8,128)}, f32[576,1024]{1,0:T(8,128)S(1)}, u32[]{:S(2)}) copy-start(f32[576,1024]{1,0:T(8,128)S(1)} %get-tuple-element.306) | copy-start | bytes 7077892
  544.6 471.4 %reduce-scatter.11.cloned.1.call-start = ((), (), s32[]{:S(2)}) async-start(), calls=%async_computation.10 | async-start | bytes 35651584 | tf_op jit(solution)/shard_map/reduce_scatter | solution.py:202
  589.6 496.2 %reduce-scatter.15.cloned.1.call-start = ((), (), s32[]{:S(2)}) async-start(), calls=%async_computation.12 | async-start | bytes 1114112
  894.4 327.9 %reduce-scatter.13.cloned.1.call-start = ((), (), s32[]{:S(2)}) async-start(), calls=%async_computation.11 | async-start | bytes 540672
  907.6 595.0 %all-reduce.57.cloned.1.call-start = ((), (), s32[]{:S(2)}) async-start(), calls=%async_computation.13 | async-start | bytes 33554432
  968.4 540.2 %all-to-all-start = ((bf16[576,16,256]{2,0,1:T(8,128)(2,1)}), bf16[576,16,256]{2,0,1:T(8,128)(2,1)}, u32[]{:S(2)}, u32[]{:S(2)}) async-start(bf16[576,16,256]{2,0,1:T(8,128)(2,1)} %bitcast.161), calls=%async_computation | async-start | bytes 9437184 | tf_op jit(solution)/shard_map/all_to_all | solution.py:186
  972.9 606.5 %all-reduce.59.cloned.1.call-start = ((), (), s32[]{:S(2)}) async-start(), calls=%async_computation.14 | async-start | bytes 5242880 | tf_op jit(solution)/shard_map/psum | solution.py:213
  1016.1 75.6 %copy-start.142 = (f32[2,256]{1,0:T(2,128)S(1)}, f32[2,256]{1,0:T(2,128)}, u32[]{:S(2)}) copy-start(f32[2,256]{1,0:T(2,128)} %param.42) | copy-start | bytes 6148
  1016.1 75.6 %copy-start.155 = (f32[2,256]{1,0:T(2,128)S(1)}, f32[2,256]{1,0:T(2,128)}, u32[]{:S(2)}) copy-start(f32[2,256]{1,0:T(2,128)} %param.43) | copy-start | bytes 6148
  1016.1 75.6 %copy-start.156 = (f32[2,256]{1,0:T(2,128)S(1)}, f32[2,256]{1,0:T(2,128)}, u32[]{:S(2)}) copy-start(f32[2,256]{1,0:T(2,128)} %param.44) | copy-start | bytes 6148
  1016.1 76.2 %copy-start.157 = (f32[2,256]{1,0:T(2,128)S(1)}, f32[2,256]{1,0:T(2,128)}, u32[]{:S(2)}) copy-start(f32[2,256]{1,0:T(2,128)} %param.45) | copy-start | bytes 6148
  1016.1 207.1 %copy-start.65 = (f32[2,15,32]{2,0,1:T(2,128)S(1)}, f32[2,15,32]{2,0,1:T(2,128)}, u32[]{:S(2)}) copy-start(f32[2,15,32]{2,0,1:T(2,128)} %param.30) | copy-start | bytes 11524
  1016.1 207.1 %copy-start.137 = (f32[2,15,32]{2,0,1:T(2,128)S(1)}, f32[2,15,32]{2,0,1:T(2,128)}, u32[]{:S(2)}) copy-start(f32[2,15,32]{2,0,1:T(2,128)} %param.31) | copy-start | bytes 11524
  1016.1 207.1 %copy-start.138 = (f32[2,15,32]{2,0,1:T(2,128)S(1)}, f32[2,15,32]{2,0,1:T(2,128)}, u32[]{:S(2)}) copy-start(f32[2,15,32]{2,0,1:T(2,128)} %param.32) | copy-start | bytes 11524
  1016.1 209.5 %copy-start.136 = (f32[2,15,32]{2,0,1:T(2,128)S(1)}, f32[2,15,32]{2,0,1:T(2,128)}, u32[]{:S(2)}) copy-start(f32[2,15,32]{2,0,1:T(2,128)} %param.33) | copy-start | bytes 11524
  1016.1 487.6 %copy-start.27 = (f32[4,32,1024]{2,1,0:T(8,128)S(1)}, f32[4,32,1024]{2,1,0:T(8,128)}, u32[]{:S(2)}) copy-start(f32[4,32,1024]{2,1,0:T(8,128)} %param.26) | copy-start | bytes 1572868
  1027.7 551.7 %copy-start.18 = (f32[1024,256]{1,0:T(8,128)S(1)}, f32[1024,256]{1,0:T(8,128)}, u32[]{:S(2)}) copy-start(f32[1024,256]{1,0:T(8,128)} %param.34) | copy-start | bytes 3145732
  1027.7 551.7 %copy-start.31 = (f32[1024,256]{1,0:T(8,128)S(1)}, f32[1024,256]{1,0:T(8,128)}, u32[]{:S(2)}) copy-start(f32[1024,256]{1,0:T(8,128)} %param.35) | copy-start | bytes 3145732
  1092.2 490.7 %copy-start.140 = (f32[2,256]{1,0:T(2,128)}, f32[2,256]{1,0:T(2,128)S(1)}, u32[]{:S(2)}) copy-start(f32[2,256]{1,0:T(2,128)S(1)} %get-tuple-element.361) | copy-start | bytes 6148
  1506.5 79.9 %copy-start.26 = (f32[4,32,1024]{2,1,0:T(8,128)}, f32[4,32,1024]{2,1,0:T(8,128)S(1)}, u32[]{:S(2)}) copy-start(f32[4,32,1024]{2,1,0:T(8,128)S(1)} %get-tuple-element.341) | copy-start | bytes 1572868
  (134 other events, 1339.8 us)
Sparse Core Ops, SparseCore 0:
  11.5 147.9 all-gather.3
  162.2 79.9 all-gather.5
  244.3 175.2 all-gather.7
  544.8 105.2 reduce-scatter.8
  654.1 361.8 reduce-scatter.10
  1020.1 65.6 reduce-scatter.14
  1088.7 133.5 reduce-scatter.12
  1228.3 274.2 all-reduce.56
  1505.0 74.4 all-reduce.58
where the time goes:
time: 1620 us; the launch traced here: 1610 us
  waiting for transfers between devices  578 us (36%)
  other arithmetic  344 us (21%)
  matrix products  232 us (14%)
  local copies, waits for them, and re-layouts  228 us (14%)
  blocking collectives  197 us (12%)
  between operations  17.1 us (1%)
    unnamed x12, waiting for transfers between devices  464 us
    all_gather x1, blocking collectives, shards(): lax.all_gather(vectors.astype(jnp.bfloat16), ('dp', 'wide'), axis=2, tile...  174 us
    dot_general x6, matrix products, contract_cols(): lax.dot_general(left, right, (((1,), (1,)), ((), ())), preferred_element_...  99.6 us
    reduce_sum x4, other arithmetic, depthwise(): padded[:, row:row + side, column:column + side, :] * taps[row * 3 + column]  84.8 us
    slice x1, local copies, waits for them, and re-layouts, middle(): return jax.nn.silu(layer_norm(mixed, vecs[11], vecs[12]))  77.1 us
    dot_general x6, matrix products, contract_rows(): lax.dot_general(left, right, (((0,), (0,)), ((), ())), preferred_element_...  73.1 us
    psum x1, waiting for transfers between devices, shards(): lax.psum(g_expand.astype(jnp.bfloat16), 'dp').astype(jnp.float32)  70.8 us
    add_any x4, other arithmetic, depthwise(): padded[:, row:row + side, column:column + side, :] * taps[row * 3 + column]  57.4 us
  transfers between devices with their start and end apart: 11, of which 5 were waited for; matrix products, arithmetic and copies ran while one was open for 44% of the time, Pallas kernels for 0%

commit v1 on v0

v1 whole, which is shorter than its diff:
```python
import math
from functools import partial

import jax
import jax.numpy as jnp
from jax import lax
from jax.experimental import pallas as pl
from jax.experimental.pallas import tpu as pltpu
from jax.sharding import Mesh
from jax.sharding import PartitionSpec as P

GRID = 24
POOL = 12
SLOTS = 4
STEP = 3
LINE = 4
WIDE = ("line", "spot")
ALL = ("dp", "line", "spot")


beta_one = 0.5
beta_two = 0.5
adam_eps = 1e-08
ema_keep = 0.75
norm_eps = 1e-06


def contract_rows(left, right):
    return lax.dot_general(
        left, right, (((0,), (0,)), ((), ())), preferred_element_type=jnp.float32
    )


def contract_cols(left, right):
    return lax.dot_general(
        left, right, (((1,), (1,)), ((), ())), preferred_element_type=jnp.float32
    )


CHUNK = 48
LANE = 128


def shape_of(shape, kind):
    return jax.ShapeDtypeStruct(shape, kind)


def sigmoid(value):
    return 0.5 * jnp.tanh(0.5 * value) + 0.5


def fold_rows(value):
    return jnp.sum(value.reshape(value.shape[0] // 8, 8, value.shape[1]), axis=0)


def row_span(k, size):
    return pl.ds(pl.multiple_of(k * size, 16), size)


def lane_span(j):
    return pl.ds(j * LANE, LANE)


def row_total(parts):
    total = parts[0]
    for part in parts[1:]:
        total = total + part
    return jnp.sum(total, axis=1, keepdims=True)


def normalize(read, norm_ref, scale_ref, span, finish):
    width = norm_ref.shape[1]
    spans = [lane_span(j) for j in range(width // LANE)]
    center = row_total([read(lanes) for lanes in spans]) * (1.0 / width)
    spread = row_total([jnp.square(read(lanes) - center) for lanes in spans]) * (1.0 / width)
    scale = lax.rsqrt(spread + norm_eps)
    scale_ref[span, :] = jnp.broadcast_to(scale, (span.size, LANE))
    for lanes in spans:
        unit = (read(lanes) - center) * scale
        norm_ref[span, lanes] = unit
        finish(lanes, unit)


def shift_rows(value, amount, mask):
    return pltpu.roll(value, amount % value.shape[0], 0) * mask


def masks_for(side, rows):
    cell = jnp.arange(rows, dtype=jnp.int32)
    x, y = cell % side, (cell // side) % side
    flags = jnp.stack([x > 0, x < side - 1, y > 0, y < side - 1]).astype(jnp.float32)
    return jnp.broadcast_to(flags[:, :, None], (4, rows, LANE))


def conv_block(above, level, below, taps, mask_ref):
    columns = [
        taps[c] * above + taps[3 + c] * level + taps[6 + c] * below for c in range(3)
    ]
    return (
        columns[1]
        + shift_rows(columns[0], 1, mask_ref[0])
        + shift_rows(columns[2], -1, mask_ref[1])
    )


def taps_at(vec_ref, lanes):
    return [vec_ref[k : k + 1, lanes] for k in range(9)]


def forward_kernel(side, *refs):
    pooled = side == GRID
    if pooled:
        x_ref, in_ref, out_ref, vec_ref, mask_ref, pool_ref = refs[:6]
        n1_ref, n2_ref, n3_ref, r1_ref, r2_ref, r3_ref, b_ref, y_ref = refs[6:14]
        lin_ref, act_ref, hi_ref, lo_ref = refs[14:]
    else:
        live_ref, x_ref, in_ref, out_ref, vec_ref, mask_ref = refs[:6]
        n1_ref, n2_ref, n3_ref, r1_ref, r2_ref, r3_ref, b_ref, y_ref = refs[6:14]
        lin_ref, act_ref = refs[14:]
    rows, width = x_ref.shape
    count = rows // CHUNK
    edge = side if pooled else 0
    lin_ref[...] = jnp.dot(x_ref[...], in_ref[...], preferred_element_type=jnp.float32)
    if pooled:
        act_ref[0:side, :] = jnp.zeros((side, width), jnp.float32)
        act_ref[rows + side : rows + 2 * side, :] = jnp.zeros((side, width), jnp.float32)

    @pl.loop(0, count)
    def _(k):
        span = row_span(k, CHUNK)
        above = pl.ds(pl.multiple_of(k * CHUNK + edge, 8), CHUNK)

        def finish(lanes, unit):
            value = unit * vec_ref[9:10, lanes] + vec_ref[10:11, lanes]
            act_ref[above, lanes] = value * sigmoid(value)

        normalize(lambda lanes: lin_ref[span, lanes], n1_ref, r1_ref, span, finish)

    if pooled:

        @pl.loop(0, count)
        def _(k):
            for j in range(width // LANE):
                lanes = lane_span(j)
                near = [
                    act_ref[pl.ds(pl.multiple_of(k * CHUNK + r * side, 8), CHUNK), lanes]
                    for r in range(3)
                ]
                lin_ref[row_span(k, CHUNK), lanes] = conv_block(
                    near[0], near[1], near[2], taps_at(vec_ref, lanes), mask_ref
                )
    else:
        cells = side * side

        @pl.loop(0, rows // cells)
        def _(k):
            for j in range(width // LANE):
                lanes = lane_span(j)
                level = act_ref[row_span(k, cells), lanes]
                lin_ref[row_span(k, cells), lanes] = conv_block(
                    shift_rows(level, side, mask_ref[2]),
                    level,
                    shift_rows(level, -side, mask_ref[3]),
                    taps_at(vec_ref, lanes),
                    mask_ref,
                )

    @pl.loop(0, count)
    def _(k):
        span = row_span(k, CHUNK)

        def finish(lanes, unit):
            value = unit * vec_ref[11:12, lanes] + vec_ref[12:13, lanes]
            b_ref[span, lanes] = (value * sigmoid(value)).astype(jnp.bfloat16)

        normalize(lambda lanes: lin_ref[span, lanes], n2_ref, r2_ref, span, finish)

    lin_ref[...] = jnp.dot(b_ref[...], out_ref[...], preferred_element_type=jnp.float32)

    @pl.loop(0, count)
    def _(k):
        span = row_span(k, CHUNK)
        if not pooled:
            scale = live_ref[k * CHUNK // (side * side)]

        def finish(lanes, unit):
            value = (
                x_ref[span, lanes].astype(jnp.float32)
                + unit * vec_ref[13:14, lanes]
                + vec_ref[14:15, lanes]
            )
            value = value * sigmoid(value)
            if pooled:
                high = value.astype(jnp.bfloat16)
                hi_ref[span, lanes] = high
                lo_ref[span, lanes] = (value - high.astype(jnp.float32)).astype(jnp.bfloat16)
            else:
                y_ref[span, lanes] = (value * scale).astype(jnp.bfloat16)

        normalize(lambda lanes: lin_ref[span, lanes], n3_ref, r3_ref, span, finish)

    if pooled:
        y_ref[...] = (
            jnp.dot(pool_ref[...], hi_ref[...], preferred_element_type=jnp.float32)
            + jnp.dot(pool_ref[...], lo_ref[...], preferred_element_type=jnp.float32)
        ).astype(jnp.bfloat16)


def backward_kernel(side, *refs):
    pooled = side == GRID
    if pooled:
        up_ref, d_ref, x_ref, in_ref, out_ref, vec_ref, mask_ref = refs[:7]
    else:
        live_ref, d_ref, x_ref, in_ref, out_ref, vec_ref, mask_ref = refs[:7]
    n1_ref, n2_ref, n3_ref, r1_ref, r2_ref, r3_ref = refs[7:13]
    dx_ref, da_ref, dc_ref, sum_ref = refs[13:17]
    res_ref, mix_ref, act_ref = refs[17:20]
    rows, width = x_ref.shape
    count = rows // CHUNK
    edge = side if pooled else 0
    spans = [lane_span(j) for j in range(width // LANE)]

    @pl.when(pl.program_id(0) == 0)
    def _():
        sum_ref[...] = jnp.zeros(sum_ref.shape, jnp.float32)

    def add_sum(k, lanes, value):
        sum_ref[8 * k : 8 * k + 8, lanes] += fold_rows(value)

    if pooled:
        grads = d_ref[...]
        high = grads.astype(jnp.bfloat16)
        low = (grads - high.astype(jnp.float32)).astype(jnp.bfloat16)
        res_ref[...] = jnp.dot(
            up_ref[...], high, preferred_element_type=jnp.float32
        ) + jnp.dot(up_ref[...], low, preferred_element_type=jnp.float32)

    def norm_back(unit_ref, scale_ref, span, gain, read_grad, store):
        first, second = [], []
        for lanes in spans:
            grad = read_grad(lanes) * vec_ref[gain : gain + 1, lanes]
            first.append(grad)
            second.append(grad * unit_ref[span, lanes])
        mean_grad = row_total(first) * (1.0 / width)
        mean_unit = row_total(second) * (1.0 / width)
        for lanes in spans:
            grad = read_grad(lanes) * vec_ref[gain : gain + 1, lanes]
            store(
                lanes,
                scale_ref[span, :]
                * (grad - mean_grad - unit_ref[span, lanes] * mean_unit),
            )

    @pl.loop(0, count)
    def _(k):
        span = row_span(k, CHUNK)
        if not pooled:
            scale = live_ref[k * CHUNK // (side * side)]
        for lanes in spans:
            unit = n3_ref[span, lanes]
            value = (
                x_ref[span, lanes].astype(jnp.float32)
                + unit * vec_ref[13:14, lanes]
                + vec_ref[14:15, lanes]
            )
            gate = sigmoid(value)
            grad = res_ref[span, lanes] if pooled else d_ref[span, lanes] * scale
            grad = grad * (gate * (1.0 + value * (1.0 - gate)))
            res_ref[span, lanes] = grad
            add_sum(13, lanes, grad * unit)
            add_sum(14, lanes, grad)

        def store(lanes, value):
            dc_ref[span, lanes] = value.astype(jnp.bfloat16)

        norm_back(n3_ref, r3_ref, span, 13, lambda lanes: res_ref[span, lanes], store)

    if pooled:
        mix_ref[0:side, :] = jnp.zeros((side, width), jnp.float32)
        mix_ref[rows + side : rows + 2 * side, :] = jnp.zeros((side, width), jnp.float32)
    mix_ref[edge : rows + edge, :] = contract_cols(dc_ref[...], out_ref[...])

    @pl.loop(0, count)
    def _(k):
        span = row_span(k, CHUNK)
        at = pl.ds(pl.multiple_of(k * CHUNK + edge, 8), CHUNK)
        for lanes in spans:
            unit = n2_ref[span, lanes]
            value = unit * vec_ref[11:12, lanes] + vec_ref[12:13, lanes]
            gate = sigmoid(value)
            grad = mix_ref[at, lanes] * (gate * (1.0 + value * (1.0 - gate)))
            mix_ref[at, lanes] = grad
            add_sum(11, lanes, grad * unit)
            add_sum(12, lanes, grad)

        def store(lanes, value):
            mix_ref[at, lanes] = value

        norm_back(n2_ref, r2_ref, span, 11, lambda lanes: mix_ref[at, lanes], store)

    size = CHUNK if pooled else side * side

    @pl.loop(0, rows // size)
    def _(k):
        span = row_span(k, size)
        for lanes in spans:
            if pooled:
                near = [
                    mix_ref[pl.ds(pl.multiple_of(k * size + (2 - r) * side, 8), size), lanes]
                    for r in range(3)
                ]
            else:
                level = mix_ref[span, lanes]
                near = [
                    shift_rows(level, -side, mask_ref[3]),
                    level,
                    shift_rows(level, side, mask_ref[2]),
                ]
            taps = taps_at(vec_ref, lanes)
            mixed = [
                taps[c] * near[0] + taps[3 + c] * near[1] + taps[6 + c] * near[2]
                for c in range(3)
            ]
            grad = (
                mixed[1]
                + shift_rows(mixed[0], -1, mask_ref[1])
                + shift_rows(mixed[2], 1, mask_ref[0])
            )
            unit = n1_ref[span, lanes]
            value = unit * vec_ref[9:10, lanes] + vec_ref[10:11, lanes]
            gate = sigmoid(value)
            active = value * gate
            sides = [
                shift_rows(active, 1, mask_ref[0]),
                active,
                shift_rows(active, -1, mask_ref[1]),
            ]
            for r in range(3):
                for c in range(3):
                    add_sum(3 * r + c, lanes, sides[c] * near[r])
            grad = grad * (gate * (1.0 + value * (1.0 - gate)))
            act_ref[span, lanes] = grad
            add_sum(9, lanes, grad * unit)
            add_sum(10, lanes, grad)

    @pl.loop(0, count)
    def _(k):
        span = row_span(k, CHUNK)

        def store(lanes, value):
            da_ref[span, lanes] = value.astype(jnp.bfloat16)

        norm_back(n1_ref, r1_ref, span, 9, lambda lanes: act_ref[span, lanes], store)

    step = 256
    for j in range(width // step):
        dx_ref[:, j * step : (j + 1) * step] = (
            res_ref[:, j * step : (j + 1) * step]
            + contract_cols(da_ref[...], in_ref[j * step : (j + 1) * step, :])
        ).astype(dx_ref.dtype)


def pool_matrix():
    cell = jnp.arange(GRID * GRID, dtype=jnp.int32)
    home = (cell // GRID // 2) * POOL + (cell % GRID) // 2
    spot = jnp.arange(POOL * POOL, dtype=jnp.int32)
    return jnp.where(home[None, :] == spot[:, None], 0.25, 0.0).astype(jnp.bfloat16)


def block_specs(side, rows, width):
    whole = lambda shape: pl.BlockSpec(shape, lambda i: (0,) * len(shape))
    part = lambda cells, lanes: pl.BlockSpec((cells, lanes), lambda i: (i, 0))
    size = side * side if side == GRID else rows
    return whole, part, size


def kernel_params(axes=1):
    return pltpu.CompilerParams(
        dimension_semantics=("arbitrary",) * axes, vmem_limit_bytes=60 * 1024 * 1024
    )


def block_forward(rows, w_in, w_out, vecs, side, live=None):
    total, width = rows.shape
    whole, part, size = block_specs(side, total, width)
    pooled = side == GRID
    mask_rows = CHUNK if pooled else side * side
    vecs = jnp.pad(vecs, ((0, 1), (0, 0)))
    masks = masks_for(side, mask_rows)
    norm = shape_of((total, width), jnp.float32)
    scale = shape_of((total, LANE), jnp.float32)
    out_cells = POOL * POOL if pooled else size
    operands = [rows, w_in, w_out, vecs, masks]
    in_specs = [
        part(size, width),
        whole(w_in.shape),
        whole(w_out.shape),
        whole(vecs.shape),
        whole(masks.shape),
    ]
    scratch = [
        pltpu.VMEM((size, width), jnp.float32),
        pltpu.VMEM((size + 2 * side, width) if pooled else (size, width), jnp.float32),
    ]
    if pooled:
        operands.append(pool_matrix())
        in_specs.append(whole((POOL * POOL, GRID * GRID)))
        scratch += [pltpu.VMEM((size, width), jnp.bfloat16)] * 2
    else:
        operands.insert(0, live)
        in_specs.insert(0, pl.BlockSpec(memory_space=pltpu.SMEM))
    outs = pl.pallas_call(
        partial(forward_kernel, side),
        grid=(total // size,),
        in_specs=in_specs,
        out_specs=[part(size, width)] * 3
        + [part(size, LANE)] * 3
        + [part(size, width), part(out_cells, width)],
        out_shape=[norm] * 3
        + [scale] * 3
        + [
            shape_of((total, width), jnp.bfloat16),
            shape_of((total // size * out_cells, width), jnp.bfloat16),
        ],
        scratch_shapes=scratch,
        compiler_params=kernel_params(),
        name="block_forward_" + str(side),
    )(*operands)
    return outs[7], (rows, outs[6], tuple(outs[:6]))


def block_backward(d_result, saved, w_in, w_out, vecs, side, live=None):
    rows, narrow, kept = saved
    total, width = rows.shape
    whole, part, size = block_specs(side, total, width)
    pooled = side == GRID
    mask_rows = CHUNK if pooled else side * side
    vecs = jnp.pad(vecs, ((0, 1), (0, 0)))
    masks = masks_for(side, mask_rows)
    in_cells = POOL * POOL if pooled else size
    if pooled:
        first = pool_matrix().T
        first_spec = whole(first.shape)
    else:
        first = live
        first_spec = pl.BlockSpec(memory_space=pltpu.SMEM)
    low = shape_of((total, width), jnp.bfloat16)
    dx, da, dc, sums = pl.pallas_call(
        partial(backward_kernel, side),
        grid=(total // size,),
        in_specs=[
            first_spec,
            part(in_cells, width),
            part(size, width),
            whole(w_in.shape),
            whole(w_out.shape),
            whole(vecs.shape),
            whole(masks.shape),
        ]
        + [part(size, width)] * 3
        + [part(size, LANE)] * 3,
        out_specs=[part(size, width)] * 3 + [whole((128, width))],
        out_shape=[
            shape_of((total, width), jnp.bfloat16 if pooled else jnp.float32),
            low,
            low,
            shape_of((128, width), jnp.float32),
        ],
        scratch_shapes=[
            pltpu.VMEM((size, width), jnp.float32),
            pltpu.VMEM((size + 2 * side, width) if pooled else (size, width), jnp.float32),
            pltpu.VMEM((size, width), jnp.float32),
        ],
        compiler_params=kernel_params(),
        name="block_backward_" + str(side),
    )(first, d_result, rows, w_in, w_out, vecs, masks, *kept)
    grad_out = contract_rows(narrow, dc)
    grad_in = contract_rows(rows, da)
    grad_vecs = jnp.sum(sums[:120].reshape(15, 8, width), axis=1)
    return dx, grad_in, grad_out, grad_vecs


def adamw(weight, grad, moment, square, average, rate, decay):
    momentum = beta_one * moment + (1.0 - beta_one) * grad
    variance = beta_two * square + (1.0 - beta_two) * grad * grad
    scaled_m = momentum / (1.0 - beta_one**STEP)
    scaled_v = variance / (1.0 - beta_two**STEP)
    updated = weight - rate * (scaled_m / (jnp.sqrt(scaled_v) + adam_eps) + decay * weight)
    smoothed = ema_keep * average + (1.0 - ema_keep) * updated
    return (updated, momentum, variance, smoothed, updated.astype(jnp.bfloat16))


def pad_row(row, width):
    return jnp.pad(row, ((0, 0), (0, width - row.shape[1])))


def over_groups(value, group):
    if group == 2:
        other = lax.ppermute(value, "dp", [(0, 1), (1, 0)])
        return value.astype(jnp.float32) + other.astype(jnp.float32)
    return lax.psum(value, "dp").astype(jnp.float32)


def reduce_block(grad_in, grad_out, grad_vecs, devices):
    width = grad_in.shape[1]
    share = width // devices
    rows = [
        grad_in.astype(jnp.bfloat16).reshape(devices, share, width),
        grad_out.astype(jnp.bfloat16).reshape(devices, share, width),
        jnp.pad(
            grad_vecs.astype(jnp.bfloat16)
            .reshape(15, devices, share)
            .transpose(1, 0, 2)
            .reshape(devices, 1, 15 * share),
            ((0, 0), (0, 15), (0, width - 15 * share)),
        ),
    ]
    return jnp.concatenate(rows, axis=1)


def pick(value, at, axis):
    return lax.dynamic_index_in_dim(value, at, axis, False)


def halve_blocks(blocks, order):
    count = blocks.shape[0]
    bits = count.bit_length() - 1
    me = lax.axis_index(ALL)
    blocks = blocks.reshape((2,) * bits + blocks.shape[1:])
    left = list(range(bits))[::-1]
    for bit in order:
        axis = left.index(bit)
        left.pop(axis)
        mine = (me >> bit) & 1
        pairs = [(i, i ^ (1 << bit)) for i in range(count)]
        theirs = lax.ppermute(pick(blocks, 1 - mine, axis), ALL, pairs)
        blocks = (
            pick(blocks, mine, axis).astype(jnp.float32) + theirs.astype(jnp.float32)
        ).astype(jnp.bfloat16)
    return blocks


def spread_reduce(blocks):
    bits = blocks.shape[0].bit_length() - 1
    return halve_blocks(blocks, [0, 1] + list(range(bits - 1, 1, -1)))


def held(value):
    return lax.optimization_barrier(value)


def gelu_slope(value):
    return 0.5 * (1.0 + lax.erf(value * (0.5**0.5))) + value * jnp.exp(-0.5 * value * value) * (
        0.5 / math.pi
    ) ** 0.5


def hidden_kernel(tokens_ref, expand_ref, bias_ref, out_ref):
    pre = jnp.dot(tokens_ref[...], expand_ref[...], preferred_element_type=jnp.float32)
    pre = pre + bias_ref[...]
    out_ref[...] = (0.5 * pre * (1.0 + lax.erf(pre * (0.5**0.5)))).astype(jnp.bfloat16)


def hidden_forward(tokens, readers, bias):
    total, width = tokens.shape
    depth = readers.shape[1]
    rows, step = total // LINE, 512
    return pl.pallas_call(
        hidden_kernel,
        grid=(depth // step, LINE),
        in_specs=[
            pl.BlockSpec((rows, width), lambda j, i: (i, 0)),
            pl.BlockSpec((width, step), lambda j, i: (0, j)),
            pl.BlockSpec((1, step), lambda j, i: (0, j)),
        ],
        out_specs=pl.BlockSpec((rows, step), lambda j, i: (i, j)),
        out_shape=shape_of((total, depth), jnp.bfloat16),
        compiler_params=kernel_params(2),
        name="hidden_forward",
    )(tokens, readers, bias[None])


def adamw_kernel(rate, decay, grad_ref, *refs):
    old, new = refs[:4], refs[4:]
    results = adamw(old[0][...], grad_ref[...].T, *[ref[...] for ref in old[1:]], rate, decay)
    for ref, result in zip(new, results):
        ref[...] = result


def adamw_turned(weight, grad, moment, square, average, rate, decay):
    depth, columns = weight.shape
    step = 512
    part = pl.BlockSpec((step, columns), lambda i: (i, 0))
    return pl.pallas_call(
        partial(adamw_kernel, rate, decay),
        grid=(depth // step,),
        in_specs=[pl.BlockSpec((columns, step), lambda i: (0, i))] + [part] * 4,
        out_specs=[part] * 5,
        out_shape=[shape_of(weight.shape, jnp.float32)] * 4
        + [shape_of(weight.shape, jnp.bfloat16)],
        compiler_params=kernel_params(),
        name="adamw_turned",
    )(grad, weight, moment, square, average)


def pre_kernel(d_ref, tokens_ref, project_ref, expand_ref, bias_ref, out_ref):
    grad = contract_cols(d_ref[...], project_ref[...])
    pre = jnp.dot(tokens_ref[...], expand_ref[...], preferred_element_type=jnp.float32)
    out_ref[...] = (grad * gelu_slope(pre + bias_ref[...])).astype(jnp.bfloat16)


def pre_backward(d_full, tokens, readers, bias):
    rows, width = tokens.shape
    depth = d_full.shape[1]
    step = 512
    skip = width // step
    return pl.pallas_call(
        pre_kernel,
        grid=(depth // step,),
        in_specs=[
            pl.BlockSpec((rows, depth), lambda i: (0, 0)),
            pl.BlockSpec((rows, width), lambda i: (0, 0)),
            pl.BlockSpec((step, depth), lambda i: (i + skip, 0)),
            pl.BlockSpec((width, step), lambda i: (0, i)),
            pl.BlockSpec((1, step), lambda i: (0, i)),
        ],
        out_specs=pl.BlockSpec((rows, step), lambda i: (0, i)),
        out_shape=shape_of((rows, depth), jnp.bfloat16),
        compiler_params=kernel_params(),
        name="pre_backward",
    )(d_full, tokens, readers, readers, bias[None])


def shards(
    patches,
    counts,
    cotangent,
    filters,
    filters_moment,
    filters_square,
    filters_average,
    vectors,
    vectors_moment,
    vectors_square,
    vectors_average,
    expand,
    expand_moment,
    expand_square,
    expand_average,
    project,
    project_moment,
    project_square,
    project_average,
    offsets,
    offsets_moment,
    offsets_square,
    offsets_average,
):
    inner = lax.axis_size("spot")
    wide = LINE * inner
    group = lax.axis_size("dp")
    devices = wide * group
    share = filters.shape[1]
    lanes = vectors.shape[2]
    columns = expand.shape[1]
    packed = jnp.concatenate(
        [
            filters.astype(jnp.bfloat16).reshape(4 * share, filters.shape[2]),
            pad_row(vectors.astype(jnp.bfloat16).reshape(1, -1), filters.shape[2]),
            pad_row(offsets.astype(jnp.bfloat16).reshape(1, -1), filters.shape[2]),
            jnp.zeros((14, filters.shape[2]), jnp.bfloat16),
        ]
    )
    spread = lax.all_gather(packed, ALL, axis=0)
    whole_filters = [
        spread[:, k * share : (k + 1) * share].reshape(devices * share, -1) for k in range(4)
    ]
    vec_full = (
        spread[:, 4 * share, : 30 * lanes]
        .reshape(devices, 2, 15, lanes)
        .transpose(1, 2, 0, 3)
        .reshape(2, 15, devices * lanes)
        .astype(jnp.float32)
    )
    full_offsets = (
        spread[:wide, 4 * share + 1, : 2 * columns]
        .reshape(wide, 2, columns)
        .transpose(1, 0, 2)
        .reshape(2, wide * columns)
        .astype(jnp.float32)
    )
    images = patches.shape[0]
    width = patches.shape[2]
    samples = counts.shape[0]
    image_index = jnp.arange(images, dtype=jnp.int32)
    owner = image_index // SLOTS
    slot = image_index % SLOTS
    matches = owner[:, None] == jnp.arange(samples, dtype=jnp.int32)[None, :]
    chosen = jnp.sum(jnp.where(matches, counts[None, :], 0), axis=1)
    live = (slot < chosen).astype(jnp.float32)
    rows = patches.reshape(images * GRID * GRID, width)
    pooled, first_saved = block_forward(
        rows, whole_filters[0], whole_filters[1], vec_full[0], GRID
    )
    tokens, second_saved = block_forward(
        pooled, whole_filters[2], whole_filters[3], vec_full[1], POOL, live
    )
    d_cols = cotangent.reshape(-1, columns)
    part = d_cols.shape[0] // wide
    readers = jnp.concatenate([expand.astype(jnp.bfloat16), project.astype(jnp.bfloat16)])
    readers = lax.all_gather(readers, WIDE, axis=1, tiled=True)
    d_full = lax.all_to_all(d_cols, WIDE, split_axis=0, concat_axis=1, tiled=True)
    g_out = jnp.sum(d_cols.astype(jnp.float32), axis=0)
    tokens_after, readers, d_late = lax.optimization_barrier((tokens, readers, d_cols))
    d_line = d_late.reshape(LINE, inner, part, columns).transpose(1, 0, 2, 3)
    d_line = lax.all_to_all(d_line, "spot", split_axis=0, concat_axis=0, tiled=True)
    d_line = d_line.reshape(inner, LINE * part, columns)
    full_expand = readers[:width]
    tokens_line = lax.all_gather(tokens_after, "line", axis=0, tiled=True)
    hidden_line = hidden_forward(tokens_line, readers, full_offsets[0])
    core = lax.axis_index("spot") % 2
    d_cores = d_line.reshape(inner // 2, 2, LINE * part, columns)

    def project_part(at):
        return lax.dot_general(
            held(pick(d_cores, at, 1)),
            hidden_line,
            (((1,), (0,)), ((), ())),
            preferred_element_type=jnp.float32,
        )

    d_pre = pre_backward(d_full, tokens, readers, full_offsets[0])
    theirs_sent = project_part(1 - core).astype(jnp.bfloat16)
    theirs = lax.ppermute(theirs_sent, "spot", [(i, i ^ 1) for i in range(inner)])
    g_project = project_part(core) + theirs.astype(jnp.float32)
    spot = lax.axis_index("spot") // 2
    step = 1
    while g_project.shape[0] > 1:
        halves = g_project.reshape(g_project.shape[0] // 2, 2, columns, -1)
        theirs_sent = pick(halves, 1 - spot % 2, 1).astype(jnp.bfloat16)
        step *= 2
        theirs = lax.ppermute(theirs_sent, "spot", [(i, i ^ step) for i in range(inner)])
        g_project = pick(halves, spot % 2, 1) + theirs.astype(jnp.float32)
        spot = spot // 2
    g_project = over_groups(g_project[0].astype(jnp.bfloat16), group)
    ones = jnp.ones((tokens.shape[0], 1), jnp.bfloat16)
    tokens_more = jnp.concatenate(
        [tokens, ones, jnp.zeros((tokens.shape[0], 15), jnp.bfloat16)], axis=1
    )
    g_expand_full = contract_rows(tokens_more, d_pre).astype(jnp.bfloat16)
    d_tokens = contract_cols(d_pre, full_expand)
    g_expand = lax.psum_scatter(g_expand_full, WIDE, scatter_dimension=1, tiled=True)
    g_expand = jnp.concatenate(
        [g_expand[: width + 1], g_out[None].astype(jnp.bfloat16), g_expand[width + 2 :]]
    )
    g_expand = over_groups(g_expand, group)
    g_offsets = g_expand[width : width + 2]
    g_expand = g_expand[:width]
    d_pooled, g_in_two, g_out_two, g_vec_two = block_backward(
        d_tokens, second_saved, whole_filters[2], whole_filters[3], vec_full[1], POOL, live
    )
    d_pooled, theirs_sent = lax.optimization_barrier((d_pooled, theirs_sent))
    d_rows, g_in_one, g_out_one, g_vec_one = block_backward(
        d_pooled, first_saved, whole_filters[0], whole_filters[1], vec_full[0], GRID
    )
    hidden_line, d_rows = lax.optimization_barrier((hidden_line, d_rows))
    at = lax.axis_index("line") * inner * columns
    project_line = lax.dynamic_slice(
        readers, (width, at), (readers.shape[0] - width, inner * columns)
    )
    offset_line = lax.dynamic_slice_in_dim(full_offsets[1], at, inner * columns, 0)
    out_line = (
        jnp.dot(hidden_line, project_line, preferred_element_type=jnp.float32) + offset_line
    ).astype(jnp.bfloat16)
    out_line = out_line.reshape(LINE * part, inner, columns).transpose(1, 0, 2)
    out_cols = lax.all_to_all(out_line, "spot", split_axis=0, concat_axis=0, tiled=True)
    readout = (
        out_cols.reshape(inner, LINE, part, columns)
        .transpose(1, 0, 2, 3)
        .reshape(-1, POOL * POOL, columns)
    )
    patch_gradient = d_rows.reshape(images, GRID * GRID, width)
    g_two = reduce_block(g_in_two, g_out_two, g_vec_two, devices)
    g_two = spread_reduce(g_two)
    g_one = reduce_block(g_in_one, g_out_one, g_vec_one, devices)
    g_one = spread_reduce(g_one)
    g_filters = jnp.stack(
        [g_one[:share], g_one[share : 2 * share], g_two[:share], g_two[share : 2 * share]]
    ).astype(jnp.float32)
    g_vectors = jnp.stack(
        [g_one[2 * share, : 15 * lanes], g_two[2 * share, : 15 * lanes]]
    ).reshape(2, 15, lanes).astype(jnp.float32)
    filters_out = adamw(
        filters, g_filters, filters_moment, filters_square, filters_average, 0.03, 0.05
    )
    vectors_out = adamw(
        vectors, g_vectors, vectors_moment, vectors_square, vectors_average, 0.3, 0.0
    )
    expand_out = adamw(expand, g_expand, expand_moment, expand_square, expand_average, 0.03, 0.05)
    project_out = adamw_turned(
        project, g_project, project_moment, project_square, project_average, 0.016, 0.05
    )
    offsets_out = adamw(
        offsets, g_offsets, offsets_moment, offsets_square, offsets_average, 0.1, 0.0
    )
    return (
        readout,
        patch_gradient,
        filters_out[0],
        filters_out[1],
        filters_out[2],
        filters_out[3],
        filters_out[4],
        vectors_out[0],
        vectors_out[1],
        vectors_out[2],
        vectors_out[3],
        vectors_out[4],
        expand_out[0],
        expand_out[1],
        expand_out[2],
        expand_out[3],
        expand_out[4],
        project_out[0],
        project_out[1],
        project_out[2],
        project_out[3],
        project_out[4],
        offsets_out[0],
        offsets_out[1],
        offsets_out[2],
        offsets_out[3],
        offsets_out[4],
    )


def solution(mesh):
    in_specs = (
        P(ALL, None, None),
        P(ALL),
        P("dp", None, WIDE),
        P(None, ALL, None),
        P(None, ALL, None),
        P(None, ALL, None),
        P(None, ALL, None),
        P(None, None, ALL),
        P(None, None, ALL),
        P(None, None, ALL),
        P(None, None, ALL),
        P(None, WIDE),
        P(None, WIDE),
        P(None, WIDE),
        P(None, WIDE),
        P(None, WIDE),
        P(None, WIDE),
        P(None, WIDE),
        P(None, WIDE),
        P(None, WIDE),
        P(None, WIDE),
        P(None, WIDE),
        P(None, WIDE),
    )
    out_specs = (
        P("dp", None, WIDE),
        P(ALL, None, None),
        P(None, ALL, None),
        P(None, ALL, None),
        P(None, ALL, None),
        P(None, ALL, None),
        P(None, ALL, None),
        P(None, None, ALL),
        P(None, None, ALL),
        P(None, None, ALL),
        P(None, None, ALL),
        P(None, None, ALL),
        P(None, WIDE),
        P(None, WIDE),
        P(None, WIDE),
        P(None, WIDE),
        P(None, WIDE),
        P(None, WIDE),
        P(None, WIDE),
        P(None, WIDE),
        P(None, WIDE),
        P(None, WIDE),
        P(None, WIDE),
        P(None, WIDE),
        P(None, WIDE),
        P(None, WIDE),
        P(None, WIDE),
    )
    devices = mesh.devices
    lines = Mesh(
        devices.reshape(devices.shape[0], LINE, devices.shape[1] // LINE), ("dp", "line", "spot")
    )
    return jax.shard_map(shards, mesh=lines, in_specs=in_specs, out_specs=out_specs, check_vma=False)
```

time: 1620 us -> 908 us (0.56)
  other arithmetic: 344 us -> 50.5 us
  Pallas kernels: 0 us -> 267 us
  waiting for transfers between devices: 578 us -> 364 us
  blocking collectives: 197 us -> 0 us
  local copies, waits for them, and re-layouts: 228 us -> 64.4 us
  matrix products: 232 us -> 107 us
  starting transfers between devices: 12.3 us -> 29.8 us
    unnamed x12 -> x4, waiting for transfers between devices: 464 us -> 0.07 us
    pallas_call x0 -> x7, Pallas kernels: none -> 267 us  [the longest x2 89.8 us: block_backward(): pl.pallas_call(partial(backward_kernel, side), grid=(total // size,), in_...]
    all_gather x3, waiting for transfers between devices: 0.01 us -> 261 us  [the longest x1 138 us: shards(): spread = lax.all_gather(packed, ALL, axis=0)]
    reduce_sum x23 -> x3, other arithmetic: 208 us -> 4.86 us  [the longest x1 3.57 us: shards(): g_out = jnp.sum(d_cols.astype(jnp.float32), axis=0)]
    all_gather x2 -> x0, blocking collectives: 192 us -> none  [the longest x1 174 us: shards(): lax.all_gather(vectors.astype(jnp.bfloat16), ('dp', 'wide'), axis=2, tile...]
    slice x2 -> x8, local copies, waits for them, and re-layouts: 120 us -> 8.99 us  [the longest x1 6.2 us: shards(): spread[:, k * share:(k + 1) * share].reshape(devices * share, -1)]
    ppermute x0 -> x14, waiting for transfers between devices: none -> 103 us  [the longest x10 103 us: halve_blocks(): theirs = lax.ppermute(pick(blocks, 1 - mine, axis), ALL, pairs)]
    dot_general x6 -> x1, matrix products: 99.6 us -> 9.98 us  [contract_cols(): lax.dot_general(left, right, (((1,), (1,)), ((), ())), preferred_element_...]
  transfers between devices with their start and end apart: 11 -> 21, of which waited for: 5 -> 8; matrix products, arithmetic and copies ran while one was open for 44% -> 21% of each run, Pallas kernels for 0% -> 25%
where the time goes in v1:
time: 908 us; the launch traced here: 899 us
  waiting for transfers between devices  364 us (40%)
  Pallas kernels  267 us (29%)
  matrix products  107 us (12%)
  local copies, waits for them, and re-layouts  64.4 us (7%)
  other arithmetic  50.5 us (6%)
  starting transfers between devices  29.8 us (3%)
  between operations  15.7 us (2%)
    all_gather x1, waiting for transfers between devices, shards(): spread = lax.all_gather(packed, ALL, axis=0)  138 us
    all_gather x1, waiting for transfers between devices, shards(): readers = lax.all_gather(readers, WIDE, axis=1, tiled=True)  123 us
    ppermute x10, waiting for transfers between devices, halve_blocks(): theirs = lax.ppermute(pick(blocks, 1 - mine, axis), ALL, pairs)  103 us
    pallas_call x2, Pallas kernels, block_backward(): pl.pallas_call(partial(backward_kernel, side), grid=(total // size,), in_...  89.8 us
    pallas_call x2, Pallas kernels, block_forward(): pl.pallas_call(partial(forward_kernel, side), grid=(total // size,), in_s...  83.9 us
    pallas_call x1, Pallas kernels, hidden_forward(): pl.pallas_call(hidden_kernel, grid=(depth // step, LINE), in_specs=[pl.Bl...  42.5 us
    dot_general x5, matrix products, contract_rows(): lax.dot_general(left, right, (((0,), (0,)), ((), ())), preferred_element_...  37.2 us
    pallas_call x1, Pallas kernels, pre_backward(): pl.pallas_call(pre_kernel, grid=(depth // step,), in_specs=[pl.BlockSpec(...  34.8 us
  transfers between devices with their start and end apart: 21, of which 8 were waited for; matrix products, arithmetic and copies ran while one was open for 21% of the time, Pallas kernels for 25%

profile of v1, /device:TPU:0, one launch (start us, length us, event | category | flops | bytes accessed | tf_op | source)
XLA Modules:
  0.0 898.8 jit_solution(10436978554483396414)
XLA Ops:
  12.1 2.4 convert_element_type.305
  16.2 7.4 all-to-all-start
  25.7 137.9 %all-gather.9.cloned.1.call-done = bf16[4608,1024]{1,0:T(8,128)(2,1)} async-done(((bf16[144,1024]{1,0:T(8,128)(2,1)}), bf16[4608,1024]{1,0:T(8,128)(2,1)}) %all-gather.9.cloned.1.call-update) | async-done | bytes 9437200 | tf_op jit(solution)/shard_map/all_gather | solution.py:674
  167.0 6.2 fusion.65
  173.9 63.6 %block_forward_24.1 = (f32[2304,1024]{1,0:T(8,128)}, f32[2304,1024]{1,0:T(8,128)}, f32[2304,1024]{1,0:T(8,128)}, f32[2304,128]{1,0:T(8,128)}, f32[2304,128]{1,0:...) custom-call(bf16[2304,1024]{1,0:T(8,128)(2,1)} %bitcast.159, ...), custom_call_target="tpu_custom_call" | custom-call | tf_op jit(solution)/shard_map/block_forward_24/pallas_call | solution.py:412
  238.4 20.3 %block_forward_12.1 = (f32[576,1024]{1,0:T(8,128)}, f32[576,1024]{1,0:T(8,128)}, f32[576,1024]{1,0:T(8,128)}, f32[576,128]{1,0:T(8,128)}, f32[576,128]{1,0:T(8,1...) custom-call(f32[4]{0:T(128)} %compare_convert_fusion.refs_0_, ...), custom_call_target="tpu_custom_call" | custom-call | tf_op jit(solution)/shard_map/block_forward_12/pallas_call | solution.py:412
  258.7 122.9 %all-gather.5.cloned.1.call-done.expand_ref.project_ref = bf16[5120,4096]{1,0:T(8,128)(2,1)} async-done(((bf16[5120,256]{1,0:T(8,128)(2,1)}), bf16[5120,4096]{1,0:T(8,128)(2,1)}) %all-gather.5.cloned.1.call-update) | async-done | bytes 41943056 | tf_op jit(solution)/shard_map/all_gather | solution.py:711
  381.6 4.9 copy.120
  386.5 5.0 all-to-all-start.1
  391.6 5.5 copy.156
  399.4 34.8 %pre_backward.1 = bf16[576,4096]{1,0:T(8,128)(2,1)} custom-call(bf16[576,4096]{1,0:T(8,128)(2,1)} %bitcast.157, bf16[576,1024]{1,0:T(8,128)(2,1)} %get-tuple-element.64.tokens_ref, bf16[5120,4096]{1,0:T(8,128)(2,1)} %all-gather.5.cloned.1.call-done.expand_ref.project_ref, bf16[5120,4096]{1,0:T(8,128)(2,1)} %all-gather.5.cloned.1.call-done.expand_ref.project_ref, ...), custom_call_target="tpu_custom_call" | custom-call | tf_op jit(solution)/shard_map/pre_backward/pallas_call | solution.py:617
  434.2 10.0 %fusion.6.refs_1_ = f32[576,1024]{1,0:T(8,128)} fusion(bf16[576,4096]{1,0:T(8,128)(2,1)} %pre_backward.1, bf16[5120,4096]{1,0:T(8,128)(2,1)} %all-gather.5.cloned.1.call-done.expand_ref.project_ref), kind=kOutput, calls=%fused_computation.9 | convolution fusion | flops 4831838208 | bytes 15466496 | tf_op jit(solution)/shard_map/dot_general | solution.py:35
  444.2 22.1 %block_backward_12.1 = (f32[576,1024]{1,0:T(8,128)}, bf16[576,1024]{1,0:T(8,128)(2,1)}, bf16[576,1024]{1,0:T(8,128)(2,1)}, f32[128,1024]{1,0:T(8,128)}) custom-call(f32[4]{0:T(128)} %compare_convert_fusion.refs_0_, f32[576,1024]{1,0:T(8,128)} %fusion.6.refs_1_, bf16[576,1024]{1,0:T(8,128)(2,1)} %get-tuple-element.62.refs_1_.refs_2_, ...), custom_call_target="tpu_custom_call" | custom-call | tf_op jit(solution)/shard_map/block_backward_12/pallas_call | solution.py:448
  466.3 4.4 convolution_convert_fusion.4
  470.7 4.1 dynamic-slice_bitcast_fusion
  474.8 42.5 %hidden_forward.1 = bf16[2304,4096]{1,0:T(8,128)(2,1)} custom-call(bf16[2304,1024]{1,0:T(8,128)(2,1)} %all-gather.7.cloned.1.call-done.tokens_ref, bf16[5120,4096]{1,0:T(8,128)(2,1)} %all-gather.5.cloned.1.call-done.expand_ref.project_ref, f32[1,4096]{1,0:T(1,128)} %bitcast.186), custom_call_target="tpu_custom_call" | custom-call | tf_op jit(solution)/shard_map/hidden_forward/pallas_call | solution.py:568
  517.3 15.8 %fusion.8 = bf16[2,256,4096]{2,1,0:T(8,128)(2,1)} fusion(bf16[2,2304,256]{2,1,0:T(8,128)(2,1)S(1)} %get-tuple-element.202, bf16[2304,4096]{1,0:T(8,128)(2,1)} %hidden_forward.1), kind=kOutput, calls=%fused_computation.11 | convolution fusion | flops 9665773568 | bytes 25427968 | tf_op jit(solution)/shard_map/dot_general | solution.py:725
  534.1 3.3 convolution_convert_fusion.3
  538.1 2.4 constant_dynamic-slice_fusion.1
  543.9 11.9 %convolution_convert_fusion = bf16[1040,4096]{1,0:T(8,128)(2,1)} fusion(bf16[576,1040]{1,0:T(8,128)(2,1)S(1)} %concatenate.50, bf16[576,4096]{1,0:T(8,128)(2,1)} %pre_backward.1), kind=kOutput, calls=%fused_computation.4 | convolution fusion | flops 4911595520 | bytes 14436352 | tf_op jit(solution)/shard_map/dot_general | solution.py:29
  555.8 4.0 fusion.13
  561.0 1.9 collective-permute-start.7
  562.9 16.0 %convert_add_fusion = f32[2,256,4096]{2,1,0:T(8,128)S(1)} fusion(bf16[2,256,4096]{2,1,0:T(8,128)(2,1)} %collective-permute-done, bf16[2,2304,256]{2,1,0:T(8,128)(2,1)S(1)} %copy-done.6, bf16[2304,4096]{1,0:T(8,128)(2,1)} %hidden_forward.1), kind=kOutput, calls=%fused_computation.8 | convolution fusion | flops 9667870720 | bytes 33816576 | tf_op jit(solution)/shard_map/dot_general | solution.py:725
  579.0 3.2 copy-done.3
  583.8 67.7 %block_backward_24.1 = (bf16[2304,1024]{1,0:T(8,128)(2,1)}, bf16[2304,1024]{1,0:T(8,128)(2,1)}, bf16[2304,1024]{1,0:T(8,128)(2,1)}, f32[128,1024]{1,0:T(8,128)}) custom-call(bf16[576,144]{1,0:T(8,128)(2,1)} %select_convert_fusion.refs_0_, f32[576,1024]{1,0:T(8,128)} %get-tuple-element.74.refs_1_, bf16[2304,1024]{1,0:T(8,128)(2,1)} %bitcast.160, ...), custom_call_target="tpu_custom_call" | custom-call | tf_op jit(solution)/shard_map/block_backward_24/pallas_call | solution.py:448
  653.1 8.8 convolution_convert_fusion.2
  662.0 8.7 convolution_convert_fusion.1
  670.7 1.9 pad_maximum_fusion
  672.6 2.4 constant_dynamic-slice_fusion.3
  676.9 1.8 fusion.15
  681.5 15.6 %collective-permute-done.8 = bf16[2,2,80,1024]{3,2,1,0:T(8,128)(2,1)S(1)} collective-permute-done((bf16[2,2,80,1024]{3,2,1,0:T(8,128)(2,1)S(1)}, bf16[2,2,80,1024]{3,2,1,0:T(8,128)(2,1)S(1)}, u32[]{:S(2)}, u32[]{:S(2)}) %collective-permute-start.8) | collective-permute-done | bytes 655392 | tf_op jit(solution)/shard_map/ppermute | solution.py:536
  699.7 16.1 %collective-permute-done.9 = bf16[2,80,1024]{2,1,0:T(8,128)(2,1)S(1)} collective-permute-done((bf16[2,80,1024]{2,1,0:T(8,128)(2,1)S(1)}, bf16[2,80,1024]{2,1,0:T(8,128)(2,1)S(1)}, u32[]{:S(2)}, u32[]{:S(2)}) %collective-permute-start.9) | collective-permute-done | bytes 327712 | tf_op jit(solution)/shard_map/ppermute | solution.py:536
  716.0 3.6 reduce_sum.36
  722.0 4.0 fusion.14
  728.6 27.8 %add_convert_fusion = bf16[2304,1024]{0,1:T(8,128)(2,1)} fusion(bf16[2304,4096]{1,0:T(8,128)(2,1)} %hidden_forward.1, bf16[5120,4096]{1,0:T(8,128)(2,1)} %all-gather.5.cloned.1.call-done.expand_ref.project_ref, s32[]{:T(128)S(6)} %select_n.317, f32[1024]{0:T(1024)S(1)} %bitcast.191), kind=kOutput, calls=%fused_computation.5 | convolution fusion | flops 19332071424 | bytes 31985668 | tf_op jit(solution)/shard_map/dot_general | solution.py:773
  756.4 6.6 copy.123
  763.0 5.3 all-to-all-start.2
  769.1 1.9 slice.121
  771.0 2.9 concatenate.51
  775.5 4.7 fusion.17
  780.6 17.8 %collective-permute-done.2 = bf16[2,2,2,80,1024]{4,3,2,1,0:T(8,128)(2,1)} collective-permute-done((bf16[2,2,2,80,1024]{4,3,2,1,0:T(8,128)(2,1)}, bf16[2,2,2,80,1024]{4,3,2,1,0:T(8,128)(2,1)}, u32[]{:S(2)}, u32[]{:S(2)}) %collective-permute-start.2) | collective-permute-done | bytes 1310752 | tf_op jit(solution)/shard_map/ppermute | solution.py:536
  798.4 1.8 fusion.16
  802.9 2.1 fusion.59
  804.9 42.4 %collective-permute-done.3 = bf16[2,2,80,1024]{3,2,1,0:T(8,128)(2,1)S(1)} collective-permute-done((bf16[2,2,80,1024]{3,2,1,0:T(8,128)(2,1)S(1)}, bf16[2,2,80,1024]{3,2,1,0:T(8,128)(2,1)S(1)}, u32[]{:S(2)}, u32[]{:S(2)}) %collective-permute-start.3) | collective-permute-done | bytes 655392 | tf_op jit(solution)/shard_map/ppermute | solution.py:536
  849.9 4.9 copy.124
  854.8 9.8 %collective-permute-done.4 = bf16[2,80,1024]{2,1,0:T(8,128)(2,1)S(1)} collective-permute-done((bf16[2,80,1024]{2,1,0:T(8,128)(2,1)S(1)}, bf16[2,80,1024]{2,1,0:T(8,128)(2,1)S(1)}, u32[]{:S(2)}, u32[]{:S(2)}) %collective-permute-start.4) | collective-permute-done | bytes 327712 | tf_op jit(solution)/shard_map/ppermute | solution.py:536
  864.9 4.9 convert_add_fusion.3.grad_ref
  869.9 16.3 %adamw_turned.1 = (f32[4096,256]{1,0:T(8,128)}, f32[4096,256]{1,0:T(8,128)}, f32[4096,256]{1,0:T(8,128)}, f32[4096,256]{1,0:T(8,128)}, bf16[4096,256]{1,0:T(8,128)(2,1)}) custom-call(f32[256,4096]{1,0:T(8,128)} %convert_add_fusion.3.grad_ref, f32[4096,256]{1,0:T(8,128)} %refs_0_.1, f32[4096,256]{1,0:T(8,128)} %refs_1_.1, f32[4096,256]{1,0:T(8,128)} %refs_2_.1, ...), custom_call_target="tpu_custom_call" | custom-call | tf_op jit(solution)/shard_map/adamw_turned/pallas_call | solution.py:594
  (185 shorter events, 50.6 us)
Async XLA Ops:
  7.2 156.4 %all-gather.9.cloned.1.call-start = ((), (), s32[]{:S(2)}) async-start(), calls=%async_computation.7 | async-start | bytes 9732096 | tf_op jit(solution)/shard_map/all_gather | solution.py:674
  10.8 370.8 %all-gather.5.cloned.1.call-start = ((), (), s32[]{:S(2)}) async-start(), calls=%async_computation.4 | async-start | bytes 44564480 | tf_op jit(solution)/shard_map/all_gather | solution.py:711
  16.2 370.3 %all-to-all-start = ((bf16[16,576,256]{2,1,0:T(8,128)(2,1)}), bf16[16,576,256]{2,1,0:T(8,128)(2,1)}, u32[]{:S(2)}, u32[]{:S(2)}) async-start(bf16[16,576,256]{2,1,0:T(8,128)(2,1)} %bitcast.155), calls=%async_computation | async-start | bytes 9437184 | tf_op jit(solution)/shard_map/all_to_all | solution.py:712
  23.6 451.2 %all-gather.7.cloned.1.call-start = ((), (), s32[]{:S(2)}) async-start(), calls=%async_computation.5 | async-start | bytes 5898240 | tf_op jit(solution)/shard_map/all_gather | solution.py:719
  386.5 84.2 %all-to-all-start.1 = ((bf16[4,4,576,256]{3,2,1,0:T(8,128)(2,1)}), bf16[4,4,576,256]{3,2,1,0:T(8,128)(2,1)}, u32[]{:S(2)}, u32[]{:S(2)}) async-start(bf16[4,4,576,256]{3,2,1,0:T(8,128)(2,1)} %copy.120), calls=%async_computation.1 | async-start | bytes 9437184 | tf_op jit(solution)/shard_map/all_to_all | solution.py:716
  391.5 376.8 %reduce-scatter.2.cloned.1.call-start = ((), (), s32[]{:S(2)}) async-start(), calls=%async_computation.6 | async-start | bytes 9052160 | tf_op jit(solution)/shard_map/reduce_scatter | solution.py:752
  444.2 22.1 %copy-start.2 = (bf16[576,1024]{1,0:T(8,128)(2,1)S(1)}, bf16[576,1024]{1,0:T(8,128)(2,1)}, u32[]{:S(2)}) copy-start(bf16[576,1024]{1,0:T(8,128)(2,1)} %get-tuple-element.62.refs_1_.refs_2_) | copy-start | bytes 3538948
  517.3 16.2 %copy-start.16 = (f32[128,1024]{1,0:T(8,128)S(1)}, f32[128,1024]{1,0:T(8,128)}, u32[]{:S(2)}) copy-start(f32[128,1024]{1,0:T(8,128)} %get-tuple-element.91) | copy-start | bytes 1572868
  517.3 16.8 %copy-start.27 = (bf16[576,1024]{1,0:T(8,128)(2,1)S(1)}, bf16[576,1024]{1,0:T(8,128)(2,1)}, u32[]{:S(2)}) copy-start(bf16[576,1024]{1,0:T(8,128)(2,1)} %get-tuple-element.89) | copy-start | bytes 3538948
  533.1 29.9 %collective-permute-start = (bf16[2,256,4096]{2,1,0:T(8,128)(2,1)}, bf16[2,256,4096]{2,1,0:T(8,128)(2,1)}, u32[]{:S(2)}, u32[]{:S(2)}) collective-permute-start(bf16[2,256,4096]{2,1,0:T(8,128)(2,1)} %fusion.8), channel_id=1, source_target_pairs={{0,1},{1,0},{2,3},{3,2},{4,5},{5,4},{6,7},{7,6},{8,9},{9,8},{10,11... | collective-permute-start | bytes 12582920 | tf_op jit(solution)/shard_map/ppermute | solution.py:734
  534.1 3.3 copy-start.7
  540.5 2.8 copy-start
  542.3 13.5 %collective-permute-start.6 = (bf16[2,2,2,2,80,1024]{5,4,2,1,0,3:T(8,128)(2,1)}, bf16[2,2,2,2,80,1024]{5,4,2,1,0,3:T(8,128)(2,1)}, u32[]{:S(2)}, u32[]{:S(2)}) collective-permute-start(bf16[2,2,2,2,80,1024]{5,4,2,1,0,3:T(8,128)(2,1)} %bitcast.150), channel_id=1, source_target_pairs={{0,1},{1,0},{2,3},{3,2},{4,5},{5,4},{6,7},{7,6},{8,9},{9,8},{10,11... | collective-permute-start | bytes 7864328 | tf_op jit(solution)/shard_map/ppermute | solution.py:536
  559.8 3.1 copy-start.6
  561.0 115.9 %collective-permute-start.7 = (bf16[2,2,2,80,1024]{4,3,2,1,0:T(8,128)(2,1)}, bf16[2,2,2,80,1024]{4,3,2,1,0:T(8,128)(2,1)}, u32[]{:S(2)}, u32[]{:S(2)}) collective-permute-start(bf16[2,2,2,80,1024]{4,3,2,1,0:T(8,128)(2,1)} %dynamic-slice_bitcast_fusion.2), channel_id=1, source_target_pairs={{0,2},{1,3},{2,0},{3,1},{4,6},{5,7},{6,4},{7,5},{8,10},{9,11},{10,... | collective-permute-start | bytes 3932168 | tf_op jit(solution)/shard_map/ppermute | solution.py:536
  579.0 3.2 copy-start.3
  653.0 9.0 %slice-start = ((s8[4718592]{0:T(1024)(128)(4,1)}), s8[4194304]{0:T(1024)(128)(4,1)S(1)}, s32[]{:S(2)}) async-start(s8[4718592]{0:T(1024)(128)(4,1)} %bitcast.193), calls=%async_computation.8 | async-start | bytes 8388608
  653.1 8.9 slice-start.1
  676.9 45.1 %collective-permute-start.1 = (bf16[2,2,2,2,80,1024]{5,4,2,1,0,3:T(8,128)(2,1)}, bf16[2,2,2,2,80,1024]{5,4,2,1,0,3:T(8,128)(2,1)}, u32[]{:S(2)}, u32[]{:S(2)}) collective-permute-start(bf16[2,2,2,2,80,1024]{5,4,2,1,0,3:T(8,128)(2,1)} %bitcast.151), channel_id=1, source_target_pairs={{0,1},{1,0},{2,3},{3,2},{4,5},{5,4},{6,7},{7,6},{8,9},{9,8},{10,11... | collective-permute-start | bytes 7864328 | tf_op jit(solution)/shard_map/ppermute | solution.py:536
  679.8 17.2 %collective-permute-start.8 = (bf16[2,2,80,1024]{3,2,1,0:T(8,128)(2,1)S(1)}, bf16[2,2,80,1024]{3,2,1,0:T(8,128)(2,1)S(1)}, u32[]{:S(2)}, u32[]{:S(2)}) collective-permute-start(bf16[2,2,80,1024]{3,2,1,0:T(8,128)(2,1)S(1)} %dynamic-slice_bitcast_fusion.4), channel_id=1, source_target_pairs={{0,16},{1,17},{2,18},{3,19},{4,20},{5,21},{6,22},{7,23},{8,24},{9,... | collective-permute-start | bytes 1966088 | tf_op jit(solution)/shard_map/ppermute | solution.py:536
  698.4 17.3 %collective-permute-start.9 = (bf16[2,80,1024]{2,1,0:T(8,128)(2,1)S(1)}, bf16[2,80,1024]{2,1,0:T(8,128)(2,1)S(1)}, u32[]{:S(2)}, u32[]{:S(2)}) collective-permute-start(bf16[2,80,1024]{2,1,0:T(8,128)(2,1)S(1)} %dynamic-slice_bitcast_fusion.6), channel_id=1, source_target_pairs={{0,8},{1,9},{2,10},{3,11},{4,12},{5,13},{6,14},{7,15},{8,0},{9,1},... | collective-permute-start | bytes 983048 | tf_op jit(solution)/shard_map/ppermute | solution.py:536
  715.8 3.7 copy-start.17
  715.9 5.4 collective-permute-start.10
  721.4 54.2 %collective-permute-start.12 = (bf16[1,256,4096]{2,1,0:T(8,128)(2,1)}, bf16[1,256,4096]{2,1,0:T(8,128)(2,1)}, u32[]{:S(2)}, u32[]{:S(2)}) collective-permute-start(bf16[1,256,4096]{2,1,0:T(8,128)(2,1)} %dynamic-slice_convert_fusion), channel_id=1, source_target_pairs={{0,2},{1,3},{2,0},{3,1},{4,6},{5,7},{6,4},{7,5},{8,10},{9,11},{10,... | collective-permute-start | bytes 6291464 | tf_op jit(solution)/shard_map/ppermute | solution.py:742
  727.2 71.2 %collective-permute-start.2 = (bf16[2,2,2,80,1024]{4,3,2,1,0:T(8,128)(2,1)}, bf16[2,2,2,80,1024]{4,3,2,1,0:T(8,128)(2,1)}, u32[]{:S(2)}, u32[]{:S(2)}) collective-permute-start(bf16[2,2,2,80,1024]{4,3,2,1,0:T(8,128)(2,1)} %dynamic-slice_bitcast_fusion.3), channel_id=1, source_target_pairs={{0,2},{1,3},{2,0},{3,1},{4,6},{5,7},{6,4},{7,5},{8,10},{9,11},{10,... | collective-permute-start | bytes 3932168 | tf_op jit(solution)/shard_map/ppermute | solution.py:536
  763.0 86.9 %all-to-all-start.2 = ((bf16[4,2304,256]{2,1,0:T(8,128)(2,1)}), bf16[4,2304,256]{2,1,0:T(8,128)(2,1)}, u32[]{:S(2)}, u32[]{:S(2)}) async-start(bf16[4,2304,256]{2,1,0:T(8,128)(2,1)} %bitcast.158), calls=%async_computation.2 | async-start | bytes 9437184 | tf_op jit(solution)/shard_map/all_to_all | solution.py:776
  773.8 28.2 %collective-permute-start.11 = (bf16[1040,256]{1,0:T(8,128)(2,1)S(1)}, bf16[1040,256]{1,0:T(8,128)(2,1)S(1)}, u32[]{:S(2)}, u32[]{:S(2)}) collective-permute-start(bf16[1040,256]{1,0:T(8,128)(2,1)S(1)} %concatenate.51), channel_id=1, source_target_pairs={{0,16},{16,0},{1,17},{17,1},{2,18},{18,2},{3,19},{19,3},{4,20},{20... | collective-permute-start | bytes 1597448 | tf_op jit(solution)/shard_map/ppermute | solution.py:499
  780.2 84.6 %collective-permute-start.13 = (bf16[256,4096]{1,0:T(8,128)(2,1)}, bf16[256,4096]{1,0:T(8,128)(2,1)}, u32[]{:S(2)}, u32[]{:S(2)}) collective-permute-start(bf16[256,4096]{1,0:T(8,128)(2,1)} %fusion.17), channel_id=1, source_target_pairs={{0,16},{16,0},{1,17},{17,1},{2,18},{18,2},{3,19},{19,3},{4,20},{20... | collective-permute-start | bytes 6291464 | tf_op jit(solution)/shard_map/ppermute | solution.py:499
  800.2 2.0 copy-start.23
  800.3 2.0 copy-start.24
  800.3 2.6 copy-start.5
  800.3 2.6 copy-start.10
  800.3 2.5 copy-start.11
  800.4 47.0 %collective-permute-start.3 = (bf16[2,2,80,1024]{3,2,1,0:T(8,128)(2,1)S(1)}, bf16[2,2,80,1024]{3,2,1,0:T(8,128)(2,1)S(1)}, u32[]{:S(2)}, u32[]{:S(2)}) collective-permute-start(bf16[2,2,80,1024]{3,2,1,0:T(8,128)(2,1)S(1)} %dynamic-slice_bitcast_fusion.5), channel_id=1, source_target_pairs={{0,16},{1,17},{2,18},{3,19},{4,20},{5,21},{6,22},{7,23},{8,24},{9,... | collective-permute-start | bytes 1966088 | tf_op jit(solution)/shard_map/ppermute | solution.py:536
  802.8 45.4 %copy-start.22 = (f32[2,256]{1,0:T(2,128)}, f32[2,256]{1,0:T(2,128)S(1)}, u32[]{:S(2)}) copy-start(f32[2,256]{1,0:T(2,128)S(1)} %get-tuple-element.179) | copy-start | bytes 6148
  804.9 45.0 %copy-start.4 = (f32[1024,256]{1,0:T(8,128)}, f32[1024,256]{1,0:T(8,128)S(1)}, u32[]{:S(2)}) copy-start(f32[1024,256]{1,0:T(8,128)S(1)} %get-tuple-element.183) | copy-start | bytes 3145732
  804.9 43.3 %copy-start.26 = (f32[2,256]{1,0:T(2,128)S(1)}, f32[2,256]{1,0:T(2,128)}, u32[]{:S(2)}) copy-start(f32[2,256]{1,0:T(2,128)} %param.45) | copy-start | bytes 6148
  804.9 43.9 %copy-start.12 = (f32[1024,256]{1,0:T(8,128)S(1)}, f32[1024,256]{1,0:T(8,128)}, u32[]{:S(2)}) copy-start(f32[1024,256]{1,0:T(8,128)} %param.37) | copy-start | bytes 3145732
  847.6 17.0 %collective-permute-start.4 = (bf16[2,80,1024]{2,1,0:T(8,128)(2,1)S(1)}, bf16[2,80,1024]{2,1,0:T(8,128)(2,1)S(1)}, u32[]{:S(2)}, u32[]{:S(2)}) collective-permute-start(bf16[2,80,1024]{2,1,0:T(8,128)(2,1)S(1)} %dynamic-slice_bitcast_fusion.7), channel_id=1, source_target_pairs={{0,8},{1,9},{2,10},{3,11},{4,12},{5,13},{6,14},{7,15},{8,0},{9,1},... | collective-permute-start | bytes 983048 | tf_op jit(solution)/shard_map/ppermute | solution.py:536
  864.8 21.4 %collective-permute-start.5 = (bf16[80,1024]{1,0:T(8,128)(2,1)S(1)}, bf16[80,1024]{1,0:T(8,128)(2,1)S(1)}, u32[]{:S(2)}, u32[]{:S(2)}) collective-permute-start(bf16[80,1024]{1,0:T(8,128)(2,1)S(1)} %dynamic-slice_bitcast_fusion.9), channel_id=1, source_target_pairs={{0,4},{1,5},{2,6},{3,7},{4,0},{5,1},{6,2},{7,3},{8,12},{9,13},{10,... | collective-permute-start | bytes 491528 | tf_op jit(solution)/shard_map/ppermute | solution.py:536
  869.8 16.6 %copy-start.18 = (f32[2,15,32]{2,0,1:T(2,128)S(1)}, f32[2,15,32]{2,0,1:T(2,128)}, u32[]{:S(2)}) copy-start(f32[2,15,32]{2,0,1:T(2,128)} %param.30) | copy-start | bytes 11524
  869.8 16.6 %copy-start.20 = (f32[2,15,32]{2,0,1:T(2,128)S(1)}, f32[2,15,32]{2,0,1:T(2,128)}, u32[]{:S(2)}) copy-start(f32[2,15,32]{2,0,1:T(2,128)} %param.31) | copy-start | bytes 11524
  869.8 16.6 %copy-start.21 = (f32[2,15,32]{2,0,1:T(2,128)S(1)}, f32[2,15,32]{2,0,1:T(2,128)}, u32[]{:S(2)}) copy-start(f32[2,15,32]{2,0,1:T(2,128)} %param.32) | copy-start | bytes 11524
  869.8 19.0 %copy-start.19 = (f32[2,15,32]{2,0,1:T(2,128)S(1)}, f32[2,15,32]{2,0,1:T(2,128)}, u32[]{:S(2)}) copy-start(f32[2,15,32]{2,0,1:T(2,128)} %param.33) | copy-start | bytes 11524
  869.8 19.7 %copy-start.9 = (f32[4,32,1024]{2,1,0:T(8,128)S(1)}, f32[4,32,1024]{2,1,0:T(8,128)}, u32[]{:S(2)}) copy-start(f32[4,32,1024]{2,1,0:T(8,128)} %param.26) | copy-start | bytes 1572868
  869.8 19.6 %copy-start.13 = (f32[4,32,1024]{2,1,0:T(8,128)S(1)}, f32[4,32,1024]{2,1,0:T(8,128)}, u32[]{:S(2)}) copy-start(f32[4,32,1024]{2,1,0:T(8,128)} %param.27) | copy-start | bytes 1572868
  869.8 19.6 %copy-start.14 = (f32[4,32,1024]{2,1,0:T(8,128)S(1)}, f32[4,32,1024]{2,1,0:T(8,128)}, u32[]{:S(2)}) copy-start(f32[4,32,1024]{2,1,0:T(8,128)} %param.28) | copy-start | bytes 1572868
  886.2 4.6 copy-start.15
  (3 other events, 4.0 us)
Sparse Core Ops, SparseCore 0:
  11.5 152.0 all-gather.8
  165.7 215.8 all-gather.4
  383.2 88.8 all-gather.6
  555.9 108.0 reduce-scatter.1

commit v2 on v1

--- a/solution.py
+++ b/solution.py
@@ -494,6 +494,54 @@
     return jnp.pad(row, ((0, 0), (0, width - row.shape[1])))
 
 
+def ring_order(chips):
+    inner = chips // LINE
+    cells = [(o, 0) for o in range(LINE)]
+    for turn, o in enumerate(reversed(range(LINE))):
+        line = list(range(1, inner))
+        cells += [(o, i) for i in (line if turn % 2 == 0 else line[::-1])]
+    return [o * inner + i for o, i in cells]
+
+
+def ring_gather(value, inner, group):
+    chips = LINE * inner // 2
+    ring = ring_order(chips)
+    back = sorted(range(chips), key=lambda place: ring[place])
+    index = lax.axis_index(WIDE)
+    core = index % 2
+    place = jnp.asarray(back, jnp.int32)[index // 2]
+    turn = 1 - 2 * core
+    pairs = []
+    for r in range(chips):
+        ahead, behind = ring[(r + 1) % chips], ring[(r - 1) % chips]
+        pairs += [(ring[r] * 2, ahead * 2), (ring[r] * 2 + 1, behind * 2 + 1)]
+    spots = jnp.asarray(ring, jnp.int32)
+    held_all = jnp.zeros((chips,) + value.shape, value.dtype)
+    for s in range(chips):
+        if s:
+            value = lax.ppermute(value, WIDE, pairs)
+        if s == chips // 2:
+            middle = value
+        spot = spots[(place - turn * s) % chips]
+        held_all = lax.dynamic_update_index_in_dim(held_all, value, spot, 0)
+    if group == 2:
+        other = lax.ppermute(held_all, "dp", [(0, 1), (1, 0)])
+        first = lax.axis_index("dp") == 0
+        planes = jnp.stack(
+            [jnp.where(first, held_all, other), jnp.where(first, other, held_all)]
+        )
+    else:
+        planes = lax.all_gather(held_all, "dp", axis=0)
+    other = lax.ppermute(planes, "spot", [(i, i ^ 1) for i in range(inner)])
+    first = core == 0
+    planes = jnp.stack([jnp.where(first, planes, other), jnp.where(first, other, planes)], axis=2)
+    return planes, middle
+
+
+def swap_groups(value, group):
+    return lax.ppermute(value, "dp", [(i, i ^ 1) for i in range(group)])
+
+
 def over_groups(value, group):
     if group == 2:
         other = lax.ppermute(value, "dp", [(0, 1), (1, 0)])
@@ -522,29 +570,32 @@
     return lax.dynamic_index_in_dim(value, at, axis, False)
 
 
-def halve_blocks(blocks, order):
+def after(value, *others):
+    return lax.optimization_barrier((value,) + others)[0]
+
+
+def spread_reduce(blocks, works):
     count = blocks.shape[0]
     bits = count.bit_length() - 1
+    order = [0, 1] + list(range(bits - 1, 1, -1))
     me = lax.axis_index(ALL)
     blocks = blocks.reshape((2,) * bits + blocks.shape[1:])
     left = list(range(bits))[::-1]
-    for bit in order:
+    for stage, bit in enumerate(order):
         axis = left.index(bit)
         left.pop(axis)
         mine = (me >> bit) & 1
         pairs = [(i, i ^ (1 << bit)) for i in range(count)]
-        theirs = lax.ppermute(pick(blocks, 1 - mine, axis), ALL, pairs)
+        sent = pick(blocks, 1 - mine, axis)
+        theirs = lax.ppermute(sent, ALL, pairs)
+        if stage < len(works):
+            theirs = after(theirs, works[stage](blocks))
         blocks = (
             pick(blocks, mine, axis).astype(jnp.float32) + theirs.astype(jnp.float32)
         ).astype(jnp.bfloat16)
     return blocks
 
 
-def spread_reduce(blocks):
-    bits = blocks.shape[0].bit_length() - 1
-    return halve_blocks(blocks, [0, 1] + list(range(bits - 1, 1, -1)))
-
-
 def held(value):
     return lax.optimization_barrier(value)
 
@@ -561,17 +612,18 @@
     out_ref[...] = (0.5 * pre * (1.0 + lax.erf(pre * (0.5**0.5)))).astype(jnp.bfloat16)
 
 
-def hidden_forward(tokens, readers, bias):
+def hidden_forward(tokens, readers, bias, half):
     total, width = tokens.shape
-    depth = readers.shape[1]
+    depth = readers.shape[1] // 2
     rows, step = total // LINE, 512
+    skip = half * depth // step
     return pl.pallas_call(
         hidden_kernel,
         grid=(depth // step, LINE),
         in_specs=[
             pl.BlockSpec((rows, width), lambda j, i: (i, 0)),
-            pl.BlockSpec((width, step), lambda j, i: (0, j)),
-            pl.BlockSpec((1, step), lambda j, i: (0, j)),
+            pl.BlockSpec((width, step), lambda j, i: (0, j + skip)),
+            pl.BlockSpec((1, step), lambda j, i: (0, j + skip)),
         ],
         out_specs=pl.BlockSpec((rows, step), lambda j, i: (i, j)),
         out_shape=shape_of((total, depth), jnp.bfloat16),
@@ -603,32 +655,67 @@
     )(grad, weight, moment, square, average)
 
 
-def pre_kernel(d_ref, tokens_ref, project_ref, expand_ref, bias_ref, out_ref):
-    grad = contract_cols(d_ref[...], project_ref[...])
+def pre_kernel(counts, at_ref, d_ref, tokens_ref, *refs):
+    sources, (expand_ref, bias_ref, out_ref) = refs[: len(counts)], refs[len(counts) :]
     pre = jnp.dot(tokens_ref[...], expand_ref[...], preferred_element_type=jnp.float32)
-    out_ref[...] = (grad * gelu_slope(pre + bias_ref[...])).astype(jnp.bfloat16)
-
-
-def pre_backward(d_full, tokens, readers, bias):
+    slope = gelu_slope(pre + bias_ref[...])
+    index = pl.program_id(0)
+    start = 0
+    for count, source in zip(counts, sources):
+
+        @pl.when((index >= start) & (index < start + count))
+        def _(source=source):
+            grad = contract_cols(d_ref[...], source[...])
+            out_ref[...] = (grad * slope).astype(jnp.bfloat16)
+
+        start += count
+
+
+def pre_backward(d_full, tokens, shared, bias, pieces):
     rows, width = tokens.shape
     depth = d_full.shape[1]
     step = 512
-    skip = width // step
+    counts = [size // step for _, _, _, size in pieces]
+    order = jnp.concatenate(
+        [
+            jnp.asarray(start // step, jnp.int32) + jnp.arange(size // step, dtype=jnp.int32)
+            for _, _, start, size in pieces
+        ]
+    )
+    specs = []
+    first = 0
+    for (source, skip, _, size), count in zip(pieces, counts):
+        low, high = skip // step, skip // step + count - 1
+        specs.append(
+            pl.BlockSpec(
+                (step, depth),
+                lambda i, at, low=low, high=high, first=first: (
+                    jnp.clip(i - first + low, low, high),
+                    0,
+                ),
+            )
+        )
+        first += count
     return pl.pallas_call(
-        pre_kernel,
-        grid=(depth // step,),
-        in_specs=[
-            pl.BlockSpec((rows, depth), lambda i: (0, 0)),
-            pl.BlockSpec((rows, width), lambda i: (0, 0)),
-            pl.BlockSpec((step, depth), lambda i: (i + skip, 0)),
-            pl.BlockSpec((width, step), lambda i: (0, i)),
-            pl.BlockSpec((1, step), lambda i: (0, i)),
-        ],
-        out_specs=pl.BlockSpec((rows, step), lambda i: (0, i)),
+        partial(pre_kernel, counts),
+        grid_spec=pltpu.PrefetchScalarGridSpec(
+            num_scalar_prefetch=1,
+            grid=(depth // step,),
+            in_specs=[
+                pl.BlockSpec((rows, depth), lambda i, at: (0, 0)),
+                pl.BlockSpec((rows, width), lambda i, at: (0, 0)),
+            ]
+            + specs
+            + [
+                pl.BlockSpec((width, step), lambda i, at: (0, at[i])),
+                pl.BlockSpec((1, step), lambda i, at: (0, at[i])),
+            ],
+            out_specs=pl.BlockSpec((rows, step), lambda i, at: (0, at[i])),
+        ),
         out_shape=shape_of((rows, depth), jnp.bfloat16),
         compiler_params=kernel_params(),
         name="pre_backward",
-    )(d_full, tokens, readers, readers, bias[None])
+    )(order, d_full, tokens, *[piece[0] for piece in pieces], shared, bias[None])
 
 
 def shards(
@@ -671,19 +758,21 @@
             jnp.zeros((14, filters.shape[2]), jnp.bfloat16),
         ]
     )
-    spread = lax.all_gather(packed, ALL, axis=0)
+    spread, middle = ring_gather(packed, inner, group)
     whole_filters = [
-        spread[:, k * share : (k + 1) * share].reshape(devices * share, -1) for k in range(4)
+        spread[:, :, :, k * share : (k + 1) * share].reshape(devices * share, -1)
+        for k in range(4)
     ]
+    spread = spread[:, :, :, 4 * share : 4 * share + 2].reshape(devices, 2, -1)
     vec_full = (
-        spread[:, 4 * share, : 30 * lanes]
+        spread[:, 0, : 30 * lanes]
         .reshape(devices, 2, 15, lanes)
         .transpose(1, 2, 0, 3)
         .reshape(2, 15, devices * lanes)
         .astype(jnp.float32)
     )
     full_offsets = (
-        spread[:wide, 4 * share + 1, : 2 * columns]
+        spread[:wide, 1, : 2 * columns]
         .reshape(wide, 2, columns)
         .transpose(1, 0, 2)
         .reshape(2, wide * columns)
@@ -699,91 +788,193 @@
     chosen = jnp.sum(jnp.where(matches, counts[None, :], 0), axis=1)
     live = (slot < chosen).astype(jnp.float32)
     rows = patches.reshape(images * GRID * GRID, width)
+    d_cols = cotangent.reshape(-1, columns)
+    part = d_cols.shape[0] // wide
+    plane = lax.axis_index("dp") % 2
+    swap = [(i, i ^ 1) for i in range(inner)]
+    cross = [(i, i ^ 1) for i in range(group)]
+    core = lax.axis_index("spot") % 2
+    depth = project.shape[0]
+    quarter = depth // 4
+    project_low = project.astype(jnp.bfloat16)
+    own = lax.dynamic_slice_in_dim(project_low, depth // 2 + plane * quarter, quarter, 0)
+    shared = jnp.concatenate([expand.astype(jnp.bfloat16), project_low[: depth // 2]])
+    own = lax.all_gather(own, WIDE, axis=1, tiled=True)
+    shared = lax.all_gather(after(shared, middle), WIDE, axis=1, tiled=True)
+    near = pick(after(own, whole_filters[0]).reshape(2, quarter // 2, -1), core, 0)
+    near = lax.ppermute(near, "dp", cross)
     pooled, first_saved = block_forward(
         rows, whole_filters[0], whole_filters[1], vec_full[0], GRID
     )
     tokens, second_saved = block_forward(
         pooled, whole_filters[2], whole_filters[3], vec_full[1], POOL, live
     )
-    d_cols = cotangent.reshape(-1, columns)
-    part = d_cols.shape[0] // wide
-    readers = jnp.concatenate([expand.astype(jnp.bfloat16), project.astype(jnp.bfloat16)])
-    readers = lax.all_gather(readers, WIDE, axis=1, tiled=True)
-    d_full = lax.all_to_all(d_cols, WIDE, split_axis=0, concat_axis=1, tiled=True)
+    near = after(near, tokens)
+    far = lax.ppermute(near, "spot", swap)
+    d_full = lax.all_to_all(d_cols, WIDE, split_axis=0, concat_axis=0, tiled=True)
+    d_full = after(d_full, whole_filters[0]).reshape(wide, part, columns)
+    d_full = d_full.transpose(1, 0, 2).reshape(part, wide * columns)
     g_out = jnp.sum(d_cols.astype(jnp.float32), axis=0)
-    tokens_after, readers, d_late = lax.optimization_barrier((tokens, readers, d_cols))
-    d_line = d_late.reshape(LINE, inner, part, columns).transpose(1, 0, 2, 3)
+    d_line = d_cols.reshape(LINE, inner, part, columns).transpose(1, 0, 2, 3)
+    tokens_after, shared, d_line, d_full, g_out = lax.optimization_barrier(
+        (tokens, shared, d_line, d_full, g_out)
+    )
+    full_expand = shared[:width]
+    tokens_line = lax.all_gather(tokens_after, "line", axis=0, tiled=True)
     d_line = lax.all_to_all(d_line, "spot", split_axis=0, concat_axis=0, tiled=True)
     d_line = d_line.reshape(inner, LINE * part, columns)
-    full_expand = readers[:width]
-    tokens_line = lax.all_gather(tokens_after, "line", axis=0, tiled=True)
-    hidden_line = hidden_forward(tokens_line, readers, full_offsets[0])
-    core = lax.axis_index("spot") % 2
     d_cores = d_line.reshape(inner // 2, 2, LINE * part, columns)
-
-    def project_part(at):
+    near_at = depth // 2 + (1 - plane) * quarter + core * (quarter // 2)
+    far_at = depth // 2 + (1 - plane) * quarter + (1 - core) * (quarter // 2)
+    d_pre = pre_backward(
+        d_full,
+        tokens,
+        shared,
+        full_offsets[0],
+        [
+            (shared, width, 0, depth // 2),
+            (own, 0, depth // 2 + plane * quarter, quarter),
+            (near, 0, near_at, quarter // 2),
+            (far, 0, far_at, quarter // 2),
+        ],
+    )
+    d_tokens = contract_cols(d_pre, full_expand)
+    d_pooled, g_in_two, g_out_two, g_vec_two = block_backward(
+        d_tokens, second_saved, whole_filters[2], whole_filters[3], vec_full[1], POOL, live
+    )
+    g_two = reduce_block(g_in_two, g_out_two, g_vec_two, devices)
+    d_pooled, g_two, d_theirs, d_mine = held(
+        (d_pooled, g_two, pick(d_cores, 1 - core, 1), pick(d_cores, core, 1))
+    )
+    g_two = lax.psum_scatter(g_two, ALL, scatter_dimension=0, tiled=False)
+    d_rows, g_in_one, g_out_one, g_vec_one = block_backward(
+        d_pooled, first_saved, whole_filters[0], whole_filters[1], vec_full[0], GRID
+    )
+    patch_gradient = d_rows.reshape(images, GRID * GRID, width)
+    g_one = reduce_block(g_in_one, g_out_one, g_vec_one, devices)
+    got = {}
+
+    def expand_work(done):
+        ones = jnp.ones((tokens.shape[0], 1), jnp.bfloat16)
+        more = [after(tokens, done), ones, jnp.zeros((tokens.shape[0], 15), jnp.bfloat16)]
+        got["expand"] = contract_rows(jnp.concatenate(more, axis=1), d_pre).astype(jnp.bfloat16)
+        return got["expand"]
+
+    def hidden_work(half, done):
+        tokens_all = after(tokens_line, done)
+        got["hidden", half] = hidden_forward(tokens_all, shared, full_offsets[0], half)
+        return got["hidden", half]
+
+    def project_part(d_part, half):
         return lax.dot_general(
-            held(pick(d_cores, at, 1)),
-            hidden_line,
+            d_part,
+            got["hidden", half],
             (((1,), (0,)), ((), ())),
             preferred_element_type=jnp.float32,
         )
 
-    d_pre = pre_backward(d_full, tokens, readers, full_offsets[0])
-    theirs_sent = project_part(1 - core).astype(jnp.bfloat16)
-    theirs = lax.ppermute(theirs_sent, "spot", [(i, i ^ 1) for i in range(inner)])
-    g_project = project_part(core) + theirs.astype(jnp.float32)
-    spot = lax.axis_index("spot") // 2
-    step = 1
-    while g_project.shape[0] > 1:
-        halves = g_project.reshape(g_project.shape[0] // 2, 2, columns, -1)
-        theirs_sent = pick(halves, 1 - spot % 2, 1).astype(jnp.bfloat16)
-        step *= 2
-        theirs = lax.ppermute(theirs_sent, "spot", [(i, i ^ step) for i in range(inner)])
-        g_project = pick(halves, spot % 2, 1) + theirs.astype(jnp.float32)
-        spot = spot // 2
-    g_project = over_groups(g_project[0].astype(jnp.bfloat16), group)
-    ones = jnp.ones((tokens.shape[0], 1), jnp.bfloat16)
-    tokens_more = jnp.concatenate(
-        [tokens, ones, jnp.zeros((tokens.shape[0], 15), jnp.bfloat16)], axis=1
-    )
-    g_expand_full = contract_rows(tokens_more, d_pre).astype(jnp.bfloat16)
-    d_tokens = contract_cols(d_pre, full_expand)
-    g_expand = lax.psum_scatter(g_expand_full, WIDE, scatter_dimension=1, tiled=True)
+    def theirs_work(half, *done):
+        theirs = project_part(after(d_theirs, *done), half).astype(jnp.bfloat16)
+        got["sent", half] = lax.ppermute(theirs, "spot", [(i, i ^ 1) for i in range(inner)])
+        return theirs
+
+    def mine_work(half, done):
+        mine = project_part(after(d_mine, done), half)
+        got["sum", half] = mine + got["sent", half].astype(jnp.float32)
+        spot = lax.axis_index("spot") // 2
+        halves = got["sum", half].reshape(inner // 4, 2, columns, -1)
+        theirs = pick(halves, 1 - spot % 2, 1).astype(jnp.bfloat16)
+        got["sent", half] = lax.ppermute(theirs, "spot", [(i, i ^ 2) for i in range(inner)])
+        return theirs
+
+    def finish_work(half, done):
+        spot = lax.axis_index("spot") // 2
+        total = got["sum", half].reshape(inner // 4, 2, columns, -1)
+        theirs = after(got["sent", half], done)
+        total = pick(total, spot % 2, 1) + theirs.astype(jnp.float32)
+        step = 4
+        while total.shape[0] > 1:
+            spot = spot // 2
+            halves = total.reshape(total.shape[0] // 2, 2, columns, -1)
+            theirs = pick(halves, 1 - spot % 2, 1).astype(jnp.bfloat16)
+            theirs = lax.ppermute(theirs, "spot", [(i, i ^ step) for i in range(inner)])
+            total = pick(halves, spot % 2, 1) + theirs.astype(jnp.float32)
+            step *= 2
+        total = total[0].astype(jnp.bfloat16)
+        got["total", half] = total
+        got["sent", half] = swap_groups(total, group)
+        return total
+
+    def swap_work(half, done):
+        total = got["total", half]
+        other = after(got["sent", half], done)
+        got["project", half] = total.astype(jnp.float32) + other.astype(jnp.float32)
+        if group != 2:
+            got["project", half] = over_groups(total, group)
+        return got["project", half]
+
+    def work_two(done):
+        return hidden_work(0, done)
+
+    def work_three(done):
+        sent = mine_work(0, theirs_work(0, done))
+        got["order"] = finish_work(0, hidden_work(1, sent))
+        return got["order"]
+
+    def work_four(done):
+        return mine_work(1, theirs_work(1, done, got["order"]))
+
+    at = lax.axis_index("line") * inner * columns
+    other = jnp.concatenate(
+        [
+            lax.dynamic_slice_in_dim(piece, at, inner * columns, 1)
+            for piece in (near, far)
+        ]
+    )
+    other = jnp.roll(other.reshape(2, quarter // 2, -1), core, 0).reshape(quarter, -1)
+    sides = jnp.stack([lax.dynamic_slice_in_dim(own, at, inner * columns, 1), other])
+    column_sides = jnp.roll(sides, plane, 0).reshape(2 * quarter, -1)
+    column_shared = lax.dynamic_slice(
+        shared, (width, at), (depth // 2, inner * columns)
+    )
+    got["columns", 0] = column_shared
+    got["columns", 1] = column_sides
+
+    def readout_part(half, *done):
+        return jnp.dot(
+            after(got["hidden", half], *done),
+            got["columns", half],
+            preferred_element_type=jnp.float32,
+        )
+
+    def work_five(done):
+        at = lax.axis_index("line") * inner * columns
+        bias = lax.dynamic_slice_in_dim(full_offsets[1], at, inner * columns, 0)
+        out = readout_part(0, done) + bias
+        first = swap_work(0, out)
+        second = finish_work(1, out)
+        out = out + readout_part(1, first, second)
+        got["out"] = out.astype(jnp.bfloat16)
+        return got["out"]
+
+    g_one = spread_reduce(g_one, [expand_work, work_two, work_three, work_four, work_five])
+    swap_work(1, got["out"])
+    g_expand = lax.psum_scatter(got["expand"], WIDE, scatter_dimension=1, tiled=True)
+    g_expand = after(g_expand, got["out"])
     g_expand = jnp.concatenate(
         [g_expand[: width + 1], g_out[None].astype(jnp.bfloat16), g_expand[width + 2 :]]
     )
     g_expand = over_groups(g_expand, group)
     g_offsets = g_expand[width : width + 2]
     g_expand = g_expand[:width]
-    d_pooled, g_in_two, g_out_two, g_vec_two = block_backward(
-        d_tokens, second_saved, whole_filters[2], whole_filters[3], vec_full[1], POOL, live
-    )
-    d_pooled, theirs_sent = lax.optimization_barrier((d_pooled, theirs_sent))
-    d_rows, g_in_one, g_out_one, g_vec_one = block_backward(
-        d_pooled, first_saved, whole_filters[0], whole_filters[1], vec_full[0], GRID
-    )
-    hidden_line, d_rows = lax.optimization_barrier((hidden_line, d_rows))
-    at = lax.axis_index("line") * inner * columns
-    project_line = lax.dynamic_slice(
-        readers, (width, at), (readers.shape[0] - width, inner * columns)
-    )
-    offset_line = lax.dynamic_slice_in_dim(full_offsets[1], at, inner * columns, 0)
-    out_line = (
-        jnp.dot(hidden_line, project_line, preferred_element_type=jnp.float32) + offset_line
-    ).astype(jnp.bfloat16)
-    out_line = out_line.reshape(LINE * part, inner, columns).transpose(1, 0, 2)
+    g_project = jnp.concatenate([got["project", 0], got["project", 1]], axis=1)
+    out_line = got["out"].reshape(LINE * part, inner, columns).transpose(1, 0, 2)
     out_cols = lax.all_to_all(out_line, "spot", split_axis=0, concat_axis=0, tiled=True)
     readout = (
         out_cols.reshape(inner, LINE, part, columns)
         .transpose(1, 0, 2, 3)
         .reshape(-1, POOL * POOL, columns)
     )
-    patch_gradient = d_rows.reshape(images, GRID * GRID, width)
-    g_two = reduce_block(g_in_two, g_out_two, g_vec_two, devices)
-    g_two = spread_reduce(g_two)
-    g_one = reduce_block(g_in_one, g_out_one, g_vec_one, devices)
-    g_one = spread_reduce(g_one)
     g_filters = jnp.stack(
         [g_one[:share], g_one[share : 2 * share], g_two[:share], g_two[share : 2 * share]]
     ).astype(jnp.float32)

time: 908 us -> 842 us (0.927)
  waiting for transfers between devices: 364 us -> 222 us
  starting transfers between devices: 29.8 us -> 59.9 us
  between operations: 15.7 us -> 38.1 us
  other arithmetic: 50.5 us -> 66 us
    all_gather x2, waiting for transfers between devices: 261 us -> 23.7 us  [the longest x1 23.7 us: shards(): shared = lax.all_gather(after(shared, middle), WIDE, axis=1, tiled=True)]
    ppermute x12 -> x22, waiting for transfers between devices: 103 us -> 164 us  [the longest x1 47.5 us: ring_gather(): other = lax.ppermute(held_all, 'dp', [(0, 1), (1, 0)])]
    ppermute x12 -> x22, starting transfers between devices: 9.79 us -> 42.7 us  [the longest x7 22.2 us: ring_gather(): value = lax.ppermute(value, WIDE, pairs)]
    reduce_scatter x1 -> x2, waiting for transfers between devices: 0.02 us -> 18.2 us  [the longest x1 18.1 us: shards(): lax.psum_scatter(got['expand'], WIDE, scatter_dimension=1, tiled=True)]
    all_to_all x1, waiting for transfers between devices: 0.01 us -> 16 us  [shards(): lax.all_to_all(d_cols, WIDE, split_axis=0, concat_axis=0, tiled=True)]
    another operation x0 -> x5, other arithmetic: none -> 13.6 us  [the longest x3 8.05 us: ring_gather(): jnp.stack([jnp.where(first, planes, other), jnp.where(first, other, plane...]
    concatenate x1 -> x6, other arithmetic: 1.66 us -> 11.2 us  [the longest x1 4.4 us: shards(): column_sides = jnp.roll(sides, plane, 0).reshape(2 * quarter, -1)]
    convert_element_type x14 -> x10, other arithmetic: 22.9 us -> 13.4 us  [the longest x5 8.36 us: spread_reduce(): blocks = (pick(blocks, mine, axis).astype(jnp.float32) + theirs.astype(jn...]
  transfers between devices with their start and end apart: 21 -> 31, of which waited for: 8 -> 18; matrix products, arithmetic and copies ran while one was open for 21% -> 27% of each run, Pallas kernels for 25% -> 33%
where the time goes in v2:
time: 842 us; the launch traced here: 837 us
  Pallas kernels  274 us (33%)
  waiting for transfers between devices  222 us (26%)
  matrix products  113 us (13%)
  other arithmetic  66 us (8%)
  local copies, waits for them, and re-layouts  64 us (8%)
  starting transfers between devices  59.9 us (7%)
  between operations  38.1 us (5%)
    pallas_call x2, Pallas kernels, block_backward(): pl.pallas_call(partial(backward_kernel, side), grid=(total // size,), in_...  89.6 us
    pallas_call x2, Pallas kernels, block_forward(): pl.pallas_call(partial(forward_kernel, side), grid=(total // size,), in_s...  83.8 us
    ppermute x1, waiting for transfers between devices, ring_gather(): other = lax.ppermute(held_all, 'dp', [(0, 1), (1, 0)])  47.5 us
    ppermute x7, waiting for transfers between devices, ring_gather(): value = lax.ppermute(value, WIDE, pairs)  47.2 us
    pallas_call x2, Pallas kernels, hidden_forward(): pl.pallas_call(hidden_kernel, grid=(depth // step, LINE), in_specs=[pl.Bl...  44.3 us
    pallas_call x1, Pallas kernels, pre_backward(): pl.pallas_call(partial(pre_kernel, counts), grid_spec=pltpu.PrefetchScala...  40.1 us
    dot_general x4, matrix products, project_part(): lax.dot_general(d_part, got['hidden', half], (((1,), (0,)), ((), ())), pr...  35.5 us
    dot_general x5, matrix products, contract_rows(): lax.dot_general(left, right, (((0,), (0,)), ((), ())), preferred_element_...  34.1 us
  transfers between devices with their start and end apart: 31, of which 18 were waited for; matrix products, arithmetic and copies ran while one was open for 27% of the time, Pallas kernels for 33%

profile of v2, /device:TPU:0, one launch (start us, length us, event | category | flops | bytes accessed | tf_op | source)
XLA Modules:
  0.0 836.7 jit_solution(3363046169440776843)
XLA Ops:
  15.2 4.6 collective-permute-done
  21.9 9.2 %collective-permute-done.1 = bf16[144,1024]{1,0:T(8,128)(2,1)S(1)} collective-permute-done((bf16[144,1024]{1,0:T(8,128)(2,1)S(1)}, bf16[144,1024]{1,0:T(8,128)(2,1)S(1)}, u32[]{:S(2)}, u32[]{:S(2)}) %collective-permute-start.1) | collective-permute-done | bytes 294944 | tf_op jit(solution)/shard_map/ppermute | solution.py:522
  33.8 10.2 %collective-permute-done.2 = bf16[144,1024]{1,0:T(8,128)(2,1)} collective-permute-done((bf16[144,1024]{1,0:T(8,128)(2,1)S(1)}, bf16[144,1024]{1,0:T(8,128)(2,1)}, u32[]{:S(2)}, u32[]{:S(2)}) %collective-permute-start.2) | collective-permute-done | bytes 294944 | tf_op jit(solution)/shard_map/ppermute | solution.py:522
  78.7 10.6 %collective-permute-done.4 = bf16[144,1024]{1,0:T(8,128)(2,1)S(1)} collective-permute-done((bf16[144,1024]{1,0:T(8,128)(2,1)}, bf16[144,1024]{1,0:T(8,128)(2,1)S(1)}, u32[]{:S(2)}, u32[]{:S(2)}) %collective-permute-start.4) | collective-permute-done | bytes 294944 | tf_op jit(solution)/shard_map/ppermute | solution.py:522
  89.4 6.0 collective-permute-start.5
  102.1 6.0 collective-permute-done.6
  109.7 47.5 %collective-permute-done.7 = bf16[8,144,1024]{2,1,0:T(8,128)(2,1)} collective-permute-done((bf16[8,144,1024]{2,1,0:T(8,128)(2,1)S(1)}, bf16[8,144,1024]{2,1,0:T(8,128)(2,1)}, u32[]{:S(2)}, u32[]{:S(2)}) %collective-permute-start.7) | collective-permute-done | bytes 2359328 | tf_op jit(solution)/shard_map/ppermute | solution.py:528
  162.9 4.8 all-to-all-start
  167.7 5.5 collective-permute-done.8
  180.3 3.6 pad_maximum_fusion.3
  183.9 4.8 dynamic-slice_bitcast_fusion
  195.9 63.5 %block_forward_24.1 = (f32[2304,1024]{1,0:T(8,128)}, f32[2304,1024]{1,0:T(8,128)}, f32[2304,1024]{1,0:T(8,128)}, f32[2304,128]{1,0:T(8,128)}, f32[2304,128]{1,0:...) custom-call(bf16[2304,1024]{1,0:T(8,128)(2,1)} %bitcast.186, ...), custom_call_target="tpu_custom_call" | custom-call | tf_op jit(solution)/shard_map/block_forward_24/pallas_call | solution.py:412
  260.2 20.3 %block_forward_12.1 = (f32[576,1024]{1,0:T(8,128)}, f32[576,1024]{1,0:T(8,128)}, f32[576,1024]{1,0:T(8,128)}, f32[576,128]{1,0:T(8,128)}, f32[576,128]{1,0:T(8,1...) custom-call(f32[4]{0:T(128)} %compare_convert_fusion.refs_0_, ...), custom_call_target="tpu_custom_call" | custom-call | tf_op jit(solution)/shard_map/block_forward_12/pallas_call | solution.py:412
  282.5 4.1 convert_reduce_fusion
  286.6 16.0 %all-to-all-done = bf16[16,576,256]{2,1,0:T(8,128)(2,1)} async-done(((bf16[16,576,256]{2,1,0:T(8,128)(2,1)}), bf16[16,576,256]{2,1,0:T(8,128)(2,1)}, u32[]{:S(2)}, u32[]{:S(2)}) %all-to-all-start) | async-done | bytes 4718624 | tf_op jit(solution)/shard_map/all_to_all | solution.py:814
  302.6 5.2 copy.149
  307.8 23.7 %all-gather.4.cloned.1.call-done.refs_0_.refs_4_.expand_ref = bf16[3072,4096]{1,0:T(8,128)(2,1)} async-done(((bf16[3072,256]{1,0:T(8,128)(2,1)}), bf16[3072,4096]{1,0:T(8,128)(2,1)}) %all-gather.4.cloned.1.call-update) | async-done | bytes 25165840 | tf_op jit(solution)/shard_map/all_gather | solution.py:803
  331.5 4.9 copy.117
  336.4 4.9 all-to-all-start.1
  343.2 40.1 %pre_backward.1 = bf16[576,4096]{1,0:T(8,128)(2,1)} custom-call(s32[8]{0:T(128)} %pad_add_fusion.at_ref, bf16[576,4096]{1,0:T(8,128)(2,1)} %bitcast.180, bf16[576,1024]{1,0:T(8,128)(2,1)} %get-tuple-element.120.tokens_ref, bf16[3072,4096]{1,0:T(8,128)(2,1)} %all-gather.4.cloned.1.call-done.refs_0_.refs_4_.expand_ref, ...), custom_call_target="tpu_custom_call" | custom-call | tf_op jit(solution)/shard_map/pre_backward/pallas_call | solution.py:699
  383.3 10.0 %fusion.9.refs_1_ = f32[576,1024]{1,0:T(8,128)} fusion(bf16[576,4096]{1,0:T(8,128)(2,1)} %pre_backward.1, bf16[3072,4096]{1,0:T(8,128)(2,1)} %all-gather.4.cloned.1.call-done.refs_0_.refs_4_.expand_ref), kind=kOutput, calls=%fused_computation.25 | convolution fusion | flops 4831838208 | bytes 15466496 | tf_op jit(solution)/shard_map/dot_general | solution.py:35
  393.3 22.5 %block_backward_12.1 = (f32[576,1024]{1,0:T(8,128)}, bf16[576,1024]{1,0:T(8,128)(2,1)}, bf16[576,1024]{1,0:T(8,128)(2,1)}, f32[128,1024]{1,0:T(8,128)}) custom-call(f32[4]{0:T(128)} %compare_convert_fusion.refs_0_, f32[576,1024]{1,0:T(8,128)} %fusion.9.refs_1_, bf16[576,1024]{1,0:T(8,128)(2,1)} %get-tuple-element.88.refs_1_.refs_2_, ...), custom_call_target="tpu_custom_call" | custom-call | tf_op jit(solution)/shard_map/block_backward_12/pallas_call | solution.py:448
  425.3 4.9 dynamic-slice_bitcast_fusion.2
  430.2 67.1 %block_backward_24.1 = (bf16[2304,1024]{1,0:T(8,128)(2,1)}, bf16[2304,1024]{1,0:T(8,128)(2,1)}, bf16[2304,1024]{1,0:T(8,128)(2,1)}, f32[128,1024]{1,0:T(8,128)}) custom-call(bf16[576,144]{1,0:T(8,128)(2,1)} %select_convert_fusion.refs_0_, f32[576,1024]{1,0:T(8,128)} %get-tuple-element.109.refs_1_, bf16[2304,1024]{1,0:T(8,128)(2,1)} %bitcast.187, ...), custom_call_target="tpu_custom_call" | custom-call | tf_op jit(solution)/shard_map/block_backward_24/pallas_call | solution.py:448
  499.0 8.8 %convolution_convert_fusion.1 = bf16[1024,1024]{1,0:T(8,128)(2,1)S(1)} fusion(bf16[2304,1024]{1,0:T(8,128)(2,1)} %get-tuple-element.117, bf16[2304,1024]{1,0:T(8,128)(2,1)} %get-tuple-element.118), kind=kOutput, calls=%fused_computation.67 | convolution fusion | flops 4832886784 | bytes 11534336 | tf_op jit(solution)/shard_map/dot_general | solution.py:29
  507.8 8.4 %convolution_convert_fusion.2 = bf16[1024,1024]{0,1:T(8,128)(2,1)S(1)} fusion(bf16[2304,1024]{1,0:T(8,128)(2,1)S(1)} %bitcast.228, bf16[2304,1024]{1,0:T(8,128)(2,1)} %bitcast.188), kind=kOutput, calls=%fused_computation.68 | convolution fusion | flops 4832886784 | bytes 11534336 | tf_op jit(solution)/shard_map/dot_general | solution.py:29
  520.4 11.7 %convolution_convert_fusion = bf16[1040,4096]{1,0:T(8,128)(2,1)} fusion(bf16[576,1040]{1,0:T(8,128)(2,1)S(1)} %concatenate.59, bf16[576,4096]{1,0:T(8,128)(2,1)} %pre_backward.1), kind=kOutput, calls=%fused_computation | convolution fusion | flops 4911595520 | bytes 14436352 | tf_op jit(solution)/shard_map/dot_general | solution.py:29
  538.4 22.1 %hidden_forward.2 = bf16[2304,2048]{1,0:T(8,128)(2,1)} custom-call(bf16[2304,1024]{1,0:T(8,128)(2,1)} %all-gather.6.cloned.1.call-done.tokens_ref, bf16[3072,4096]{1,0:T(8,128)(2,1)} %all-gather.4.cloned.1.call-done.refs_0_.refs_4_.expand_ref, f32[1,4096]{1,0:T(1,128)} %bitcast.218), custom_call_target="tpu_custom_call" | custom-call | tf_op jit(solution)/shard_map/hidden_forward/pallas_call | solution.py:620
  560.5 27.2 %collective-permute-done.12 = bf16[2,2,2,80,1024]{4,3,2,1,0:T(8,128)(2,1)} collective-permute-done((bf16[2,2,2,80,1024]{4,3,2,1,0:T(8,128)(2,1)}, bf16[2,2,2,80,1024]{4,3,2,1,0:T(8,128)(2,1)}, u32[]{:S(2)}, u32[]{:S(2)}) %collective-permute-start.12) | collective-permute-done | bytes 1310752 | tf_op jit(solution)/shard_map/ppermute | solution.py:590
  590.7 9.4 %fusion.17 = bf16[2,256,2048]{2,1,0:T(8,128)(2,1)} fusion(bf16[2,2304,256]{2,1,0:T(8,128)(2,1)} %get-tuple-element.131, bf16[2304,2048]{1,0:T(8,128)(2,1)} %hidden_forward.2), kind=kOutput, calls=%fused_computation.45 | convolution fusion | flops 4832886784 | bytes 13893632 | tf_op jit(solution)/shard_map/dot_general | solution.py:869
  600.1 4.5 collective-permute-done.14
  604.6 8.7 %convert_add_fusion.2 = f32[2,256,2048]{2,1,0:T(8,128)S(1)} fusion(bf16[2,256,2048]{2,1,0:T(8,128)(2,1)} %collective-permute-done.14, bf16[2,2304,256]{2,1,0:T(8,128)(2,1)} %get-tuple-element.132, bf16[2304,2048]{1,0:T(8,128)(2,1)} %hidden_forward.2), kind=kOutput, calls=%fused_computation.43 | convolution fusion | flops 4833935360 | bytes 18087936 | tf_op jit(solution)/shard_map/dot_general | solution.py:869
  620.6 22.1 %hidden_forward.3 = bf16[2304,2048]{1,0:T(8,128)(2,1)} custom-call(bf16[2304,1024]{1,0:T(8,128)(2,1)} %all-gather.6.cloned.1.call-done.tokens_ref, bf16[3072,4096]{1,0:T(8,128)(2,1)} %all-gather.4.cloned.1.call-done.refs_0_.refs_4_.expand_ref, f32[1,4096]{1,0:T(1,128)} %bitcast.219), custom_call_target="tpu_custom_call" | custom-call | tf_op jit(solution)/shard_map/hidden_forward/pallas_call | solution.py:620
  642.7 13.4 %collective-permute-done.15 = bf16[1,256,2048]{2,1,0:T(8,128)(2,1)} collective-permute-done((bf16[1,256,2048]{2,1,0:T(8,128)(2,1)S(1)}, bf16[1,256,2048]{2,1,0:T(8,128)(2,1)}, u32[]{:S(2)}, u32[]{:S(2)}) %collective-permute-start.15) | collective-permute-done | bytes 1048608 | tf_op jit(solution)/shard_map/ppermute | solution.py:887
  659.6 10.4 %fusion.20 = bf16[2,256,2048]{2,1,0:T(8,128)(2,1)} fusion(bf16[2,2304,256]{2,1,0:T(8,128)(2,1)S(1)} %copy-done.15, bf16[2304,2048]{1,0:T(8,128)(2,1)} %hidden_forward.3), kind=kOutput, calls=%fused_computation.46 | convolution fusion | flops 4832886784 | bytes 13893632 | tf_op jit(solution)/shard_map/dot_general | solution.py:869
  676.1 4.4 fusion.15
  681.7 7.5 collective-permute-start.16
  689.2 7.0 convert_add_fusion.1
  698.0 5.6 collective-permute-done.16
  703.7 15.8 %convolution_add_fusion = f32[2304,1024]{0,1:T(8,128)} fusion(bf16[2304,2048]{1,0:T(8,128)(2,1)S(1)} %bitcast.194, f32[1024]{0:T(1024)S(1)} %bitcast.225, bf16[3072,4096]{1,0:T(8,128)(2,1)} %all-gather.4.cloned.1.call-done.refs_0_.refs_4_.expand_ref, s32[]{:T(128)S(6)} %select_n.521), kind=kOutput, calls=%fused_computation.27 | convolution fusion | flops 9666035712 | bytes 23072772 | tf_op jit(solution)/shard_map/dot_general | solution.py:944
  720.5 11.7 %collective-permute-done.19 = bf16[1,256,2048]{2,1,0:T(8,128)(2,1)S(1)} collective-permute-done((bf16[1,256,2048]{2,1,0:T(8,128)(2,1)S(1)}, bf16[1,256,2048]{2,1,0:T(8,128)(2,1)S(1)}, u32[]{:S(2)}, u32[]{:S(2)}) %collective-permute-start.19) | collective-permute-done | bytes 1048608 | tf_op jit(solution)/shard_map/ppermute | solution.py:887
  733.3 17.5 %add_convert_fusion = bf16[2304,1024]{0,1:T(8,128)(2,1)} fusion(f32[2304,1024]{0,1:T(8,128)} %convolution_add_fusion, bf16[2304,2048]{1,0:T(8,128)(2,1)} %hidden_forward.3, bf16[2048,1024]{1,0:T(8,128)(2,1)} %bitcast.207), kind=kOutput, calls=%fused_computation.19 | convolution fusion | flops 9668395008 | bytes 27787264 | tf_op jit(solution)/shard_map/dot_general | solution.py:944
  752.4 6.7 copy.127
  759.1 5.3 all-to-all-start.2
  776.5 18.1 %reduce-scatter.5.cloned.1.call-done = bf16[1040,256]{1,0:T(8,128)(2,1)} async-done(((bf16[1040,4096]{1,0:T(8,128)(2,1)}), bf16[1040,256]{1,0:T(8,128)(2,1)}) %reduce-scatter.5.cloned.1.call-update) | async-done | bytes 532496 | tf_op jit(solution)/shard_map/reduce_scatter | solution.py:962
  798.5 4.0 pad_maximum_fusion.2.grad_ref
  802.5 16.3 %adamw_turned.1 = (f32[4096,256]{1,0:T(8,128)}, f32[4096,256]{1,0:T(8,128)}, f32[4096,256]{1,0:T(8,128)}, f32[4096,256]{1,0:T(8,128)}, bf16[4096,256]{1,0:T(8,128)(2,1)}) custom-call(f32[256,4096]{1,0:T(8,128)} %pad_maximum_fusion.2.grad_ref, f32[4096,256]{1,0:T(8,128)} %refs_0_.1, f32[4096,256]{1,0:T(8,128)} %refs_1_.1, f32[4096,256]{1,0:T(8,128)} %refs_2_.1, ...), custom_call_target="tpu_custom_call" | custom-call | tf_op jit(solution)/shard_map/adamw_turned/pallas_call | solution.py:646
  825.0 4.9 copy.128
  (272 shorter events, 127.0 us)
Async XLA Ops:
  7.2 176.7 %all-gather.8.cloned.1.call-start = ((), (), s32[]{:S(2)}) async-start(), calls=%async_computation.7 | async-start | bytes 8912896 | tf_op jit(solution)/shard_map/all_gather | solution.py:802
  7.3 26.4 %copy-start.12 = (f32[1024,256]{1,0:T(8,128)S(1)}, f32[1024,256]{1,0:T(8,128)}, u32[]{:S(2)}) copy-start(f32[1024,256]{1,0:T(8,128)} %param.36) | copy-start | bytes 3145732
  10.6 320.8 %all-gather.4.cloned.1.call-start = ((), (), s32[]{:S(2)}) async-start(), calls=%async_computation.5 | async-start | bytes 26738688 | tf_op jit(solution)/shard_map/all_gather | solution.py:803
  12.1 39.1 %copy-start.43 = (s32[8]{0:T(128)S(1)}, s32[8]{0:T(128)}, u32[]{:S(2)}) copy-start(s32[8]{0:T(128)} %constant.441.clone) | copy-start | bytes 100
  12.1 46.4 %copy-start.30 = (s32[8]{0:T(128)S(1)}, s32[8]{0:T(128)}, u32[]{:S(2)}) copy-start(s32[8]{0:T(128)} %constant.442.clone) | copy-start | bytes 100
  12.1 7.7 collective-permute-start
  19.8 11.3 %collective-permute-start.1 = (bf16[144,1024]{1,0:T(8,128)(2,1)S(1)}, bf16[144,1024]{1,0:T(8,128)(2,1)S(1)}, u32[]{:S(2)}, u32[]{:S(2)}) collective-permute-start(bf16[144,1024]{1,0:T(8,128)(2,1)S(1)} %collective-permute-done), channel_id=1, source_target_pairs={{0,4},{1,3},{4,8},{5,1},{8,12},{9,5},{12,14},{13,9},{14,10},{15,13... | collective-permute-start | bytes 884744 | tf_op jit(solution)/shard_map/ppermute | solution.py:522
  31.2 12.8 %collective-permute-start.2 = (bf16[144,1024]{1,0:T(8,128)(2,1)S(1)}, bf16[144,1024]{1,0:T(8,128)(2,1)}, u32[]{:S(2)}, u32[]{:S(2)}) collective-permute-start(bf16[144,1024]{1,0:T(8,128)(2,1)S(1)} %collective-permute-done.1), channel_id=1, source_target_pairs={{0,4},{1,3},{4,8},{5,1},{8,12},{9,5},{12,14},{13,9},{14,10},{15,13... | collective-permute-start | bytes 884744 | tf_op jit(solution)/shard_map/ppermute | solution.py:522
  33.8 44.9 %copy-start.23 = (bf16[144,1024]{1,0:T(8,128)(2,1)S(1)}, bf16[144,1024]{1,0:T(8,128)(2,1)}, u32[]{:S(2)}) copy-start(bf16[144,1024]{1,0:T(8,128)(2,1)} %copy-done.22) | copy-start | bytes 884740
  44.0 34.7 %copy-start.25 = (bf16[144,1024]{1,0:T(8,128)(2,1)S(1)}, bf16[144,1024]{1,0:T(8,128)(2,1)}, u32[]{:S(2)}) copy-start(bf16[144,1024]{1,0:T(8,128)(2,1)} %copy-done.24) | copy-start | bytes 884740
  44.0 7.1 collective-permute-start.3
  51.2 22.8 %copy-start.26 = (bf16[144,1024]{1,0:T(8,128)(2,1)}, bf16[144,1024]{1,0:T(8,128)(2,1)S(1)}, u32[]{:S(2)}) copy-start(bf16[144,1024]{1,0:T(8,128)(2,1)S(1)} %collective-permute-done.3) | copy-start | bytes 884740
  74.7 21.7 %copy-start.27 = (bf16[144,1024]{1,0:T(8,128)(2,1)S(1)}, bf16[144,1024]{1,0:T(8,128)(2,1)}, u32[]{:S(2)}) copy-start(bf16[144,1024]{1,0:T(8,128)(2,1)} %copy-done.26) | copy-start | bytes 884740
  75.1 14.3 %collective-permute-start.4 = (bf16[144,1024]{1,0:T(8,128)(2,1)}, bf16[144,1024]{1,0:T(8,128)(2,1)S(1)}, u32[]{:S(2)}, u32[]{:S(2)}) collective-permute-start(bf16[144,1024]{1,0:T(8,128)(2,1)} %copy-done.26), channel_id=1, source_target_pairs={{0,4},{1,3},{4,8},{5,1},{8,12},{9,5},{12,14},{13,9},{14,10},{15,13... | collective-permute-start | bytes 884744 | tf_op jit(solution)/shard_map/ppermute | solution.py:522
  89.4 10.2 %collective-permute-start.5 = (bf16[144,1024]{1,0:T(8,128)(2,1)S(1)}, bf16[144,1024]{1,0:T(8,128)(2,1)S(1)}, u32[]{:S(2)}, u32[]{:S(2)}) collective-permute-start(bf16[144,1024]{1,0:T(8,128)(2,1)S(1)} %collective-permute-done.4), channel_id=1, source_target_pairs={{0,4},{1,3},{4,8},{5,1},{8,12},{9,5},{12,14},{13,9},{14,10},{15,13... | collective-permute-start | bytes 884744 | tf_op jit(solution)/shard_map/ppermute | solution.py:522
  99.6 8.5 %collective-permute-start.6 = (bf16[144,1024]{1,0:T(8,128)(2,1)S(1)}, bf16[144,1024]{1,0:T(8,128)(2,1)S(1)}, u32[]{:S(2)}, u32[]{:S(2)}) collective-permute-start(bf16[144,1024]{1,0:T(8,128)(2,1)S(1)} %collective-permute-done.5), channel_id=1, source_target_pairs={{0,4},{1,3},{4,8},{5,1},{8,12},{9,5},{12,14},{13,9},{14,10},{15,13... | collective-permute-start | bytes 884744 | tf_op jit(solution)/shard_map/ppermute | solution.py:522
  108.1 49.1 %collective-permute-start.7 = (bf16[8,144,1024]{2,1,0:T(8,128)(2,1)S(1)}, bf16[8,144,1024]{2,1,0:T(8,128)(2,1)}, u32[]{:S(2)}, u32[]{:S(2)}) collective-permute-start(bf16[8,144,1024]{2,1,0:T(8,128)(2,1)S(1)} %bitcast_dynamic-update-slice_fusion), channel_id=1, source_target_pairs={{0,16},{16,0},{1,17},{17,1},{2,18},{18,2},{3,19},{19,3},{4,20},{20... | collective-permute-start | bytes 7077896 | tf_op jit(solution)/shard_map/ppermute | solution.py:528
  162.9 10.3 %collective-permute-start.8 = (bf16[2,8,144,1024]{3,2,1,0:T(8,128)(2,1)}, bf16[2,8,144,1024]{3,2,1,0:T(8,128)(2,1)}, u32[]{:S(2)}, u32[]{:S(2)}) collective-permute-start(bf16[2,8,144,1024]{3,2,1,0:T(8,128)(2,1)} %pad_maximum_fusion.1), channel_id=1, source_target_pairs={{0,1},{1,0},{2,3},{3,2},{4,5},{5,4},{6,7},{7,6},{8,9},{9,8},{10,11... | collective-permute-start | bytes 14155784 | tf_op jit(solution)/shard_map/ppermute | solution.py:535
  162.9 139.8 %all-to-all-start = ((bf16[16,576,256]{2,1,0:T(8,128)(2,1)}), bf16[16,576,256]{2,1,0:T(8,128)(2,1)}, u32[]{:S(2)}, u32[]{:S(2)}) async-start(bf16[16,576,256]{2,1,0:T(8,128)(2,1)} %bitcast.177), calls=%async_computation | async-start | bytes 9437184 | tf_op jit(solution)/shard_map/all_to_all | solution.py:814
  188.7 92.9 %collective-permute-start.9 = (bf16[512,4096]{1,0:T(8,128)(2,1)}, bf16[512,4096]{1,0:T(8,128)(2,1)}, u32[]{:S(2)}, u32[]{:S(2)}) collective-permute-start(bf16[512,4096]{1,0:T(8,128)(2,1)} %dynamic-slice_bitcast_fusion), channel_id=1, source_target_pairs={{0,16},{16,0},{1,17},{17,1},{2,18},{18,2},{3,19},{19,3},{4,20},{20... | collective-permute-start | bytes 12582920 | tf_op jit(solution)/shard_map/ppermute | solution.py:805
  281.7 61.6 %collective-permute-start.10 = (bf16[512,4096]{1,0:T(8,128)(2,1)}, bf16[512,4096]{1,0:T(8,128)(2,1)}, u32[]{:S(2)}, u32[]{:S(2)}) collective-permute-start(bf16[512,4096]{1,0:T(8,128)(2,1)} %collective-permute-done.9.refs_2_), channel_id=1, source_target_pairs={{0,1},{1,0},{2,3},{3,2},{4,5},{5,4},{6,7},{7,6},{8,9},{9,8},{10,11... | collective-permute-start | bytes 12582920 | tf_op jit(solution)/shard_map/ppermute | solution.py:813
  336.4 88.9 %all-to-all-start.1 = ((bf16[4,4,576,256]{3,2,1,0:T(8,128)(2,1)}), bf16[4,4,576,256]{3,2,1,0:T(8,128)(2,1)}, u32[]{:S(2)}, u32[]{:S(2)}) async-start(bf16[4,4,576,256]{3,2,1,0:T(8,128)(2,1)} %copy.117), calls=%async_computation.1 | async-start | bytes 9437184 | tf_op jit(solution)/shard_map/all_to_all | solution.py:824
  341.3 197.1 %all-gather.6.cloned.1.call-start = ((), (), s32[]{:S(2)}) async-start(), calls=%async_computation.6 | async-start | bytes 5898240 | tf_op jit(solution)/shard_map/all_gather | solution.py:823
  342.7 421.8 %reduce-scatter.3.cloned.1.call-start = ((), (), s32[]{:S(2)}) async-start(), calls=%async_computation.8 | async-start | bytes 5406720 | tf_op jit(solution)/shard_map/reduce_scatter | solution.py:849
  393.3 24.0 %copy-start.10 = (bf16[576,1024]{1,0:T(8,128)(2,1)S(1)}, bf16[576,1024]{1,0:T(8,128)(2,1)}, u32[]{:S(2)}) copy-start(bf16[576,1024]{1,0:T(8,128)(2,1)} %get-tuple-element.88.refs_1_.refs_2_) | copy-start | bytes 3538948
  498.9 17.4 %copy-start.6 = (bf16[32,16,1024]{2,1,0:T(8,128)(2,1)}, bf16[32,16,1024]{2,1,0:T(8,128)(2,1)S(1)}, u32[]{:S(2)}) copy-start(bf16[32,16,1024]{2,1,0:T(8,128)(2,1)S(1)} %pad.29.clone) | copy-start | bytes 3145732
  518.5 13.7 %collective-permute-start.11 = (bf16[2,2,2,2,80,1024]{5,4,2,1,0,3:T(8,128)(2,1)}, bf16[2,2,2,2,80,1024]{5,4,2,1,0,3:T(8,128)(2,1)}, u32[]{:S(2)}, u32[]{:S(2)}) collective-permute-start(bf16[2,2,2,2,80,1024]{5,4,2,1,0,3:T(8,128)(2,1)} %dynamic-slice_bitcast_fusion.1), channel_id=1, source_target_pairs={{0,1},{1,0},{2,3},{3,2},{4,5},{5,4},{6,7},{7,6},{8,9},{9,8},{10,11... | collective-permute-start | bytes 7864328 | tf_op jit(solution)/shard_map/ppermute | solution.py:590
  518.8 275.8 %reduce-scatter.5.cloned.1.call-start = ((), (), s32[]{:S(2)}) async-start(), calls=%async_computation.9 | async-start | bytes 9052160 | tf_op jit(solution)/shard_map/reduce_scatter | solution.py:962
  536.4 51.3 %collective-permute-start.12 = (bf16[2,2,2,80,1024]{4,3,2,1,0:T(8,128)(2,1)}, bf16[2,2,2,80,1024]{4,3,2,1,0:T(8,128)(2,1)}, u32[]{:S(2)}, u32[]{:S(2)}) collective-permute-start(bf16[2,2,2,80,1024]{4,3,2,1,0:T(8,128)(2,1)} %dynamic-slice_bitcast_fusion.5), channel_id=1, source_target_pairs={{0,2},{1,3},{2,0},{3,1},{4,6},{5,7},{6,4},{7,5},{8,10},{9,11},{10,... | collective-permute-start | bytes 3932168 | tf_op jit(solution)/shard_map/ppermute | solution.py:590
  600.1 4.5 collective-permute-start.14
  600.1 18.3 %copy-start.9 = (bf16[2,2,2,80,1024]{4,3,2,1,0:T(8,128)(2,1)S(1)}, bf16[2,2,2,80,1024]{4,3,2,1,0:T(8,128)(2,1)}, u32[]{:S(2)}) copy-start(bf16[2,2,2,80,1024]{4,3,2,1,0:T(8,128)(2,1)} %fusion.23) | copy-start | bytes 3932164
  615.5 40.6 %collective-permute-start.15 = (bf16[1,256,2048]{2,1,0:T(8,128)(2,1)S(1)}, bf16[1,256,2048]{2,1,0:T(8,128)(2,1)}, u32[]{:S(2)}, u32[]{:S(2)}) collective-permute-start(bf16[1,256,2048]{2,1,0:T(8,128)(2,1)S(1)} %dynamic-slice_convert_fusion.1), channel_id=1, source_target_pairs={{0,2},{1,3},{2,0},{3,1},{4,6},{5,7},{6,4},{7,5},{8,10},{9,11},{10,... | collective-permute-start | bytes 3145736 | tf_op jit(solution)/shard_map/ppermute | solution.py:887
  619.3 39.0 %collective-permute-start.13 = (bf16[2,2,80,1024]{3,2,1,0:T(8,128)(2,1)}, bf16[2,2,80,1024]{3,2,1,0:T(8,128)(2,1)}, u32[]{:S(2)}, u32[]{:S(2)}) collective-permute-start(bf16[2,2,80,1024]{3,2,1,0:T(8,128)(2,1)} %dynamic-slice_bitcast_fusion.6), channel_id=1, source_target_pairs={{0,16},{1,17},{2,18},{3,19},{4,20},{5,21},{6,22},{7,23},{8,24},{9,... | collective-permute-start | bytes 1966088 | tf_op jit(solution)/shard_map/ppermute | solution.py:590
  642.7 16.9 %copy-start.15 = (bf16[2,2304,256]{2,1,0:T(8,128)(2,1)S(1)}, bf16[2,2304,256]{2,1,0:T(8,128)(2,1)}, u32[]{:S(2)}) copy-start(bf16[2,2304,256]{2,1,0:T(8,128)(2,1)} %get-tuple-element.131) | copy-start | bytes 7077892
  670.1 19.0 %collective-permute-start.17 = (bf16[2,256,2048]{2,1,0:T(8,128)(2,1)}, bf16[2,256,2048]{2,1,0:T(8,128)(2,1)}, u32[]{:S(2)}, u32[]{:S(2)}) collective-permute-start(bf16[2,256,2048]{2,1,0:T(8,128)(2,1)} %fusion.20), channel_id=1, source_target_pairs={{0,1},{1,0},{2,3},{3,2},{4,5},{5,4},{6,7},{7,6},{8,9},{9,8},{10,11... | collective-permute-start | bytes 6291464 | tf_op jit(solution)/shard_map/ppermute | solution.py:878
  672.0 17.1 %slice-start.3 = ((s8[9437184]{0:T(1024)(128)(4,1)}), s8[4194304]{0:T(1024)(128)(4,1)S(1)}, s32[]{:S(2)}) async-start(s8[9437184]{0:T(1024)(128)(4,1)} %bitcast.195), calls=%async_computation.13 | async-start | bytes 8388608
  680.5 39.0 %collective-permute-start.18 = (bf16[256,2048]{1,0:T(8,128)(2,1)S(1)}, bf16[256,2048]{1,0:T(8,128)(2,1)S(1)}, u32[]{:S(2)}, u32[]{:S(2)}) collective-permute-start(bf16[256,2048]{1,0:T(8,128)(2,1)S(1)} %fusion.30), channel_id=1, source_target_pairs={{0,16},{16,0},{1,17},{17,1},{2,18},{18,2},{3,19},{19,3},{4,20},{20... | collective-permute-start | bytes 3145736 | tf_op jit(solution)/shard_map/ppermute | solution.py:542
  681.6 22.0 %slice-start = ((s8[9437184]{0:T(1024)(128)(4,1)}), s8[4194304]{0:T(1024)(128)(4,1)S(1)}, s32[]{:S(2)}) async-start(s8[9437184]{0:T(1024)(128)(4,1)} %bitcast.193), calls=%async_computation.10 | async-start | bytes 8388608
  681.6 22.0 %slice-start.1 = ((s8[9437184]{0:T(1024)(128)(4,1)}), s8[4194304]{0:T(1024)(128)(4,1)S(1)}, s32[]{:S(2)}) async-start(s8[9437184]{0:T(1024)(128)(4,1)} %bitcast.193), calls=%async_computation.11 | async-start | bytes 8388608
  681.7 22.0 %slice-start.2 = ((s8[9437184]{0:T(1024)(128)(4,1)}), s8[1048576]{0:T(1024)(128)(4,1)S(1)}, s32[]{:S(2)}) async-start(s8[9437184]{0:T(1024)(128)(4,1)} %bitcast.193), calls=%async_computation.12 | async-start | bytes 2097152
  681.7 21.9 %collective-permute-start.16 = (bf16[2,80,1024]{2,1,0:T(8,128)(2,1)S(1)}, bf16[2,80,1024]{2,1,0:T(8,128)(2,1)S(1)}, u32[]{:S(2)}, u32[]{:S(2)}) collective-permute-start(bf16[2,80,1024]{2,1,0:T(8,128)(2,1)S(1)} %dynamic-slice_bitcast_fusion.7), channel_id=1, source_target_pairs={{0,8},{1,9},{2,10},{3,11},{4,12},{5,13},{6,14},{7,15},{8,0},{9,1},... | collective-permute-start | bytes 983048 | tf_op jit(solution)/shard_map/ppermute | solution.py:590
  696.3 35.9 %collective-permute-start.19 = (bf16[1,256,2048]{2,1,0:T(8,128)(2,1)S(1)}, bf16[1,256,2048]{2,1,0:T(8,128)(2,1)S(1)}, u32[]{:S(2)}, u32[]{:S(2)}) collective-permute-start(bf16[1,256,2048]{2,1,0:T(8,128)(2,1)S(1)} %dynamic-slice_convert_fusion), channel_id=1, source_target_pairs={{0,2},{1,3},{2,0},{3,1},{4,6},{5,7},{6,4},{7,5},{8,10},{9,11},{10,... | collective-permute-start | bytes 3145736 | tf_op jit(solution)/shard_map/ppermute | solution.py:887
  720.2 30.6 %collective-permute-start.20 = (bf16[80,1024]{1,0:T(8,128)(2,1)}, bf16[80,1024]{1,0:T(8,128)(2,1)}, u32[]{:S(2)}, u32[]{:S(2)}) collective-permute-start(bf16[80,1024]{1,0:T(8,128)(2,1)} %dynamic-slice_bitcast_fusion.8), channel_id=1, source_target_pairs={{0,4},{1,5},{2,6},{3,7},{4,0},{5,1},{6,2},{7,3},{8,12},{9,13},{10,... | collective-permute-start | bytes 491528 | tf_op jit(solution)/shard_map/ppermute | solution.py:590
  732.5 41.1 %collective-permute-start.22 = (bf16[256,2048]{1,0:T(8,128)(2,1)S(1)}, bf16[256,2048]{1,0:T(8,128)(2,1)}, u32[]{:S(2)}, u32[]{:S(2)}) collective-permute-start(bf16[256,2048]{1,0:T(8,128)(2,1)S(1)} %fusion.31), channel_id=1, source_target_pairs={{0,16},{16,0},{1,17},{17,1},{2,18},{18,2},{3,19},{19,3},{4,20},{20... | collective-permute-start | bytes 3145736 | tf_op jit(solution)/shard_map/ppermute | solution.py:542
  759.1 65.9 %all-to-all-start.2 = ((bf16[4,2304,256]{2,1,0:T(8,128)(2,1)}), bf16[4,2304,256]{2,1,0:T(8,128)(2,1)}, u32[]{:S(2)}, u32[]{:S(2)}) async-start(bf16[4,2304,256]{2,1,0:T(8,128)(2,1)} %bitcast.185), calls=%async_computation.2 | async-start | bytes 9437184 | tf_op jit(solution)/shard_map/all_to_all | solution.py:972
  796.9 21.9 %collective-permute-start.21 = (bf16[1040,256]{1,0:T(8,128)(2,1)S(1)}, bf16[1040,256]{1,0:T(8,128)(2,1)S(1)}, u32[]{:S(2)}, u32[]{:S(2)}) collective-permute-start(bf16[1040,256]{1,0:T(8,128)(2,1)S(1)} %concatenate.63), channel_id=1, source_target_pairs={{0,16},{16,0},{1,17},{17,1},{2,18},{18,2},{3,19},{19,3},{4,20},{20... | collective-permute-start | bytes 1597448 | tf_op jit(solution)/shard_map/ppermute | solution.py:547
  802.5 17.1 %copy-start.39 = (f32[2,256]{1,0:T(2,128)S(1)}, f32[2,256]{1,0:T(2,128)}, u32[]{:S(2)}) copy-start(f32[2,256]{1,0:T(2,128)} %param.47) | copy-start | bytes 6148
  802.5 17.7 %copy-start.13 = (f32[1024,256]{1,0:T(8,128)S(1)}, f32[1024,256]{1,0:T(8,128)}, u32[]{:S(2)}) copy-start(f32[1024,256]{1,0:T(8,128)} %param.36) | copy-start | bytes 3145732
  (35 other events, 230.3 us)
Sparse Core Ops, SparseCore 0:
  10.8 88.6 all-gather.7
  100.9 230.5 all-gather.3
  343.7 95.5 all-gather.5
  518.9 149.8 reduce-scatter.2
  672.7 121.8 reduce-scatter.4

commit v3 on v2

--- a/solution.py
+++ b/solution.py
@@ -879,7 +879,10 @@
         return theirs
 
     def mine_work(half, done):
-        mine = project_part(after(d_mine, done), half)
+        d_part = after(d_mine, done)
+        if half == 0:
+            d_part, got["two"] = held((d_part, g_two))
+        mine = project_part(d_part, half)
         got["sum", half] = mine + got["sent", half].astype(jnp.float32)
         spot = lax.axis_index("spot") // 2
         halves = got["sum", half].reshape(inner // 4, 2, columns, -1)
@@ -975,6 +978,7 @@
         .transpose(1, 0, 2, 3)
         .reshape(-1, POOL * POOL, columns)
     )
+    g_two = got["two"]
     g_filters = jnp.stack(
         [g_one[:share], g_one[share : 2 * share], g_two[:share], g_two[share : 2 * share]]
     ).astype(jnp.float32)

time: 842 us -> 823 us (0.977)
  waiting for transfers between devices: 222 us -> 210 us
  starting transfers between devices: 59.9 us -> 49.6 us
    all_to_all x1, waiting for transfers between devices: 0.01 us -> 23.9 us  [shards(): lax.all_to_all(out_line, 'spot', split_axis=0, concat_axis=0, tiled=True)]
    reduce_scatter x1, waiting for transfers between devices: 18.1 us -> 0.01 us  [shards(): lax.psum_scatter(got['expand'], WIDE, scatter_dimension=1, tiled=True)]
    ppermute x2, waiting for transfers between devices: 25.1 us -> 8.16 us  [mine_work(): lax.ppermute(theirs, 'spot', [(i, i ^ 2) for i in range(inner)])]
  transfers between devices with their start and end apart: 31 -> 31, of which waited for: 18 -> 18; matrix products, arithmetic and copies ran while one was open for 27% -> 28% of each run, Pallas kernels for 33% -> 34%
where the time goes in v3:
time: 823 us; the launch traced here: 814 us
  Pallas kernels  276 us (34%)
  waiting for transfers between devices  210 us (26%)
  matrix products  112 us (14%)
  other arithmetic  64.9 us (8%)
  local copies, waits for them, and re-layouts  63.3 us (8%)
  starting transfers between devices  49.6 us (6%)
  between operations  38.2 us (5%)
    pallas_call x2, Pallas kernels, block_backward(): pl.pallas_call(partial(backward_kernel, side), grid=(total // size,), in_...  89.7 us
    pallas_call x2, Pallas kernels, block_forward(): pl.pallas_call(partial(forward_kernel, side), grid=(total // size,), in_s...  83.7 us
    ppermute x1, waiting for transfers between devices, ring_gather(): other = lax.ppermute(held_all, 'dp', [(0, 1), (1, 0)])  47.5 us
    ppermute x7, waiting for transfers between devices, ring_gather(): value = lax.ppermute(value, WIDE, pairs)  47.2 us
    pallas_call x2, Pallas kernels, hidden_forward(): pl.pallas_call(hidden_kernel, grid=(depth // step, LINE), in_specs=[pl.Bl...  45.3 us
    pallas_call x1, Pallas kernels, pre_backward(): pl.pallas_call(partial(pre_kernel, counts), grid_spec=pltpu.PrefetchScala...  41.1 us
    dot_general x4, matrix products, project_part(): lax.dot_general(d_part, got['hidden', half], (((1,), (0,)), ((), ())), pr...  35.3 us
    dot_general x5, matrix products, contract_rows(): lax.dot_general(left, right, (((0,), (0,)), ((), ())), preferred_element_...  34.2 us
  transfers between devices with their start and end apart: 31, of which 18 were waited for; matrix products, arithmetic and copies ran while one was open for 28% of the time, Pallas kernels for 34%

profile of v3, /device:TPU:0, one launch (start us, length us, event | category | flops | bytes accessed | tf_op | source)
XLA Modules:
  0.0 814.3 jit_solution(15882514724364964771)
XLA Ops:
  15.2 4.6 collective-permute-done
  21.9 9.2 %collective-permute-done.1 = bf16[144,1024]{1,0:T(8,128)(2,1)S(1)} collective-permute-done((bf16[144,1024]{1,0:T(8,128)(2,1)S(1)}, bf16[144,1024]{1,0:T(8,128)(2,1)S(1)}, u32[]{:S(2)}, u32[]{:S(2)}) %collective-permute-start.1) | collective-permute-done | bytes 294944 | tf_op jit(solution)/shard_map/ppermute | solution.py:522
  33.8 10.2 %collective-permute-done.2 = bf16[144,1024]{1,0:T(8,128)(2,1)} collective-permute-done((bf16[144,1024]{1,0:T(8,128)(2,1)S(1)}, bf16[144,1024]{1,0:T(8,128)(2,1)}, u32[]{:S(2)}, u32[]{:S(2)}) %collective-permute-start.2) | collective-permute-done | bytes 294944 | tf_op jit(solution)/shard_map/ppermute | solution.py:522
  75.1 3.6 collective-permute-start.4
  78.7 10.6 %collective-permute-done.4 = bf16[144,1024]{1,0:T(8,128)(2,1)S(1)} collective-permute-done((bf16[144,1024]{1,0:T(8,128)(2,1)}, bf16[144,1024]{1,0:T(8,128)(2,1)S(1)}, u32[]{:S(2)}, u32[]{:S(2)}) %collective-permute-start.4) | collective-permute-done | bytes 294944 | tf_op jit(solution)/shard_map/ppermute | solution.py:522
  89.4 6.0 collective-permute-start.5
  102.1 6.0 collective-permute-done.6
  109.7 47.5 %collective-permute-done.7 = bf16[8,144,1024]{2,1,0:T(8,128)(2,1)} collective-permute-done((bf16[8,144,1024]{2,1,0:T(8,128)(2,1)S(1)}, bf16[8,144,1024]{2,1,0:T(8,128)(2,1)}, u32[]{:S(2)}, u32[]{:S(2)}) %collective-permute-start.7) | collective-permute-done | bytes 2359328 | tf_op jit(solution)/shard_map/ppermute | solution.py:528
  162.9 4.6 all-to-all-start
  167.7 5.4 collective-permute-done.8
  173.1 3.4 select_bitcast_fusion
  180.3 3.6 pad_maximum_fusion.3
  183.9 4.8 dynamic-slice_bitcast_fusion
  195.8 63.5 %block_forward_24.1 = (f32[2304,1024]{1,0:T(8,128)}, f32[2304,1024]{1,0:T(8,128)}, f32[2304,1024]{1,0:T(8,128)}, f32[2304,128]{1,0:T(8,128)}, f32[2304,128]{1,0:...) custom-call(bf16[2304,1024]{1,0:T(8,128)(2,1)} %bitcast.190, ...), custom_call_target="tpu_custom_call" | custom-call | tf_op jit(solution)/shard_map/block_forward_24/pallas_call | solution.py:412
  260.2 20.2 %block_forward_12.1 = (f32[576,1024]{1,0:T(8,128)}, f32[576,1024]{1,0:T(8,128)}, f32[576,1024]{1,0:T(8,128)}, f32[576,128]{1,0:T(8,128)}, f32[576,128]{1,0:T(8,1...) custom-call(f32[4]{0:T(128)} %compare_convert_fusion.refs_0_, ...), custom_call_target="tpu_custom_call" | custom-call | tf_op jit(solution)/shard_map/block_forward_12/pallas_call | solution.py:412
  281.6 4.1 convert_reduce_fusion
  285.7 15.9 %all-to-all-done = bf16[16,576,256]{2,1,0:T(8,128)(2,1)} async-done(((bf16[16,576,256]{2,1,0:T(8,128)(2,1)}), bf16[16,576,256]{2,1,0:T(8,128)(2,1)}, u32[]{:S(2)}, u32[]{:S(2)}) %all-to-all-start) | async-done | bytes 4718624 | tf_op jit(solution)/shard_map/all_to_all | solution.py:814
  301.6 5.2 copy.149
  306.8 24.9 %all-gather.4.cloned.1.call-done.refs_0_.refs_4_.expand_ref = bf16[3072,4096]{1,0:T(8,128)(2,1)} async-done(((bf16[3072,256]{1,0:T(8,128)(2,1)}), bf16[3072,4096]{1,0:T(8,128)(2,1)}) %all-gather.4.cloned.1.call-update) | async-done | bytes 25165840 | tf_op jit(solution)/shard_map/all_gather | solution.py:803
  332.6 4.9 copy.117
  337.6 4.9 all-to-all-start.1
  343.9 41.1 %pre_backward.1 = bf16[576,4096]{1,0:T(8,128)(2,1)} custom-call(s32[8]{0:T(128)} %pad_add_fusion.at_ref, bf16[576,4096]{1,0:T(8,128)(2,1)} %bitcast.184, bf16[576,1024]{1,0:T(8,128)(2,1)} %get-tuple-element.122.tokens_ref, bf16[3072,4096]{1,0:T(8,128)(2,1)} %all-gather.4.cloned.1.call-done.refs_0_.refs_4_.expand_ref, ...), custom_call_target="tpu_custom_call" | custom-call | tf_op jit(solution)/shard_map/pre_backward/pallas_call | solution.py:699
  385.0 9.9 %fusion.9.refs_1_ = f32[576,1024]{1,0:T(8,128)} fusion(bf16[576,4096]{1,0:T(8,128)(2,1)} %pre_backward.1, bf16[3072,4096]{1,0:T(8,128)(2,1)} %all-gather.4.cloned.1.call-done.refs_0_.refs_4_.expand_ref), kind=kOutput, calls=%fused_computation.25 | convolution fusion | flops 4831838208 | bytes 15466496 | tf_op jit(solution)/shard_map/dot_general | solution.py:35
  394.9 22.4 %block_backward_12.1 = (f32[576,1024]{1,0:T(8,128)}, bf16[576,1024]{1,0:T(8,128)(2,1)}, bf16[576,1024]{1,0:T(8,128)(2,1)}, f32[128,1024]{1,0:T(8,128)}) custom-call(f32[4]{0:T(128)} %compare_convert_fusion.refs_0_, f32[576,1024]{1,0:T(8,128)} %fusion.9.refs_1_, bf16[576,1024]{1,0:T(8,128)(2,1)} %get-tuple-element.90.refs_1_.refs_2_, ...), custom_call_target="tpu_custom_call" | custom-call | tf_op jit(solution)/shard_map/block_backward_12/pallas_call | solution.py:448
  426.9 4.9 dynamic-slice_bitcast_fusion.2
  431.8 67.3 %block_backward_24.1 = (bf16[2304,1024]{1,0:T(8,128)(2,1)}, bf16[2304,1024]{1,0:T(8,128)(2,1)}, bf16[2304,1024]{1,0:T(8,128)(2,1)}, f32[128,1024]{1,0:T(8,128)}) custom-call(bf16[576,144]{1,0:T(8,128)(2,1)} %select_convert_fusion.refs_0_, f32[576,1024]{1,0:T(8,128)} %get-tuple-element.111.refs_1_, bf16[2304,1024]{1,0:T(8,128)(2,1)} %bitcast.191, ...), custom_call_target="tpu_custom_call" | custom-call | tf_op jit(solution)/shard_map/block_backward_24/pallas_call | solution.py:448
  499.1 8.4 %convolution_convert_fusion.1 = bf16[1024,1024]{1,0:T(8,128)(2,1)S(1)} fusion(bf16[2304,1024]{1,0:T(8,128)(2,1)} %get-tuple-element.119, bf16[2304,1024]{1,0:T(8,128)(2,1)} %get-tuple-element.120), kind=kOutput, calls=%fused_computation.67 | convolution fusion | flops 4832886784 | bytes 11534336 | tf_op jit(solution)/shard_map/dot_general | solution.py:29
  508.2 8.8 %convolution_convert_fusion.2 = bf16[1024,1024]{0,1:T(8,128)(2,1)S(1)} fusion(bf16[2304,1024]{1,0:T(8,128)(2,1)} %get-tuple-element.118, bf16[2304,1024]{1,0:T(8,128)(2,1)} %bitcast.192), kind=kOutput, calls=%fused_computation.68 | convolution fusion | flops 4832886784 | bytes 11534336 | tf_op jit(solution)/shard_map/dot_general | solution.py:29
  520.1 11.8 %convolution_convert_fusion = bf16[1040,4096]{1,0:T(8,128)(2,1)} fusion(bf16[576,1040]{1,0:T(8,128)(2,1)S(1)} %concatenate.59, bf16[576,4096]{1,0:T(8,128)(2,1)} %pre_backward.1), kind=kOutput, calls=%fused_computation | convolution fusion | flops 4911595520 | bytes 14436352 | tf_op jit(solution)/shard_map/dot_general | solution.py:29
  531.8 3.5 fusion.12
  538.3 22.1 %hidden_forward.2 = bf16[2304,2048]{1,0:T(8,128)(2,1)} custom-call(bf16[2304,1024]{1,0:T(8,128)(2,1)} %all-gather.6.cloned.1.call-done.tokens_ref, bf16[3072,4096]{1,0:T(8,128)(2,1)} %all-gather.4.cloned.1.call-done.refs_0_.refs_4_.expand_ref, f32[1,4096]{1,0:T(1,128)} %bitcast.222), custom_call_target="tpu_custom_call" | custom-call | tf_op jit(solution)/shard_map/hidden_forward/pallas_call | solution.py:620
  560.4 22.4 %collective-permute-done.12 = bf16[2,2,2,80,1024]{4,3,2,1,0:T(8,128)(2,1)} collective-permute-done((bf16[2,2,2,80,1024]{4,3,2,1,0:T(8,128)(2,1)}, bf16[2,2,2,80,1024]{4,3,2,1,0:T(8,128)(2,1)}, u32[]{:S(2)}, u32[]{:S(2)}) %collective-permute-start.12) | collective-permute-done | bytes 1310752 | tf_op jit(solution)/shard_map/ppermute | solution.py:590
  585.7 9.3 %fusion.17 = bf16[2,256,2048]{2,1,0:T(8,128)(2,1)} fusion(bf16[2,2304,256]{2,1,0:T(8,128)(2,1)} %get-tuple-element.135, bf16[2304,2048]{1,0:T(8,128)(2,1)} %hidden_forward.2), kind=kOutput, calls=%fused_computation.45 | convolution fusion | flops 4832886784 | bytes 13893632 | tf_op jit(solution)/shard_map/dot_general | solution.py:869
  595.1 4.4 collective-permute-done.14
  599.5 8.7 %convert_add_fusion.2 = f32[2,256,2048]{2,1,0:T(8,128)S(1)} fusion(bf16[2,256,2048]{2,1,0:T(8,128)(2,1)} %collective-permute-done.14, bf16[2,2304,256]{2,1,0:T(8,128)(2,1)} %get-tuple-element.136, bf16[2304,2048]{1,0:T(8,128)(2,1)} %hidden_forward.2), kind=kOutput, calls=%fused_computation.43 | convolution fusion | flops 4833935360 | bytes 18087936 | tf_op jit(solution)/shard_map/dot_general | solution.py:869
  612.8 23.1 %hidden_forward.3 = bf16[2304,2048]{1,0:T(8,128)(2,1)} custom-call(bf16[2304,1024]{1,0:T(8,128)(2,1)} %all-gather.6.cloned.1.call-done.tokens_ref, bf16[3072,4096]{1,0:T(8,128)(2,1)} %all-gather.4.cloned.1.call-done.refs_0_.refs_4_.expand_ref, f32[1,4096]{1,0:T(1,128)} %bitcast.223), custom_call_target="tpu_custom_call" | custom-call | tf_op jit(solution)/shard_map/hidden_forward/pallas_call | solution.py:620
  641.6 10.1 %fusion.20 = bf16[2,256,2048]{2,1,0:T(8,128)(2,1)} fusion(bf16[2,2304,256]{2,1,0:T(8,128)(2,1)S(1)} %copy-done.15, bf16[2304,2048]{1,0:T(8,128)(2,1)} %hidden_forward.3), kind=kOutput, calls=%fused_computation.46 | convolution fusion | flops 4832886784 | bytes 13893632 | tf_op jit(solution)/shard_map/dot_general | solution.py:869
  657.5 4.6 fusion.15
  665.0 7.2 convert_add_fusion.1
  674.6 8.9 %collective-permute-done.16 = bf16[2,80,1024]{2,1,0:T(8,128)(2,1)S(1)} collective-permute-done((bf16[2,80,1024]{2,1,0:T(8,128)(2,1)S(1)}, bf16[2,80,1024]{2,1,0:T(8,128)(2,1)S(1)}, u32[]{:S(2)}, u32[]{:S(2)}) %collective-permute-start.16) | collective-permute-done | bytes 327712 | tf_op jit(solution)/shard_map/ppermute | solution.py:590
  683.7 15.3 %convolution_add_fusion = f32[2304,1024]{0,1:T(8,128)} fusion(bf16[2304,2048]{1,0:T(8,128)(2,1)S(1)} %bitcast.198, f32[1024]{0:T(1024)S(1)} %bitcast.230, bf16[3072,4096]{1,0:T(8,128)(2,1)} %all-gather.4.cloned.1.call-done.refs_0_.refs_4_.expand_ref, s32[]{:T(128)S(6)} %select_n.521), kind=kOutput, calls=%fused_computation.27 | convolution fusion | flops 9666035712 | bytes 23072772 | tf_op jit(solution)/shard_map/dot_general | solution.py:947
  700.1 6.1 collective-permute-done.19
  709.1 17.5 %add_convert_fusion = bf16[2304,1024]{0,1:T(8,128)(2,1)} fusion(f32[2304,1024]{0,1:T(8,128)} %convolution_add_fusion, bf16[2304,2048]{1,0:T(8,128)(2,1)} %hidden_forward.3, bf16[2048,1024]{1,0:T(8,128)(2,1)} %bitcast.211), kind=kOutput, calls=%fused_computation.19 | convolution fusion | flops 9668395008 | bytes 27787264 | tf_op jit(solution)/shard_map/dot_general | solution.py:947
  737.0 6.6 copy.127
  743.6 5.1 all-to-all-start.2
  762.5 16.2 %adamw_turned.1 = (f32[4096,256]{1,0:T(8,128)}, f32[4096,256]{1,0:T(8,128)}, f32[4096,256]{1,0:T(8,128)}, f32[4096,256]{1,0:T(8,128)}, bf16[4096,256]{1,0:T(8,128)(2,1)}) custom-call(f32[256,4096]{1,0:T(8,128)} %pad_maximum_fusion.2.grad_ref, f32[4096,256]{1,0:T(8,128)} %refs_0_.1, f32[4096,256]{1,0:T(8,128)} %refs_1_.1, f32[4096,256]{1,0:T(8,128)} %refs_2_.1, ...), custom_call_target="tpu_custom_call" | custom-call | tf_op jit(solution)/shard_map/adamw_turned/pallas_call | solution.py:646
  778.7 23.9 %all-to-all-done.2 = bf16[4,2304,256]{2,1,0:T(8,128)(2,1)} async-done(((bf16[4,2304,256]{2,1,0:T(8,128)(2,1)}), bf16[4,2304,256]{2,1,0:T(8,128)(2,1)}, u32[]{:S(2)}, u32[]{:S(2)}) %all-to-all-start.2) | async-done | bytes 4718624 | tf_op jit(solution)/shard_map/all_to_all | solution.py:975
  802.6 4.9 copy.128
  (271 shorter events, 118.3 us)
Async XLA Ops:
  7.2 176.7 %all-gather.8.cloned.1.call-start = ((), (), s32[]{:S(2)}) async-start(), calls=%async_computation.7 | async-start | bytes 8912896 | tf_op jit(solution)/shard_map/all_gather | solution.py:802
  7.3 26.4 %copy-start.12 = (f32[1024,256]{1,0:T(8,128)S(1)}, f32[1024,256]{1,0:T(8,128)}, u32[]{:S(2)}) copy-start(f32[1024,256]{1,0:T(8,128)} %param.36) | copy-start | bytes 3145732
  10.6 321.0 %all-gather.4.cloned.1.call-start = ((), (), s32[]{:S(2)}) async-start(), calls=%async_computation.5 | async-start | bytes 26738688 | tf_op jit(solution)/shard_map/all_gather | solution.py:803
  12.1 39.1 %copy-start.45 = (s32[8]{0:T(128)S(1)}, s32[8]{0:T(128)}, u32[]{:S(2)}) copy-start(s32[8]{0:T(128)} %constant.441.clone) | copy-start | bytes 100
  12.1 46.4 %copy-start.35 = (s32[8]{0:T(128)S(1)}, s32[8]{0:T(128)}, u32[]{:S(2)}) copy-start(s32[8]{0:T(128)} %constant.442.clone) | copy-start | bytes 100
  12.1 7.7 collective-permute-start
  19.8 11.4 %copy-start.26 = (bf16[144,1024]{1,0:T(8,128)(2,1)}, bf16[144,1024]{1,0:T(8,128)(2,1)S(1)}, u32[]{:S(2)}) copy-start(bf16[144,1024]{1,0:T(8,128)(2,1)S(1)} %collective-permute-done) | copy-start | bytes 884740
  19.8 11.3 %collective-permute-start.1 = (bf16[144,1024]{1,0:T(8,128)(2,1)S(1)}, bf16[144,1024]{1,0:T(8,128)(2,1)S(1)}, u32[]{:S(2)}, u32[]{:S(2)}) collective-permute-start(bf16[144,1024]{1,0:T(8,128)(2,1)S(1)} %collective-permute-done), channel_id=1, source_target_pairs={{0,4},{1,3},{4,8},{5,1},{8,12},{9,5},{12,14},{13,9},{14,10},{15,13... | collective-permute-start | bytes 884744 | tf_op jit(solution)/shard_map/ppermute | solution.py:522
  31.2 12.8 %collective-permute-start.2 = (bf16[144,1024]{1,0:T(8,128)(2,1)S(1)}, bf16[144,1024]{1,0:T(8,128)(2,1)}, u32[]{:S(2)}, u32[]{:S(2)}) collective-permute-start(bf16[144,1024]{1,0:T(8,128)(2,1)S(1)} %collective-permute-done.1), channel_id=1, source_target_pairs={{0,4},{1,3},{4,8},{5,1},{8,12},{9,5},{12,14},{13,9},{14,10},{15,13... | collective-permute-start | bytes 884744 | tf_op jit(solution)/shard_map/ppermute | solution.py:522
  33.8 44.9 %copy-start.27 = (bf16[144,1024]{1,0:T(8,128)(2,1)S(1)}, bf16[144,1024]{1,0:T(8,128)(2,1)}, u32[]{:S(2)}) copy-start(bf16[144,1024]{1,0:T(8,128)(2,1)} %copy-done.26) | copy-start | bytes 884740
  44.0 34.7 %copy-start.29 = (bf16[144,1024]{1,0:T(8,128)(2,1)S(1)}, bf16[144,1024]{1,0:T(8,128)(2,1)}, u32[]{:S(2)}) copy-start(bf16[144,1024]{1,0:T(8,128)(2,1)} %copy-done.28) | copy-start | bytes 884740
  44.0 7.1 collective-permute-start.3
  51.2 22.8 %copy-start.30 = (bf16[144,1024]{1,0:T(8,128)(2,1)}, bf16[144,1024]{1,0:T(8,128)(2,1)S(1)}, u32[]{:S(2)}) copy-start(bf16[144,1024]{1,0:T(8,128)(2,1)S(1)} %collective-permute-done.3) | copy-start | bytes 884740
  74.7 21.7 %copy-start.31 = (bf16[144,1024]{1,0:T(8,128)(2,1)S(1)}, bf16[144,1024]{1,0:T(8,128)(2,1)}, u32[]{:S(2)}) copy-start(bf16[144,1024]{1,0:T(8,128)(2,1)} %copy-done.30) | copy-start | bytes 884740
  75.1 14.3 %collective-permute-start.4 = (bf16[144,1024]{1,0:T(8,128)(2,1)}, bf16[144,1024]{1,0:T(8,128)(2,1)S(1)}, u32[]{:S(2)}, u32[]{:S(2)}) collective-permute-start(bf16[144,1024]{1,0:T(8,128)(2,1)} %copy-done.30), channel_id=1, source_target_pairs={{0,4},{1,3},{4,8},{5,1},{8,12},{9,5},{12,14},{13,9},{14,10},{15,13... | collective-permute-start | bytes 884744 | tf_op jit(solution)/shard_map/ppermute | solution.py:522
  89.4 10.2 %collective-permute-start.5 = (bf16[144,1024]{1,0:T(8,128)(2,1)S(1)}, bf16[144,1024]{1,0:T(8,128)(2,1)S(1)}, u32[]{:S(2)}, u32[]{:S(2)}) collective-permute-start(bf16[144,1024]{1,0:T(8,128)(2,1)S(1)} %collective-permute-done.4), channel_id=1, source_target_pairs={{0,4},{1,3},{4,8},{5,1},{8,12},{9,5},{12,14},{13,9},{14,10},{15,13... | collective-permute-start | bytes 884744 | tf_op jit(solution)/shard_map/ppermute | solution.py:522
  99.6 8.5 %collective-permute-start.6 = (bf16[144,1024]{1,0:T(8,128)(2,1)S(1)}, bf16[144,1024]{1,0:T(8,128)(2,1)S(1)}, u32[]{:S(2)}, u32[]{:S(2)}) collective-permute-start(bf16[144,1024]{1,0:T(8,128)(2,1)S(1)} %collective-permute-done.5), channel_id=1, source_target_pairs={{0,4},{1,3},{4,8},{5,1},{8,12},{9,5},{12,14},{13,9},{14,10},{15,13... | collective-permute-start | bytes 884744 | tf_op jit(solution)/shard_map/ppermute | solution.py:522
  108.1 49.1 %collective-permute-start.7 = (bf16[8,144,1024]{2,1,0:T(8,128)(2,1)S(1)}, bf16[8,144,1024]{2,1,0:T(8,128)(2,1)}, u32[]{:S(2)}, u32[]{:S(2)}) collective-permute-start(bf16[8,144,1024]{2,1,0:T(8,128)(2,1)S(1)} %bitcast_dynamic-update-slice_fusion), channel_id=1, source_target_pairs={{0,16},{16,0},{1,17},{17,1},{2,18},{18,2},{3,19},{19,3},{4,20},{20... | collective-permute-start | bytes 7077896 | tf_op jit(solution)/shard_map/ppermute | solution.py:528
  162.9 10.3 %collective-permute-start.8 = (bf16[2,8,144,1024]{3,2,1,0:T(8,128)(2,1)}, bf16[2,8,144,1024]{3,2,1,0:T(8,128)(2,1)}, u32[]{:S(2)}, u32[]{:S(2)}) collective-permute-start(bf16[2,8,144,1024]{3,2,1,0:T(8,128)(2,1)} %pad_maximum_fusion.1), channel_id=1, source_target_pairs={{0,1},{1,0},{2,3},{3,2},{4,5},{5,4},{6,7},{7,6},{8,9},{9,8},{10,11... | collective-permute-start | bytes 14155784 | tf_op jit(solution)/shard_map/ppermute | solution.py:535
  162.9 138.7 %all-to-all-start = ((bf16[16,576,256]{2,1,0:T(8,128)(2,1)}), bf16[16,576,256]{2,1,0:T(8,128)(2,1)}, u32[]{:S(2)}, u32[]{:S(2)}) async-start(bf16[16,576,256]{2,1,0:T(8,128)(2,1)} %bitcast.181), calls=%async_computation | async-start | bytes 9437184 | tf_op jit(solution)/shard_map/all_to_all | solution.py:814
  167.5 370.8 %all-gather.6.cloned.1.call-start = ((), (), s32[]{:S(2)}) async-start(), calls=%async_computation.6 | async-start | bytes 5898240 | tf_op jit(solution)/shard_map/all_gather | solution.py:823
  188.7 92.9 %collective-permute-start.9 = (bf16[512,4096]{1,0:T(8,128)(2,1)}, bf16[512,4096]{1,0:T(8,128)(2,1)}, u32[]{:S(2)}, u32[]{:S(2)}) collective-permute-start(bf16[512,4096]{1,0:T(8,128)(2,1)} %dynamic-slice_bitcast_fusion), channel_id=1, source_target_pairs={{0,16},{16,0},{1,17},{17,1},{2,18},{18,2},{3,19},{19,3},{4,20},{20... | collective-permute-start | bytes 12582920 | tf_op jit(solution)/shard_map/ppermute | solution.py:805
  281.6 62.2 %collective-permute-start.10 = (bf16[512,4096]{1,0:T(8,128)(2,1)}, bf16[512,4096]{1,0:T(8,128)(2,1)}, u32[]{:S(2)}, u32[]{:S(2)}) collective-permute-start(bf16[512,4096]{1,0:T(8,128)(2,1)} %collective-permute-done.9.refs_2_), channel_id=1, source_target_pairs={{0,1},{1,0},{2,3},{3,2},{4,5},{5,4},{6,7},{7,6},{8,9},{9,8},{10,11... | collective-permute-start | bytes 12582920 | tf_op jit(solution)/shard_map/ppermute | solution.py:813
  337.6 89.3 %all-to-all-start.1 = ((bf16[4,4,576,256]{3,2,1,0:T(8,128)(2,1)}), bf16[4,4,576,256]{3,2,1,0:T(8,128)(2,1)}, u32[]{:S(2)}, u32[]{:S(2)}) async-start(bf16[4,4,576,256]{3,2,1,0:T(8,128)(2,1)} %copy.117), calls=%async_computation.1 | async-start | bytes 9437184 | tf_op jit(solution)/shard_map/all_to_all | solution.py:824
  342.5 252.6 %reduce-scatter.3.cloned.1.call-start = ((), (), s32[]{:S(2)}) async-start(), calls=%async_computation.8 | async-start | bytes 5406720 | tf_op jit(solution)/shard_map/reduce_scatter | solution.py:849
  394.9 23.9 %copy-start.10 = (bf16[576,1024]{1,0:T(8,128)(2,1)S(1)}, bf16[576,1024]{1,0:T(8,128)(2,1)}, u32[]{:S(2)}) copy-start(bf16[576,1024]{1,0:T(8,128)(2,1)} %get-tuple-element.90.refs_1_.refs_2_) | copy-start | bytes 3538948
  431.8 294.8 %reduce-scatter.5.cloned.1.call-start = ((), (), s32[]{:S(2)}) async-start(), calls=%async_computation.9 | async-start | bytes 9052160 | tf_op jit(solution)/shard_map/reduce_scatter | solution.py:965
  507.6 9.5 %copy-start.7 = (bf16[1024,1024]{1,0:T(8,128)(2,1)}, bf16[1024,1024]{1,0:T(8,128)(2,1)S(1)}, u32[]{:S(2)}) copy-start(bf16[1024,1024]{1,0:T(8,128)(2,1)S(1)} %convolution_convert_fusion.1) | copy-start | bytes 6291460
  508.2 8.9 %copy-start.6 = (bf16[32,16,1024]{2,1,0:T(8,128)(2,1)}, bf16[32,16,1024]{2,1,0:T(8,128)(2,1)S(1)}, u32[]{:S(2)}) copy-start(bf16[32,16,1024]{2,1,0:T(8,128)(2,1)S(1)} %pad.29.clone) | copy-start | bytes 3145732
  519.2 12.6 %collective-permute-start.11 = (bf16[2,2,2,2,80,1024]{5,4,2,1,0,3:T(8,128)(2,1)}, bf16[2,2,2,2,80,1024]{5,4,2,1,0,3:T(8,128)(2,1)}, u32[]{:S(2)}, u32[]{:S(2)}) collective-permute-start(bf16[2,2,2,2,80,1024]{5,4,2,1,0,3:T(8,128)(2,1)} %dynamic-slice_bitcast_fusion.1), channel_id=1, source_target_pairs={{0,1},{1,0},{2,3},{3,2},{4,5},{5,4},{6,7},{7,6},{8,9},{9,8},{10,11... | collective-permute-start | bytes 7864328 | tf_op jit(solution)/shard_map/ppermute | solution.py:590
  536.5 46.3 %collective-permute-start.12 = (bf16[2,2,2,80,1024]{4,3,2,1,0:T(8,128)(2,1)}, bf16[2,2,2,80,1024]{4,3,2,1,0:T(8,128)(2,1)}, u32[]{:S(2)}, u32[]{:S(2)}) collective-permute-start(bf16[2,2,2,80,1024]{4,3,2,1,0:T(8,128)(2,1)} %dynamic-slice_bitcast_fusion.5), channel_id=1, source_target_pairs={{0,2},{1,3},{2,0},{3,1},{4,6},{5,7},{6,4},{7,5},{8,10},{9,11},{10,... | collective-permute-start | bytes 3932168 | tf_op jit(solution)/shard_map/ppermute | solution.py:590
  595.0 4.5 collective-permute-start.14
  595.1 15.4 %copy-start.9 = (bf16[2,2,2,80,1024]{4,3,2,1,0:T(8,128)(2,1)S(1)}, bf16[2,2,2,80,1024]{4,3,2,1,0:T(8,128)(2,1)}, u32[]{:S(2)}) copy-start(bf16[2,2,2,80,1024]{4,3,2,1,0:T(8,128)(2,1)} %fusion.23) | copy-start | bytes 3932164
  610.4 27.6 %collective-permute-start.15 = (bf16[1,256,2048]{2,1,0:T(8,128)(2,1)S(1)}, bf16[1,256,2048]{2,1,0:T(8,128)(2,1)}, u32[]{:S(2)}, u32[]{:S(2)}) collective-permute-start(bf16[1,256,2048]{2,1,0:T(8,128)(2,1)S(1)} %dynamic-slice_convert_fusion.1), channel_id=1, source_target_pairs={{0,2},{1,3},{2,0},{3,1},{4,6},{5,7},{6,4},{7,5},{8,10},{9,11},{10,... | collective-permute-start | bytes 3145736 | tf_op jit(solution)/shard_map/ppermute | solution.py:890
  611.4 28.9 %collective-permute-start.13 = (bf16[2,2,80,1024]{3,2,1,0:T(8,128)(2,1)}, bf16[2,2,80,1024]{3,2,1,0:T(8,128)(2,1)}, u32[]{:S(2)}, u32[]{:S(2)}) collective-permute-start(bf16[2,2,80,1024]{3,2,1,0:T(8,128)(2,1)} %dynamic-slice_bitcast_fusion.6), channel_id=1, source_target_pairs={{0,16},{1,17},{2,18},{3,19},{4,20},{5,21},{6,22},{7,23},{8,24},{9,... | collective-permute-start | bytes 1966088 | tf_op jit(solution)/shard_map/ppermute | solution.py:590
  651.7 13.3 %collective-permute-start.17 = (bf16[2,256,2048]{2,1,0:T(8,128)(2,1)}, bf16[2,256,2048]{2,1,0:T(8,128)(2,1)}, u32[]{:S(2)}, u32[]{:S(2)}) collective-permute-start(bf16[2,256,2048]{2,1,0:T(8,128)(2,1)} %fusion.20), channel_id=1, source_target_pairs={{0,1},{1,0},{2,3},{3,2},{4,5},{5,4},{6,7},{7,6},{8,9},{9,8},{10,11... | collective-permute-start | bytes 6291464 | tf_op jit(solution)/shard_map/ppermute | solution.py:878
  653.4 11.6 %slice-start.3 = ((s8[9437184]{0:T(1024)(128)(4,1)}), s8[4194304]{0:T(1024)(128)(4,1)S(1)}, s32[]{:S(2)}) async-start(s8[9437184]{0:T(1024)(128)(4,1)} %bitcast.199), calls=%async_computation.13 | async-start | bytes 8388608
  663.3 35.8 %collective-permute-start.18 = (bf16[256,2048]{1,0:T(8,128)(2,1)S(1)}, bf16[256,2048]{1,0:T(8,128)(2,1)S(1)}, u32[]{:S(2)}, u32[]{:S(2)}) collective-permute-start(bf16[256,2048]{1,0:T(8,128)(2,1)S(1)} %fusion.30), channel_id=1, source_target_pairs={{0,16},{16,0},{1,17},{17,1},{2,18},{18,2},{3,19},{19,3},{4,20},{20... | collective-permute-start | bytes 3145736 | tf_op jit(solution)/shard_map/ppermute | solution.py:542
  664.7 19.0 %slice-start = ((s8[9437184]{0:T(1024)(128)(4,1)}), s8[4194304]{0:T(1024)(128)(4,1)S(1)}, s32[]{:S(2)}) async-start(s8[9437184]{0:T(1024)(128)(4,1)} %bitcast.197), calls=%async_computation.10 | async-start | bytes 8388608
  664.7 19.0 %slice-start.1 = ((s8[9437184]{0:T(1024)(128)(4,1)}), s8[4194304]{0:T(1024)(128)(4,1)S(1)}, s32[]{:S(2)}) async-start(s8[9437184]{0:T(1024)(128)(4,1)} %bitcast.197), calls=%async_computation.11 | async-start | bytes 8388608
  664.7 19.0 %slice-start.2 = ((s8[9437184]{0:T(1024)(128)(4,1)}), s8[1048576]{0:T(1024)(128)(4,1)S(1)}, s32[]{:S(2)}) async-start(s8[9437184]{0:T(1024)(128)(4,1)} %bitcast.197), calls=%async_computation.12 | async-start | bytes 2097152
  664.7 18.8 %collective-permute-start.16 = (bf16[2,80,1024]{2,1,0:T(8,128)(2,1)S(1)}, bf16[2,80,1024]{2,1,0:T(8,128)(2,1)S(1)}, u32[]{:S(2)}, u32[]{:S(2)}) collective-permute-start(bf16[2,80,1024]{2,1,0:T(8,128)(2,1)S(1)} %dynamic-slice_bitcast_fusion.7), channel_id=1, source_target_pairs={{0,8},{1,9},{2,10},{3,11},{4,12},{5,13},{6,14},{7,15},{8,0},{9,1},... | collective-permute-start | bytes 983048 | tf_op jit(solution)/shard_map/ppermute | solution.py:590
  672.4 33.8 %collective-permute-start.19 = (bf16[1,256,2048]{2,1,0:T(8,128)(2,1)S(1)}, bf16[1,256,2048]{2,1,0:T(8,128)(2,1)S(1)}, u32[]{:S(2)}, u32[]{:S(2)}) collective-permute-start(bf16[1,256,2048]{2,1,0:T(8,128)(2,1)S(1)} %dynamic-slice_convert_fusion), channel_id=1, source_target_pairs={{0,2},{1,3},{2,0},{3,1},{4,6},{5,7},{6,4},{7,5},{8,10},{9,11},{10,... | collective-permute-start | bytes 3145736 | tf_op jit(solution)/shard_map/ppermute | solution.py:890
  699.7 31.6 %collective-permute-start.20 = (bf16[80,1024]{1,0:T(8,128)(2,1)}, bf16[80,1024]{1,0:T(8,128)(2,1)}, u32[]{:S(2)}, u32[]{:S(2)}) collective-permute-start(bf16[80,1024]{1,0:T(8,128)(2,1)} %dynamic-slice_bitcast_fusion.8), channel_id=1, source_target_pairs={{0,4},{1,5},{2,6},{3,7},{4,0},{5,1},{6,2},{7,3},{8,12},{9,13},{10,... | collective-permute-start | bytes 491528 | tf_op jit(solution)/shard_map/ppermute | solution.py:590
  707.5 50.7 %collective-permute-start.22 = (bf16[256,2048]{1,0:T(8,128)(2,1)}, bf16[256,2048]{1,0:T(8,128)(2,1)}, u32[]{:S(2)}, u32[]{:S(2)}) collective-permute-start(bf16[256,2048]{1,0:T(8,128)(2,1)} %fusion.31), channel_id=1, source_target_pairs={{0,16},{16,0},{1,17},{17,1},{2,18},{18,2},{3,19},{19,3},{4,20},{20... | collective-permute-start | bytes 3145736 | tf_op jit(solution)/shard_map/ppermute | solution.py:542
  730.8 21.7 %collective-permute-start.21 = (bf16[1040,256]{1,0:T(8,128)(2,1)S(1)}, bf16[1040,256]{1,0:T(8,128)(2,1)}, u32[]{:S(2)}, u32[]{:S(2)}) collective-permute-start(bf16[1040,256]{1,0:T(8,128)(2,1)S(1)} %concatenate.63), channel_id=1, source_target_pairs={{0,16},{16,0},{1,17},{17,1},{2,18},{18,2},{3,19},{19,3},{4,20},{20... | collective-permute-start | bytes 1597448 | tf_op jit(solution)/shard_map/ppermute | solution.py:547
  732.3 11.3 %copy-start.22 = (bf16[80,1024]{1,0:T(8,128)(2,1)}, bf16[80,1024]{1,0:T(8,128)(2,1)S(1)}, u32[]{:S(2)}) copy-start(bf16[80,1024]{1,0:T(8,128)(2,1)S(1)} %fusion.38) | copy-start | bytes 491524
  743.6 58.9 %all-to-all-start.2 = ((bf16[4,2304,256]{2,1,0:T(8,128)(2,1)}), bf16[4,2304,256]{2,1,0:T(8,128)(2,1)}, u32[]{:S(2)}, u32[]{:S(2)}) async-start(bf16[4,2304,256]{2,1,0:T(8,128)(2,1)} %bitcast.189), calls=%async_computation.3 | async-start | bytes 9437184 | tf_op jit(solution)/shard_map/all_to_all | solution.py:975
  (35 other events, 163.5 us)
Sparse Core Ops, SparseCore 0:
  10.8 88.6 all-gather.7
  100.9 230.6 all-gather.3
  333.2 94.0 all-gather.5
  431.9 148.5 reduce-scatter.2
  595.2 123.3 reduce-scatter.4

commit v4 on v3

--- a/solution.py
+++ b/solution.py
@@ -955,15 +955,21 @@
         bias = lax.dynamic_slice_in_dim(full_offsets[1], at, inner * columns, 0)
         out = readout_part(0, done) + bias
         first = swap_work(0, out)
-        second = finish_work(1, out)
-        out = out + readout_part(1, first, second)
+        out = out + readout_part(1, first)
+        finish_work(1, out)
         got["out"] = out.astype(jnp.bfloat16)
         return got["out"]
 
-    g_one = spread_reduce(g_one, [expand_work, work_two, work_three, work_four, work_five])
+    def work_last(done):
+        return work_five(work_four(done))
+
+    g_one = spread_reduce(g_one, [expand_work, work_two, work_three, work_last])
     swap_work(1, got["out"])
     g_expand = lax.psum_scatter(got["expand"], WIDE, scatter_dimension=1, tiled=True)
-    g_expand = after(g_expand, got["out"])
+    out_line = held(
+        got["out"].reshape(LINE * part, inner, columns).transpose(1, 0, 2)
+    )
+    g_expand = after(g_expand, out_line)
     g_expand = jnp.concatenate(
         [g_expand[: width + 1], g_out[None].astype(jnp.bfloat16), g_expand[width + 2 :]]
     )
@@ -971,7 +977,6 @@
     g_offsets = g_expand[width : width + 2]
     g_expand = g_expand[:width]
     g_project = jnp.concatenate([got["project", 0], got["project", 1]], axis=1)
-    out_line = got["out"].reshape(LINE * part, inner, columns).transpose(1, 0, 2)
     out_cols = lax.all_to_all(out_line, "spot", split_axis=0, concat_axis=0, tiled=True)
     readout = (
         out_cols.reshape(inner, LINE, part, columns)

time: 823 us -> 815 us (level)
  waiting for transfers between devices: 210 us -> 196 us
    all_to_all x1, waiting for transfers between devices: 23.9 us -> 0.01 us  [shards(): lax.all_to_all(out_line, 'spot', split_axis=0, concat_axis=0, tiled=True)]
    ppermute x2, waiting for transfers between devices: 0.01 us -> 20 us  [swap_groups(): return lax.ppermute(value, 'dp', [(i, i ^ 1) for i in range(group)])]
    ppermute x5, waiting for transfers between devices: 31.3 us -> 22.4 us  [spread_reduce(): theirs = lax.ppermute(sent, ALL, pairs)]
    ppermute x5, starting transfers between devices: 3.78 us -> 12.4 us  [spread_reduce(): theirs = lax.ppermute(sent, ALL, pairs)]
  transfers between devices with their start and end apart: 31 -> 31, of which waited for: 18 -> 17; matrix products, arithmetic and copies ran while one was open for 28% -> 28% of each run, Pallas kernels for 34% -> 34%
where the time goes in v4:
time: 815 us; the launch traced here: 809 us
  Pallas kernels  276 us (34%)
  waiting for transfers between devices  196 us (24%)
  matrix products  113 us (14%)
  other arithmetic  64.6 us (8%)
  local copies, waits for them, and re-layouts  64 us (8%)
  starting transfers between devices  57 us (7%)
  between operations  38.1 us (5%)
    pallas_call x2, Pallas kernels, block_backward(): pl.pallas_call(partial(backward_kernel, side), grid=(total // size,), in_...  89.7 us
    pallas_call x2, Pallas kernels, block_forward(): pl.pallas_call(partial(forward_kernel, side), grid=(total // size,), in_s...  83.7 us
    ppermute x1, waiting for transfers between devices, ring_gather(): other = lax.ppermute(held_all, 'dp', [(0, 1), (1, 0)])  47.5 us
    ppermute x7, waiting for transfers between devices, ring_gather(): value = lax.ppermute(value, WIDE, pairs)  47.2 us
    pallas_call x2, Pallas kernels, hidden_forward(): pl.pallas_call(hidden_kernel, grid=(depth // step, LINE), in_specs=[pl.Bl...  45.4 us
    pallas_call x1, Pallas kernels, pre_backward(): pl.pallas_call(partial(pre_kernel, counts), grid_spec=pltpu.PrefetchScala...  41.1 us
    dot_general x4, matrix products, project_part(): lax.dot_general(d_part, got['hidden', half], (((1,), (0,)), ((), ())), pr...  35.6 us
    dot_general x5, matrix products, contract_rows(): lax.dot_general(left, right, (((0,), (0,)), ((), ())), preferred_element_...  34.1 us
  transfers between devices with their start and end apart: 31, of which 17 were waited for; matrix products, arithmetic and copies ran while one was open for 28% of the time, Pallas kernels for 34%

profile of v4, /device:TPU:0, one launch (start us, length us, event | category | flops | bytes accessed | tf_op | source)
XLA Modules:
  0.0 808.9 jit_solution(851016746185485501)
XLA Ops:
  15.2 4.6 collective-permute-done
  21.9 9.2 %collective-permute-done.1 = bf16[144,1024]{1,0:T(8,128)(2,1)S(1)} collective-permute-done((bf16[144,1024]{1,0:T(8,128)(2,1)S(1)}, bf16[144,1024]{1,0:T(8,128)(2,1)S(1)}, u32[]{:S(2)}, u32[]{:S(2)}) %collective-permute-start.1) | collective-permute-done | bytes 294944 | tf_op jit(solution)/shard_map/ppermute | solution.py:522
  33.8 10.2 %collective-permute-done.2 = bf16[144,1024]{1,0:T(8,128)(2,1)} collective-permute-done((bf16[144,1024]{1,0:T(8,128)(2,1)S(1)}, bf16[144,1024]{1,0:T(8,128)(2,1)}, u32[]{:S(2)}, u32[]{:S(2)}) %collective-permute-start.2) | collective-permute-done | bytes 294944 | tf_op jit(solution)/shard_map/ppermute | solution.py:522
  75.1 3.6 collective-permute-start.4
  78.7 10.6 %collective-permute-done.4 = bf16[144,1024]{1,0:T(8,128)(2,1)S(1)} collective-permute-done((bf16[144,1024]{1,0:T(8,128)(2,1)}, bf16[144,1024]{1,0:T(8,128)(2,1)S(1)}, u32[]{:S(2)}, u32[]{:S(2)}) %collective-permute-start.4) | collective-permute-done | bytes 294944 | tf_op jit(solution)/shard_map/ppermute | solution.py:522
  89.4 6.0 collective-permute-start.5
  102.1 6.0 collective-permute-done.6
  109.7 47.5 %collective-permute-done.7 = bf16[8,144,1024]{2,1,0:T(8,128)(2,1)} collective-permute-done((bf16[8,144,1024]{2,1,0:T(8,128)(2,1)S(1)}, bf16[8,144,1024]{2,1,0:T(8,128)(2,1)}, u32[]{:S(2)}, u32[]{:S(2)}) %collective-permute-start.7) | collective-permute-done | bytes 2359328 | tf_op jit(solution)/shard_map/ppermute | solution.py:528
  162.9 4.6 all-to-all-start
  167.7 5.4 collective-permute-done.8
  173.1 3.4 select_bitcast_fusion
  180.3 3.6 pad_maximum_fusion.3
  183.9 4.8 dynamic-slice_bitcast_fusion
  195.8 63.5 %block_forward_24.1 = (f32[2304,1024]{1,0:T(8,128)}, f32[2304,1024]{1,0:T(8,128)}, f32[2304,1024]{1,0:T(8,128)}, f32[2304,128]{1,0:T(8,128)}, f32[2304,128]{1,0:...) custom-call(bf16[2304,1024]{1,0:T(8,128)(2,1)} %bitcast.190, ...), custom_call_target="tpu_custom_call" | custom-call | tf_op jit(solution)/shard_map/block_forward_24/pallas_call | solution.py:412
  260.2 20.2 %block_forward_12.1 = (f32[576,1024]{1,0:T(8,128)}, f32[576,1024]{1,0:T(8,128)}, f32[576,1024]{1,0:T(8,128)}, f32[576,128]{1,0:T(8,128)}, f32[576,128]{1,0:T(8,1...) custom-call(f32[4]{0:T(128)} %compare_convert_fusion.refs_0_, ...), custom_call_target="tpu_custom_call" | custom-call | tf_op jit(solution)/shard_map/block_forward_12/pallas_call | solution.py:412
  281.6 4.1 convert_reduce_fusion
  285.7 15.9 %all-to-all-done = bf16[16,576,256]{2,1,0:T(8,128)(2,1)} async-done(((bf16[16,576,256]{2,1,0:T(8,128)(2,1)}), bf16[16,576,256]{2,1,0:T(8,128)(2,1)}, u32[]{:S(2)}, u32[]{:S(2)}) %all-to-all-start) | async-done | bytes 4718624 | tf_op jit(solution)/shard_map/all_to_all | solution.py:814
  301.6 5.2 copy.149
  306.8 24.9 %all-gather.4.cloned.1.call-done.refs_0_.refs_4_.expand_ref = bf16[3072,4096]{1,0:T(8,128)(2,1)} async-done(((bf16[3072,256]{1,0:T(8,128)(2,1)}), bf16[3072,4096]{1,0:T(8,128)(2,1)}) %all-gather.4.cloned.1.call-update) | async-done | bytes 25165840 | tf_op jit(solution)/shard_map/all_gather | solution.py:803
  332.6 4.9 copy.117
  337.6 4.9 all-to-all-start.1
  343.9 41.1 %pre_backward.1 = bf16[576,4096]{1,0:T(8,128)(2,1)} custom-call(s32[8]{0:T(128)} %pad_add_fusion.at_ref, bf16[576,4096]{1,0:T(8,128)(2,1)} %bitcast.184, bf16[576,1024]{1,0:T(8,128)(2,1)} %get-tuple-element.121.tokens_ref, bf16[3072,4096]{1,0:T(8,128)(2,1)} %all-gather.4.cloned.1.call-done.refs_0_.refs_4_.expand_ref, ...), custom_call_target="tpu_custom_call" | custom-call | tf_op jit(solution)/shard_map/pre_backward/pallas_call | solution.py:699
  385.0 10.0 %fusion.9.refs_1_ = f32[576,1024]{1,0:T(8,128)} fusion(bf16[576,4096]{1,0:T(8,128)(2,1)} %pre_backward.1, bf16[3072,4096]{1,0:T(8,128)(2,1)} %all-gather.4.cloned.1.call-done.refs_0_.refs_4_.expand_ref), kind=kOutput, calls=%fused_computation.24 | convolution fusion | flops 4831838208 | bytes 15466496 | tf_op jit(solution)/shard_map/dot_general | solution.py:35
  394.9 22.4 %block_backward_12.1 = (f32[576,1024]{1,0:T(8,128)}, bf16[576,1024]{1,0:T(8,128)(2,1)}, bf16[576,1024]{1,0:T(8,128)(2,1)}, f32[128,1024]{1,0:T(8,128)}) custom-call(f32[4]{0:T(128)} %compare_convert_fusion.refs_0_, f32[576,1024]{1,0:T(8,128)} %fusion.9.refs_1_, bf16[576,1024]{1,0:T(8,128)(2,1)} %get-tuple-element.89.refs_1_.refs_2_, ...), custom_call_target="tpu_custom_call" | custom-call | tf_op jit(solution)/shard_map/block_backward_12/pallas_call | solution.py:448
  426.9 4.9 dynamic-slice_bitcast_fusion.2
  431.8 67.3 %block_backward_24.1 = (bf16[2304,1024]{1,0:T(8,128)(2,1)}, bf16[2304,1024]{1,0:T(8,128)(2,1)}, bf16[2304,1024]{1,0:T(8,128)(2,1)}, f32[128,1024]{1,0:T(8,128)}) custom-call(bf16[576,144]{1,0:T(8,128)(2,1)} %select_convert_fusion.refs_0_, f32[576,1024]{1,0:T(8,128)} %get-tuple-element.110.refs_1_, bf16[2304,1024]{1,0:T(8,128)(2,1)} %bitcast.191, ...), custom_call_target="tpu_custom_call" | custom-call | tf_op jit(solution)/shard_map/block_backward_24/pallas_call | solution.py:448
  499.1 8.4 %convolution_convert_fusion.1 = bf16[1024,1024]{1,0:T(8,128)(2,1)S(1)} fusion(bf16[2304,1024]{1,0:T(8,128)(2,1)} %get-tuple-element.118, bf16[2304,1024]{1,0:T(8,128)(2,1)} %get-tuple-element.119), kind=kOutput, calls=%fused_computation.67 | convolution fusion | flops 4832886784 | bytes 11534336 | tf_op jit(solution)/shard_map/dot_general | solution.py:29
  508.2 8.8 %convolution_convert_fusion.2 = bf16[1024,1024]{0,1:T(8,128)(2,1)S(1)} fusion(bf16[2304,1024]{1,0:T(8,128)(2,1)} %get-tuple-element.117, bf16[2304,1024]{1,0:T(8,128)(2,1)} %bitcast.192), kind=kOutput, calls=%fused_computation.68 | convolution fusion | flops 4832886784 | bytes 11534336 | tf_op jit(solution)/shard_map/dot_general | solution.py:29
  520.1 11.7 %convolution_convert_fusion = bf16[1040,4096]{1,0:T(8,128)(2,1)} fusion(bf16[576,1040]{1,0:T(8,128)(2,1)S(1)} %concatenate.59, bf16[576,4096]{1,0:T(8,128)(2,1)} %pre_backward.1), kind=kOutput, calls=%fused_computation | convolution fusion | flops 4911595520 | bytes 14436352 | tf_op jit(solution)/shard_map/dot_general | solution.py:29
  531.8 3.5 fusion.12
  538.3 22.1 %hidden_forward.2 = bf16[2304,2048]{1,0:T(8,128)(2,1)} custom-call(bf16[2304,1024]{1,0:T(8,128)(2,1)} %all-gather.6.cloned.1.call-done.tokens_ref, bf16[3072,4096]{1,0:T(8,128)(2,1)} %all-gather.4.cloned.1.call-done.refs_0_.refs_4_.expand_ref, f32[1,4096]{1,0:T(1,128)} %bitcast.222), custom_call_target="tpu_custom_call" | custom-call | tf_op jit(solution)/shard_map/hidden_forward/pallas_call | solution.py:620
  560.4 22.4 %collective-permute-done.12 = bf16[2,2,2,80,1024]{4,3,2,1,0:T(8,128)(2,1)} collective-permute-done((bf16[2,2,2,80,1024]{4,3,2,1,0:T(8,128)(2,1)}, bf16[2,2,2,80,1024]{4,3,2,1,0:T(8,128)(2,1)}, u32[]{:S(2)}, u32[]{:S(2)}) %collective-permute-start.12) | collective-permute-done | bytes 1310752 | tf_op jit(solution)/shard_map/ppermute | solution.py:590
  585.7 9.3 %fusion.17 = bf16[2,256,2048]{2,1,0:T(8,128)(2,1)} fusion(bf16[2,2304,256]{2,1,0:T(8,128)(2,1)} %get-tuple-element.134, bf16[2304,2048]{1,0:T(8,128)(2,1)} %hidden_forward.2), kind=kOutput, calls=%fused_computation.45 | convolution fusion | flops 4832886784 | bytes 13893632 | tf_op jit(solution)/shard_map/dot_general | solution.py:869
  595.1 4.4 collective-permute-done.14
  599.5 8.7 %convert_add_fusion.2 = f32[2,256,2048]{2,1,0:T(8,128)S(1)} fusion(bf16[2,256,2048]{2,1,0:T(8,128)(2,1)} %collective-permute-done.14, bf16[2,2304,256]{2,1,0:T(8,128)(2,1)} %get-tuple-element.135, bf16[2304,2048]{1,0:T(8,128)(2,1)} %hidden_forward.2), kind=kOutput, calls=%fused_computation.43 | convolution fusion | flops 4833935360 | bytes 18087936 | tf_op jit(solution)/shard_map/dot_general | solution.py:869
  612.8 23.3 %hidden_forward.3 = bf16[2304,2048]{1,0:T(8,128)(2,1)} custom-call(bf16[2304,1024]{1,0:T(8,128)(2,1)} %all-gather.6.cloned.1.call-done.tokens_ref, bf16[3072,4096]{1,0:T(8,128)(2,1)} %all-gather.4.cloned.1.call-done.refs_0_.refs_4_.expand_ref, f32[1,4096]{1,0:T(1,128)} %bitcast.223), custom_call_target="tpu_custom_call" | custom-call | tf_op jit(solution)/shard_map/hidden_forward/pallas_call | solution.py:620
  641.4 10.3 %fusion.20 = bf16[2,256,2048]{2,1,0:T(8,128)(2,1)} fusion(bf16[2,2304,256]{2,1,0:T(8,128)(2,1)S(1)} %copy-done.17, bf16[2304,2048]{1,0:T(8,128)(2,1)} %hidden_forward.3), kind=kOutput, calls=%fused_computation.46 | convolution fusion | flops 4832886784 | bytes 13893632 | tf_op jit(solution)/shard_map/dot_general | solution.py:869
  657.5 4.6 fusion.15
  665.2 7.3 convert_add_fusion.1
  673.8 15.8 %convolution_add_fusion.1 = f32[2304,1024]{0,1:T(8,128)} fusion(bf16[2304,2048]{1,0:T(8,128)(2,1)S(1)} %bitcast.198, f32[1024]{0:T(1024)S(1)} %bitcast.230, bf16[3072,4096]{1,0:T(8,128)(2,1)} %all-gather.4.cloned.1.call-done.refs_0_.refs_4_.expand_ref, s32[]{:T(128)S(6)} %select_n.519), kind=kOutput, calls=%fused_computation.27 | convolution fusion | flops 9666035712 | bytes 23072772 | tf_op jit(solution)/shard_map/dot_general | solution.py:947
  690.0 17.5 %convolution_add_fusion = bf16[2304,1024]{0,1:T(8,128)(2,1)} fusion(f32[2304,1024]{0,1:T(8,128)} %convolution_add_fusion.1, bf16[2304,2048]{1,0:T(8,128)(2,1)} %hidden_forward.3, bf16[2048,1024]{1,0:T(8,128)(2,1)} %bitcast.211), kind=kOutput, calls=%fused_computation.26 | convolution fusion | flops 9668395008 | bytes 27787264 | tf_op jit(solution)/shard_map/dot_general | solution.py:947
  709.4 8.4 %collective-permute-start.19 = (bf16[80,1024]{1,0:T(8,128)(2,1)}, bf16[80,1024]{1,0:T(8,128)(2,1)}, u32[]{:S(2)}, u32[]{:S(2)}) collective-permute-start(bf16[80,1024]{1,0:T(8,128)(2,1)} %dynamic-slice_bitcast_fusion.8), channel_id=1, source_target_pairs={{0,4},{1,5},{2,6},{3,7},{4,0},{5,1},{6,2},{7,3},{8,12},{9,13},{10,... | collective-permute-start | bytes 491528 | tf_op jit(solution)/shard_map/ppermute | solution.py:590
  721.1 6.6 copy.127
  729.0 5.2 all-to-all-start.2
  745.6 5.1 collective-permute-done.20
  758.3 20.0 %collective-permute-done.22 = bf16[256,2048]{1,0:T(8,128)(2,1)S(1)} collective-permute-done((bf16[256,2048]{1,0:T(8,128)(2,1)S(1)}, bf16[256,2048]{1,0:T(8,128)(2,1)S(1)}, u32[]{:S(2)}, u32[]{:S(2)}) %collective-permute-start.22) | collective-permute-done | bytes 1048608 | tf_op jit(solution)/shard_map/ppermute | solution.py:542
  781.0 16.2 %adamw_turned.1 = (f32[4096,256]{1,0:T(8,128)}, f32[4096,256]{1,0:T(8,128)}, f32[4096,256]{1,0:T(8,128)}, f32[4096,256]{1,0:T(8,128)}, bf16[4096,256]{1,0:T(8,128)(2,1)}) custom-call(f32[256,4096]{1,0:T(8,128)} %pad_maximum_fusion.2.grad_ref, f32[4096,256]{1,0:T(8,128)} %refs_0_.1, f32[4096,256]{1,0:T(8,128)} %refs_1_.1, f32[4096,256]{1,0:T(8,128)} %refs_2_.1, ...), custom_call_target="tpu_custom_call" | custom-call | tf_op jit(solution)/shard_map/adamw_turned/pallas_call | solution.py:646
  797.2 4.9 copy.128
  (272 shorter events, 117.4 us)
Async XLA Ops:
  7.2 176.7 %all-gather.8.cloned.1.call-start = ((), (), s32[]{:S(2)}) async-start(), calls=%async_computation.7 | async-start | bytes 8912896 | tf_op jit(solution)/shard_map/all_gather | solution.py:802
  7.3 26.4 %copy-start.12 = (f32[1024,256]{1,0:T(8,128)S(1)}, f32[1024,256]{1,0:T(8,128)}, u32[]{:S(2)}) copy-start(f32[1024,256]{1,0:T(8,128)} %param.36) | copy-start | bytes 3145732
  10.6 321.0 %all-gather.4.cloned.1.call-start = ((), (), s32[]{:S(2)}) async-start(), calls=%async_computation.5 | async-start | bytes 26738688 | tf_op jit(solution)/shard_map/all_gather | solution.py:803
  12.1 39.1 %copy-start.45 = (s32[8]{0:T(128)S(1)}, s32[8]{0:T(128)}, u32[]{:S(2)}) copy-start(s32[8]{0:T(128)} %constant.441.clone) | copy-start | bytes 100
  12.1 46.4 %copy-start.35 = (s32[8]{0:T(128)S(1)}, s32[8]{0:T(128)}, u32[]{:S(2)}) copy-start(s32[8]{0:T(128)} %constant.442.clone) | copy-start | bytes 100
  12.1 7.7 collective-permute-start
  19.8 11.4 %copy-start.27 = (bf16[144,1024]{1,0:T(8,128)(2,1)}, bf16[144,1024]{1,0:T(8,128)(2,1)S(1)}, u32[]{:S(2)}) copy-start(bf16[144,1024]{1,0:T(8,128)(2,1)S(1)} %collective-permute-done) | copy-start | bytes 884740
  19.8 11.3 %collective-permute-start.1 = (bf16[144,1024]{1,0:T(8,128)(2,1)S(1)}, bf16[144,1024]{1,0:T(8,128)(2,1)S(1)}, u32[]{:S(2)}, u32[]{:S(2)}) collective-permute-start(bf16[144,1024]{1,0:T(8,128)(2,1)S(1)} %collective-permute-done), channel_id=1, source_target_pairs={{0,4},{1,3},{4,8},{5,1},{8,12},{9,5},{12,14},{13,9},{14,10},{15,13... | collective-permute-start | bytes 884744 | tf_op jit(solution)/shard_map/ppermute | solution.py:522
  31.2 12.8 %collective-permute-start.2 = (bf16[144,1024]{1,0:T(8,128)(2,1)S(1)}, bf16[144,1024]{1,0:T(8,128)(2,1)}, u32[]{:S(2)}, u32[]{:S(2)}) collective-permute-start(bf16[144,1024]{1,0:T(8,128)(2,1)S(1)} %collective-permute-done.1), channel_id=1, source_target_pairs={{0,4},{1,3},{4,8},{5,1},{8,12},{9,5},{12,14},{13,9},{14,10},{15,13... | collective-permute-start | bytes 884744 | tf_op jit(solution)/shard_map/ppermute | solution.py:522
  33.8 44.9 %copy-start.28 = (bf16[144,1024]{1,0:T(8,128)(2,1)S(1)}, bf16[144,1024]{1,0:T(8,128)(2,1)}, u32[]{:S(2)}) copy-start(bf16[144,1024]{1,0:T(8,128)(2,1)} %copy-done.27) | copy-start | bytes 884740
  44.0 34.7 %copy-start.30 = (bf16[144,1024]{1,0:T(8,128)(2,1)S(1)}, bf16[144,1024]{1,0:T(8,128)(2,1)}, u32[]{:S(2)}) copy-start(bf16[144,1024]{1,0:T(8,128)(2,1)} %copy-done.29) | copy-start | bytes 884740
  44.0 7.1 collective-permute-start.3
  51.2 22.8 %copy-start.31 = (bf16[144,1024]{1,0:T(8,128)(2,1)}, bf16[144,1024]{1,0:T(8,128)(2,1)S(1)}, u32[]{:S(2)}) copy-start(bf16[144,1024]{1,0:T(8,128)(2,1)S(1)} %collective-permute-done.3) | copy-start | bytes 884740
  74.7 21.7 %copy-start.32 = (bf16[144,1024]{1,0:T(8,128)(2,1)S(1)}, bf16[144,1024]{1,0:T(8,128)(2,1)}, u32[]{:S(2)}) copy-start(bf16[144,1024]{1,0:T(8,128)(2,1)} %copy-done.31) | copy-start | bytes 884740
  75.1 14.3 %collective-permute-start.4 = (bf16[144,1024]{1,0:T(8,128)(2,1)}, bf16[144,1024]{1,0:T(8,128)(2,1)S(1)}, u32[]{:S(2)}, u32[]{:S(2)}) collective-permute-start(bf16[144,1024]{1,0:T(8,128)(2,1)} %copy-done.31), channel_id=1, source_target_pairs={{0,4},{1,3},{4,8},{5,1},{8,12},{9,5},{12,14},{13,9},{14,10},{15,13... | collective-permute-start | bytes 884744 | tf_op jit(solution)/shard_map/ppermute | solution.py:522
  89.4 10.2 %collective-permute-start.5 = (bf16[144,1024]{1,0:T(8,128)(2,1)S(1)}, bf16[144,1024]{1,0:T(8,128)(2,1)S(1)}, u32[]{:S(2)}, u32[]{:S(2)}) collective-permute-start(bf16[144,1024]{1,0:T(8,128)(2,1)S(1)} %collective-permute-done.4), channel_id=1, source_target_pairs={{0,4},{1,3},{4,8},{5,1},{8,12},{9,5},{12,14},{13,9},{14,10},{15,13... | collective-permute-start | bytes 884744 | tf_op jit(solution)/shard_map/ppermute | solution.py:522
  99.6 8.5 %collective-permute-start.6 = (bf16[144,1024]{1,0:T(8,128)(2,1)S(1)}, bf16[144,1024]{1,0:T(8,128)(2,1)S(1)}, u32[]{:S(2)}, u32[]{:S(2)}) collective-permute-start(bf16[144,1024]{1,0:T(8,128)(2,1)S(1)} %collective-permute-done.5), channel_id=1, source_target_pairs={{0,4},{1,3},{4,8},{5,1},{8,12},{9,5},{12,14},{13,9},{14,10},{15,13... | collective-permute-start | bytes 884744 | tf_op jit(solution)/shard_map/ppermute | solution.py:522
  108.1 49.1 %collective-permute-start.7 = (bf16[8,144,1024]{2,1,0:T(8,128)(2,1)S(1)}, bf16[8,144,1024]{2,1,0:T(8,128)(2,1)}, u32[]{:S(2)}, u32[]{:S(2)}) collective-permute-start(bf16[8,144,1024]{2,1,0:T(8,128)(2,1)S(1)} %bitcast_dynamic-update-slice_fusion), channel_id=1, source_target_pairs={{0,16},{16,0},{1,17},{17,1},{2,18},{18,2},{3,19},{19,3},{4,20},{20... | collective-permute-start | bytes 7077896 | tf_op jit(solution)/shard_map/ppermute | solution.py:528
  162.9 10.3 %collective-permute-start.8 = (bf16[2,8,144,1024]{3,2,1,0:T(8,128)(2,1)}, bf16[2,8,144,1024]{3,2,1,0:T(8,128)(2,1)}, u32[]{:S(2)}, u32[]{:S(2)}) collective-permute-start(bf16[2,8,144,1024]{3,2,1,0:T(8,128)(2,1)} %pad_maximum_fusion.1), channel_id=1, source_target_pairs={{0,1},{1,0},{2,3},{3,2},{4,5},{5,4},{6,7},{7,6},{8,9},{9,8},{10,11... | collective-permute-start | bytes 14155784 | tf_op jit(solution)/shard_map/ppermute | solution.py:535
  162.9 138.7 %all-to-all-start = ((bf16[16,576,256]{2,1,0:T(8,128)(2,1)}), bf16[16,576,256]{2,1,0:T(8,128)(2,1)}, u32[]{:S(2)}, u32[]{:S(2)}) async-start(bf16[16,576,256]{2,1,0:T(8,128)(2,1)} %bitcast.181), calls=%async_computation | async-start | bytes 9437184 | tf_op jit(solution)/shard_map/all_to_all | solution.py:814
  167.5 370.8 %all-gather.6.cloned.1.call-start = ((), (), s32[]{:S(2)}) async-start(), calls=%async_computation.6 | async-start | bytes 5898240 | tf_op jit(solution)/shard_map/all_gather | solution.py:823
  188.7 92.9 %collective-permute-start.9 = (bf16[512,4096]{1,0:T(8,128)(2,1)}, bf16[512,4096]{1,0:T(8,128)(2,1)}, u32[]{:S(2)}, u32[]{:S(2)}) collective-permute-start(bf16[512,4096]{1,0:T(8,128)(2,1)} %dynamic-slice_bitcast_fusion), channel_id=1, source_target_pairs={{0,16},{16,0},{1,17},{17,1},{2,18},{18,2},{3,19},{19,3},{4,20},{20... | collective-permute-start | bytes 12582920 | tf_op jit(solution)/shard_map/ppermute | solution.py:805
  281.6 62.2 %collective-permute-start.10 = (bf16[512,4096]{1,0:T(8,128)(2,1)}, bf16[512,4096]{1,0:T(8,128)(2,1)}, u32[]{:S(2)}, u32[]{:S(2)}) collective-permute-start(bf16[512,4096]{1,0:T(8,128)(2,1)} %collective-permute-done.9.refs_2_), channel_id=1, source_target_pairs={{0,1},{1,0},{2,3},{3,2},{4,5},{5,4},{6,7},{7,6},{8,9},{9,8},{10,11... | collective-permute-start | bytes 12582920 | tf_op jit(solution)/shard_map/ppermute | solution.py:813
  337.6 89.3 %all-to-all-start.1 = ((bf16[4,4,576,256]{3,2,1,0:T(8,128)(2,1)}), bf16[4,4,576,256]{3,2,1,0:T(8,128)(2,1)}, u32[]{:S(2)}, u32[]{:S(2)}) async-start(bf16[4,4,576,256]{3,2,1,0:T(8,128)(2,1)} %copy.117), calls=%async_computation.1 | async-start | bytes 9437184 | tf_op jit(solution)/shard_map/all_to_all | solution.py:824
  342.5 252.5 %reduce-scatter.3.cloned.1.call-start = ((), (), s32[]{:S(2)}) async-start(), calls=%async_computation.8 | async-start | bytes 5406720 | tf_op jit(solution)/shard_map/reduce_scatter | solution.py:849
  394.9 23.9 %copy-start.10 = (bf16[576,1024]{1,0:T(8,128)(2,1)S(1)}, bf16[576,1024]{1,0:T(8,128)(2,1)}, u32[]{:S(2)}) copy-start(bf16[576,1024]{1,0:T(8,128)(2,1)} %get-tuple-element.89.refs_1_.refs_2_) | copy-start | bytes 3538948
  431.8 296.0 %reduce-scatter.5.cloned.1.call-start = ((), (), s32[]{:S(2)}) async-start(), calls=%async_computation.9 | async-start | bytes 9052160 | tf_op jit(solution)/shard_map/reduce_scatter | solution.py:968
  519.2 12.6 %collective-permute-start.11 = (bf16[2,2,2,2,80,1024]{5,4,2,1,0,3:T(8,128)(2,1)}, bf16[2,2,2,2,80,1024]{5,4,2,1,0,3:T(8,128)(2,1)}, u32[]{:S(2)}, u32[]{:S(2)}) collective-permute-start(bf16[2,2,2,2,80,1024]{5,4,2,1,0,3:T(8,128)(2,1)} %dynamic-slice_bitcast_fusion.1), channel_id=1, source_target_pairs={{0,1},{1,0},{2,3},{3,2},{4,5},{5,4},{6,7},{7,6},{8,9},{9,8},{10,11... | collective-permute-start | bytes 7864328 | tf_op jit(solution)/shard_map/ppermute | solution.py:590
  536.5 46.3 %collective-permute-start.12 = (bf16[2,2,2,80,1024]{4,3,2,1,0:T(8,128)(2,1)}, bf16[2,2,2,80,1024]{4,3,2,1,0:T(8,128)(2,1)}, u32[]{:S(2)}, u32[]{:S(2)}) collective-permute-start(bf16[2,2,2,80,1024]{4,3,2,1,0:T(8,128)(2,1)} %dynamic-slice_bitcast_fusion.5), channel_id=1, source_target_pairs={{0,2},{1,3},{2,0},{3,1},{4,6},{5,7},{6,4},{7,5},{8,10},{9,11},{10,... | collective-permute-start | bytes 3932168 | tf_op jit(solution)/shard_map/ppermute | solution.py:590
  595.0 4.5 collective-permute-start.14
  595.1 15.4 %copy-start.9 = (bf16[2,2,2,80,1024]{4,3,2,1,0:T(8,128)(2,1)S(1)}, bf16[2,2,2,80,1024]{4,3,2,1,0:T(8,128)(2,1)}, u32[]{:S(2)}) copy-start(bf16[2,2,2,80,1024]{4,3,2,1,0:T(8,128)(2,1)} %fusion.23) | copy-start | bytes 3932164
  610.4 27.4 %collective-permute-start.15 = (bf16[1,256,2048]{2,1,0:T(8,128)(2,1)S(1)}, bf16[1,256,2048]{2,1,0:T(8,128)(2,1)}, u32[]{:S(2)}, u32[]{:S(2)}) collective-permute-start(bf16[1,256,2048]{2,1,0:T(8,128)(2,1)S(1)} %dynamic-slice_convert_fusion.1), channel_id=1, source_target_pairs={{0,2},{1,3},{2,0},{3,1},{4,6},{5,7},{6,4},{7,5},{8,10},{9,11},{10,... | collective-permute-start | bytes 3145736 | tf_op jit(solution)/shard_map/ppermute | solution.py:890
  611.4 28.6 %collective-permute-start.13 = (bf16[2,2,80,1024]{3,2,1,0:T(8,128)(2,1)}, bf16[2,2,80,1024]{3,2,1,0:T(8,128)(2,1)}, u32[]{:S(2)}, u32[]{:S(2)}) collective-permute-start(bf16[2,2,80,1024]{3,2,1,0:T(8,128)(2,1)} %dynamic-slice_bitcast_fusion.6), channel_id=1, source_target_pairs={{0,16},{1,17},{2,18},{3,19},{4,20},{5,21},{6,22},{7,23},{8,24},{9,... | collective-permute-start | bytes 1966088 | tf_op jit(solution)/shard_map/ppermute | solution.py:590
  641.4 23.3 %copy-start.14 = (bf16[2,2,80,1024]{3,2,1,0:T(8,128)(2,1)}, bf16[2,2,80,1024]{3,2,1,0:T(8,128)(2,1)S(1)}, u32[]{:S(2)}) copy-start(bf16[2,2,80,1024]{3,2,1,0:T(8,128)(2,1)S(1)} %fusion.28) | copy-start | bytes 1966084
  651.7 13.5 %collective-permute-start.16 = (bf16[2,256,2048]{2,1,0:T(8,128)(2,1)}, bf16[2,256,2048]{2,1,0:T(8,128)(2,1)}, u32[]{:S(2)}, u32[]{:S(2)}) collective-permute-start(bf16[2,256,2048]{2,1,0:T(8,128)(2,1)} %fusion.20), channel_id=1, source_target_pairs={{0,1},{1,0},{2,3},{3,2},{4,5},{5,4},{6,7},{7,6},{8,9},{9,8},{10,11... | collective-permute-start | bytes 6291464 | tf_op jit(solution)/shard_map/ppermute | solution.py:878
  653.4 11.8 %slice-start.3 = ((s8[9437184]{0:T(1024)(128)(4,1)}), s8[4194304]{0:T(1024)(128)(4,1)S(1)}, s32[]{:S(2)}) async-start(s8[9437184]{0:T(1024)(128)(4,1)} %bitcast.199), calls=%async_computation.13 | async-start | bytes 8388608
  663.3 26.3 %collective-permute-start.17 = (bf16[256,2048]{1,0:T(8,128)(2,1)S(1)}, bf16[256,2048]{1,0:T(8,128)(2,1)S(1)}, u32[]{:S(2)}, u32[]{:S(2)}) collective-permute-start(bf16[256,2048]{1,0:T(8,128)(2,1)S(1)} %fusion.30), channel_id=1, source_target_pairs={{0,16},{16,0},{1,17},{17,1},{2,18},{18,2},{3,19},{19,3},{4,20},{20... | collective-permute-start | bytes 3145736 | tf_op jit(solution)/shard_map/ppermute | solution.py:542
  664.7 42.8 %collective-permute-start.18 = (bf16[2,80,1024]{2,1,0:T(8,128)(2,1)S(1)}, bf16[2,80,1024]{2,1,0:T(8,128)(2,1)}, u32[]{:S(2)}, u32[]{:S(2)}) collective-permute-start(bf16[2,80,1024]{2,1,0:T(8,128)(2,1)S(1)} %dynamic-slice_bitcast_fusion.7), channel_id=1, source_target_pairs={{0,8},{1,9},{2,10},{3,11},{4,12},{5,13},{6,14},{7,15},{8,0},{9,1},... | collective-permute-start | bytes 983048 | tf_op jit(solution)/shard_map/ppermute | solution.py:590
  672.5 17.1 %copy-start.18 = (f32[2,256,2048]{2,1,0:T(8,128)}, f32[2,256,2048]{2,1,0:T(8,128)S(1)}, u32[]{:S(2)}) copy-start(f32[2,256,2048]{2,1,0:T(8,128)S(1)} %convert_add_fusion.1) | copy-start | bytes 12582916
  690.0 17.6 %copy-start.15 = (bf16[2,2,80,1024]{3,2,1,0:T(8,128)(2,1)S(1)}, bf16[2,2,80,1024]{3,2,1,0:T(8,128)(2,1)}, u32[]{:S(2)}) copy-start(bf16[2,2,80,1024]{3,2,1,0:T(8,128)(2,1)} %copy-done.14) | copy-start | bytes 1966084
  690.0 27.8 %copy-start.33 = (bf16[1,80,1024]{2,1,0:T(8,128)(2,1)S(1)}, bf16[1,80,1024]{2,1,0:T(8,128)(2,1)}, u32[]{:S(2)}) copy-start(bf16[1,80,1024]{2,1,0:T(8,128)(2,1)} %reduce-scatter.3.cloned.1.call-done) | copy-start | bytes 491524
  709.4 26.8 %collective-permute-start.19 = (bf16[80,1024]{1,0:T(8,128)(2,1)}, bf16[80,1024]{1,0:T(8,128)(2,1)}, u32[]{:S(2)}, u32[]{:S(2)}) collective-permute-start(bf16[80,1024]{1,0:T(8,128)(2,1)} %dynamic-slice_bitcast_fusion.8), channel_id=1, source_target_pairs={{0,4},{1,5},{2,6},{3,7},{4,0},{5,1},{6,2},{7,3},{8,12},{9,13},{10,... | collective-permute-start | bytes 491528 | tf_op jit(solution)/shard_map/ppermute | solution.py:590
  718.4 33.4 %collective-permute-start.21 = (bf16[1,256,2048]{2,1,0:T(8,128)(2,1)}, bf16[1,256,2048]{2,1,0:T(8,128)(2,1)}, u32[]{:S(2)}, u32[]{:S(2)}) collective-permute-start(bf16[1,256,2048]{2,1,0:T(8,128)(2,1)} %dynamic-slice_convert_fusion), channel_id=1, source_target_pairs={{0,2},{1,3},{2,0},{3,1},{4,6},{5,7},{6,4},{7,5},{8,10},{9,11},{10,... | collective-permute-start | bytes 3145736 | tf_op jit(solution)/shard_map/ppermute | solution.py:890
  729.0 68.2 %all-to-all-start.2 = ((bf16[4,2304,256]{2,1,0:T(8,128)(2,1)}), bf16[4,2304,256]{2,1,0:T(8,128)(2,1)}, u32[]{:S(2)}, u32[]{:S(2)}) async-start(bf16[4,2304,256]{2,1,0:T(8,128)(2,1)} %bitcast.189), calls=%async_computation.3 | async-start | bytes 9437184 | tf_op jit(solution)/shard_map/all_to_all | solution.py:980
  736.1 14.6 %collective-permute-start.20 = (bf16[1040,256]{1,0:T(8,128)(2,1)S(1)}, bf16[1040,256]{1,0:T(8,128)(2,1)}, u32[]{:S(2)}, u32[]{:S(2)}) collective-permute-start(bf16[1040,256]{1,0:T(8,128)(2,1)S(1)} %concatenate.63), channel_id=1, source_target_pairs={{0,16},{16,0},{1,17},{17,1},{2,18},{18,2},{3,19},{19,3},{4,20},{20... | collective-permute-start | bytes 1597448 | tf_op jit(solution)/shard_map/ppermute | solution.py:547
  737.3 14.6 %copy-start.19 = (f32[2,256,2048]{2,1,0:T(8,128)S(1)}, f32[2,256,2048]{2,1,0:T(8,128)}, u32[]{:S(2)}) copy-start(f32[2,256,2048]{2,1,0:T(8,128)} %copy-done.18) | copy-start | bytes 12582916
  753.5 24.8 %collective-permute-start.22 = (bf16[256,2048]{1,0:T(8,128)(2,1)S(1)}, bf16[256,2048]{1,0:T(8,128)(2,1)S(1)}, u32[]{:S(2)}, u32[]{:S(2)}) collective-permute-start(bf16[256,2048]{1,0:T(8,128)(2,1)S(1)} %fusion.31), channel_id=1, source_target_pairs={{0,16},{16,0},{1,17},{17,1},{2,18},{18,2},{3,19},{19,3},{4,20},{20... | collective-permute-start | bytes 3145736 | tf_op jit(solution)/shard_map/ppermute | solution.py:542
  757.1 23.9 %copy-start.11 = (f32[1024,256]{1,0:T(8,128)}, f32[1024,256]{1,0:T(8,128)S(1)}, u32[]{:S(2)}) copy-start(f32[1024,256]{1,0:T(8,128)S(1)} %get-tuple-element.237) | copy-start | bytes 3145732
  (36 other events, 229.9 us)
Sparse Core Ops, SparseCore 0:
  10.8 88.6 all-gather.7
  100.9 230.7 all-gather.3
  333.3 93.9 all-gather.5
  431.9 149.5 reduce-scatter.2
  595.2 112.6 reduce-scatter.4
